TPU v7x, 512 devices: a whole 4x8x8 slice. The times are simulated.
512 devices in a mesh: event: 2 (over core), dom: 256 (over z, y, x).
Axes of the slice: x: 4, y: 8, z: 8, core: 2. Of those that a mesh axis runs over, the one named last changes fastest.
Arguments:
- kernels: bfloat16 [4, 256, 64, 125, 128], P('event', 'dom'), may hold values from -12 to 12
- counts: int32 [4, 256, 64, 128], P('event', 'dom'), may hold values from 0 to 3
- volume: bfloat16 [256, 64, 128], P('dom', 'event'), may hold values from 0.29882812 to 3
- tables: bfloat16 [32, 128, 128], replicated, may hold values from 0.049804688 to 1
- pair_offset: int32 [256, 2, 32, 16], P('dom', 'event'), may hold values from 0 to 64, as said below
- pair_table: int32 [256, 2, 32, 16], P('dom', 'event'), may hold values from 0 to 31
Outputs:
- smoothed: bfloat16 [256, 64, 125, 128], P('dom', 'event')
Inputs may be any that keep to these rules, and one draw needn't show every extreme that they name: `pair_offset`: for each block of a device the 16 offsets are distinct and the first is 32.
All inputs are finite; a program needn't handle non-finite values.
Results may differ from a plain program's by a relative error of at most 0.0075.
Values may be sent and summed in bfloat16 or wider, within the bound.
No kernel may reach another device: no remote copies, remote signals or barrier semaphores. Data moves between devices by JAX's collectives and lax.ppermute only.
A program may use at most 64 MiB of HBM per device.

v0:
```python
import jax
import jax.numpy as jnp
from jax import lax
from jax.sharding import PartitionSpec as P

EV_DEV = 2
PB = 16


def passed_along(value, axis, steps):
    count = lax.axis_size(axis)
    first, last = (max(0, -steps), min(count, count - steps))
    return lax.ppermute(value, axis, [(source, source + steps) for source in range(first, last)])


def per_device(kernels, counts, volume, tables, pair_offset, pair_table):
    owned = volume.shape[1]
    groups = lax.axis_size("event")
    points = kernels.shape[3]
    width = kernels.shape[4]
    moved, moved_counts = (
        lax.all_to_all(kernels, "event", split_axis=2, concat_axis=0, tiled=True),
        lax.all_to_all(
            counts.astype(jnp.bfloat16), "event", split_axis=2, concat_axis=0, tiled=True
        ),
    )
    grouped = moved.reshape(groups, EV_DEV, owned, points, width)
    partial_value = jnp.sum(grouped, axis=1, dtype=jnp.float32).astype(jnp.bfloat16)
    summed = jnp.sum(partial_value, axis=0, dtype=jnp.float32)
    hits = jnp.sum(moved_counts, axis=0, dtype=jnp.float32)[0]
    vol_rows = volume[0]
    weighted = (
        summed * vol_rows.astype(jnp.float32)[:, None, :] / jnp.sqrt(1.0 + hits)[:, None, :]
    ).astype(jnp.bfloat16)
    source = jnp.concatenate([weighted, vol_rows[:, None, :]], axis=1)
    offsets = pair_offset[0, 0]
    table_ids = pair_table[0, 0]
    places = jnp.arange(owned, dtype=jnp.int32)

    def add_pairs(extended, which):
        matrices = tables[table_ids[:, which]]
        contrib = jnp.einsum("bgs,bst->bgt", source, matrices, preferred_element_type=jnp.float32)
        targets = places + offsets[:, which]
        return (extended.at[targets].add(contrib), None)

    start_buffer = jnp.zeros((3 * owned, points + 1, width), jnp.float32)
    extended, unused = lax.scan(add_pairs, start_buffer, jnp.arange(PB, dtype=jnp.int32))
    from_next = passed_along(extended[:owned].astype(jnp.bfloat16), "dom", -1).astype(jnp.float32)
    from_prev = passed_along(extended[2 * owned :].astype(jnp.bfloat16), "dom", 1).astype(
        jnp.float32
    )
    accumulated = extended[owned : 2 * owned] + from_next + from_prev
    result = accumulated[:, :points] / accumulated[:, points : points + 1]
    return result.astype(jnp.bfloat16)[None]


def solution(mesh):
    in_specs = (
        P("event", "dom", None, None, None),
        P("event", "dom", None, None),
        P("dom", "event", None),
        P(),
        P("dom", "event", None, None),
        P("dom", "event", None, None),
    )
    out_specs = P("dom", "event", None, None)
    return jax.shard_map(
        per_device, mesh=mesh, in_specs=in_specs, out_specs=out_specs, check_vma=False
    )
```

profile of v0, /device:TPU:320, one launch (start us, length us, event | category | flops | bytes accessed | tf_op | source)
XLA Modules:
  0.0 330.3 jit_solution(9981842817140324884)
XLA Ops:
  1.5 3.3 all-to-all-start.1
  5.5 6.8 %copy.34 = bf16[2,1,64,125,128]{4,3,1,0,2:T(8,128)(2,1)} copy(bf16[2,1,64,125,128]{4,2,3,1,0:T(8,128)(2,1)} %param.8) | data formatting | bytes 8192000 | tf_op args[0]
  12.3 5.8 %all-to-all-start = ((bf16[2,1,64,125,128]{4,3,1,0,2:T(8,128)(2,1)}), bf16[2,1,64,125,128]{4,3,1,0,2:T(8,128)(2,1)}, u32[]{:S(2)}, u32[]{:S(2)}) async-start(bf16[2,1,64,125,128]{4,3,1,0,2:T(8,128)(2,1)} %copy.34), calls=%async_computation | async-start | bytes 8388608 | tf_op jit(solution)/shard_map/all_to_all | solution.py:22
  18.2 4.3 %all-to-all-done = bf16[2,1,64,125,128]{4,3,1,0,2:T(8,128)(2,1)} async-done(((bf16[2,1,64,125,128]{4,3,1,0,2:T(8,128)(2,1)}), bf16[2,1,64,125,128]{4,3,1,0,2:T(8,128)(2,1)}, u32[]{:S(2)}, u32[]{:S(2)}) %all-to-all-start) | async-done | bytes 4096032 | tf_op jit(solution)/shard_map/all_to_all | solution.py:22
  22.5 3.4 %reduce_sum.37 = bf16[64,125,128]{2,1,0:T(8,128)(2,1)S(1)} reduce(bf16[2,1,64,125,128]{4,3,1,0,2:T(8,128)(2,1)} %all-to-all-done, bf16[]{:T(256)} %constant.7.clone.1), dimensions={0,1}, to_apply=%region_0.0 | reduce | flops 1024000 | bytes 6144002 | tf_op jit(solution)/shard_map/reduce_sum | solution.py:28
  28.9 3.4 %broadcast_in_dim.4 = f32[96,126,128]{2,1,0:T(8,128)} broadcast(f32[]{:T(128)} %constant.6.clone.1), dimensions={} | broadcast | bytes 6193156 | tf_op jit(solution)/shard_map/broadcast_in_dim | solution.py:46
  32.4 250.9 %while.11 = (s32[]{:T(128)}, f32[96,126,128]{2,1,0:T(8,128)}, s32[16]{0:T(128)S(1)}, s32[32,16]{0,1:T(8,128)}, s32[32,16]{0,1:T(8,128)}, /*index=5*/bf16[32,128,...) while((s32[]{:T(128)}, f32[96,126,128]{2,1,0:T(8,128)}, ...), condition=%wide.region_6.7_spmd.clone, body=%wide.region_4.6_spmd.clone.sunk | while | flops 132637920 | bytes 16569375 | solution.py:47
  37.6 2.2 convolution_bitcast_fusion.2
  39.8 2.0 copy.45
  41.9 6.3 %scatter_fusion = f32[96,126,128]{2,1,0:T(8,128)} fusion(f32[96,126,128]{2,1,0:T(8,128)} %get-tuple-element.156, s32[32]{0:T(128)S(1)} %get-tuple-element.143, f32[32,126,128]{2,1,0:T(8,128)S(1)} %copy.45), kind=kCustom, calls=%fused_computation.1.clone.clone.1 | custom fusion | flops 516096 | bytes 6193280 | tf_op jit(solution)/shard_map/while/body/eval_jaxpr/scatter-add | solution.py:44
  53.3 2.2 convolution_bitcast_fusion.2
  55.6 2.0 copy.45
  57.6 6.2 %scatter_fusion = f32[96,126,128]{2,1,0:T(8,128)} fusion(f32[96,126,128]{2,1,0:T(8,128)} %get-tuple-element.156, s32[32]{0:T(128)S(1)} %get-tuple-element.143, f32[32,126,128]{2,1,0:T(8,128)S(1)} %copy.45), kind=kCustom, calls=%fused_computation.1.clone.clone.1 | custom fusion | flops 516096 | bytes 6193280 | tf_op jit(solution)/shard_map/while/body/eval_jaxpr/scatter-add | solution.py:44
  69.0 2.2 convolution_bitcast_fusion.2
  71.2 2.0 copy.45
  73.2 6.1 %scatter_fusion = f32[96,126,128]{2,1,0:T(8,128)} fusion(f32[96,126,128]{2,1,0:T(8,128)} %get-tuple-element.156, s32[32]{0:T(128)S(1)} %get-tuple-element.143, f32[32,126,128]{2,1,0:T(8,128)S(1)} %copy.45), kind=kCustom, calls=%fused_computation.1.clone.clone.1 | custom fusion | flops 516096 | bytes 6193280 | tf_op jit(solution)/shard_map/while/body/eval_jaxpr/scatter-add | solution.py:44
  84.6 2.2 convolution_bitcast_fusion.2
  86.8 2.0 copy.45
  88.8 6.2 %scatter_fusion = f32[96,126,128]{2,1,0:T(8,128)} fusion(f32[96,126,128]{2,1,0:T(8,128)} %get-tuple-element.156, s32[32]{0:T(128)S(1)} %get-tuple-element.143, f32[32,126,128]{2,1,0:T(8,128)S(1)} %copy.45), kind=kCustom, calls=%fused_computation.1.clone.clone.1 | custom fusion | flops 516096 | bytes 6193280 | tf_op jit(solution)/shard_map/while/body/eval_jaxpr/scatter-add | solution.py:44
  100.2 2.2 convolution_bitcast_fusion.2
  104.5 6.1 %scatter_fusion = f32[96,126,128]{2,1,0:T(8,128)} fusion(f32[96,126,128]{2,1,0:T(8,128)} %get-tuple-element.156, s32[32]{0:T(128)S(1)} %get-tuple-element.143, f32[32,126,128]{2,1,0:T(8,128)S(1)} %copy.45), kind=kCustom, calls=%fused_computation.1.clone.clone.1 | custom fusion | flops 516096 | bytes 6193280 | tf_op jit(solution)/shard_map/while/body/eval_jaxpr/scatter-add | solution.py:44
  115.9 2.2 convolution_bitcast_fusion.2
  118.1 2.0 copy.45
  120.1 6.2 %scatter_fusion = f32[96,126,128]{2,1,0:T(8,128)} fusion(f32[96,126,128]{2,1,0:T(8,128)} %get-tuple-element.156, s32[32]{0:T(128)S(1)} %get-tuple-element.143, f32[32,126,128]{2,1,0:T(8,128)S(1)} %copy.45), kind=kCustom, calls=%fused_computation.1.clone.clone.1 | custom fusion | flops 516096 | bytes 6193280 | tf_op jit(solution)/shard_map/while/body/eval_jaxpr/scatter-add | solution.py:44
  131.5 2.2 convolution_bitcast_fusion.2
  135.8 6.2 %scatter_fusion = f32[96,126,128]{2,1,0:T(8,128)} fusion(f32[96,126,128]{2,1,0:T(8,128)} %get-tuple-element.156, s32[32]{0:T(128)S(1)} %get-tuple-element.143, f32[32,126,128]{2,1,0:T(8,128)S(1)} %copy.45), kind=kCustom, calls=%fused_computation.1.clone.clone.1 | custom fusion | flops 516096 | bytes 6193280 | tf_op jit(solution)/shard_map/while/body/eval_jaxpr/scatter-add | solution.py:44
  147.2 2.2 convolution_bitcast_fusion.2
  151.5 6.2 %scatter_fusion = f32[96,126,128]{2,1,0:T(8,128)} fusion(f32[96,126,128]{2,1,0:T(8,128)} %get-tuple-element.156, s32[32]{0:T(128)S(1)} %get-tuple-element.143, f32[32,126,128]{2,1,0:T(8,128)S(1)} %copy.45), kind=kCustom, calls=%fused_computation.1.clone.clone.1 | custom fusion | flops 516096 | bytes 6193280 | tf_op jit(solution)/shard_map/while/body/eval_jaxpr/scatter-add | solution.py:44
  162.9 2.2 convolution_bitcast_fusion.2
  167.2 6.2 %scatter_fusion = f32[96,126,128]{2,1,0:T(8,128)} fusion(f32[96,126,128]{2,1,0:T(8,128)} %get-tuple-element.156, s32[32]{0:T(128)S(1)} %get-tuple-element.143, f32[32,126,128]{2,1,0:T(8,128)S(1)} %copy.45), kind=kCustom, calls=%fused_computation.1.clone.clone.1 | custom fusion | flops 516096 | bytes 6193280 | tf_op jit(solution)/shard_map/while/body/eval_jaxpr/scatter-add | solution.py:44
  178.6 2.2 convolution_bitcast_fusion.2
  182.9 6.3 %scatter_fusion = f32[96,126,128]{2,1,0:T(8,128)} fusion(f32[96,126,128]{2,1,0:T(8,128)} %get-tuple-element.156, s32[32]{0:T(128)S(1)} %get-tuple-element.143, f32[32,126,128]{2,1,0:T(8,128)S(1)} %copy.45), kind=kCustom, calls=%fused_computation.1.clone.clone.1 | custom fusion | flops 516096 | bytes 6193280 | tf_op jit(solution)/shard_map/while/body/eval_jaxpr/scatter-add | solution.py:44
  194.4 2.2 convolution_bitcast_fusion.2
  198.7 6.2 %scatter_fusion = f32[96,126,128]{2,1,0:T(8,128)} fusion(f32[96,126,128]{2,1,0:T(8,128)} %get-tuple-element.156, s32[32]{0:T(128)S(1)} %get-tuple-element.143, f32[32,126,128]{2,1,0:T(8,128)S(1)} %copy.45), kind=kCustom, calls=%fused_computation.1.clone.clone.1 | custom fusion | flops 516096 | bytes 6193280 | tf_op jit(solution)/shard_map/while/body/eval_jaxpr/scatter-add | solution.py:44
  210.1 2.2 convolution_bitcast_fusion.2
  214.3 6.2 %scatter_fusion = f32[96,126,128]{2,1,0:T(8,128)} fusion(f32[96,126,128]{2,1,0:T(8,128)} %get-tuple-element.156, s32[32]{0:T(128)S(1)} %get-tuple-element.143, f32[32,126,128]{2,1,0:T(8,128)S(1)} %copy.45), kind=kCustom, calls=%fused_computation.1.clone.clone.1 | custom fusion | flops 516096 | bytes 6193280 | tf_op jit(solution)/shard_map/while/body/eval_jaxpr/scatter-add | solution.py:44
  225.8 2.2 convolution_bitcast_fusion.2
  230.0 6.2 %scatter_fusion = f32[96,126,128]{2,1,0:T(8,128)} fusion(f32[96,126,128]{2,1,0:T(8,128)} %get-tuple-element.156, s32[32]{0:T(128)S(1)} %get-tuple-element.143, f32[32,126,128]{2,1,0:T(8,128)S(1)} %copy.45), kind=kCustom, calls=%fused_computation.1.clone.clone.1 | custom fusion | flops 516096 | bytes 6193280 | tf_op jit(solution)/shard_map/while/body/eval_jaxpr/scatter-add | solution.py:44
  241.5 2.2 convolution_bitcast_fusion.2
  245.7 6.2 %scatter_fusion = f32[96,126,128]{2,1,0:T(8,128)} fusion(f32[96,126,128]{2,1,0:T(8,128)} %get-tuple-element.156, s32[32]{0:T(128)S(1)} %get-tuple-element.143, f32[32,126,128]{2,1,0:T(8,128)S(1)} %copy.45), kind=kCustom, calls=%fused_computation.1.clone.clone.1 | custom fusion | flops 516096 | bytes 6193280 | tf_op jit(solution)/shard_map/while/body/eval_jaxpr/scatter-add | solution.py:44
  257.2 2.2 convolution_bitcast_fusion.2
  261.4 6.2 %scatter_fusion = f32[96,126,128]{2,1,0:T(8,128)} fusion(f32[96,126,128]{2,1,0:T(8,128)} %get-tuple-element.156, s32[32]{0:T(128)S(1)} %get-tuple-element.143, f32[32,126,128]{2,1,0:T(8,128)S(1)} %copy.45), kind=kCustom, calls=%fused_computation.1.clone.clone.1 | custom fusion | flops 516096 | bytes 6193280 | tf_op jit(solution)/shard_map/while/body/eval_jaxpr/scatter-add | solution.py:44
  272.8 2.2 convolution_bitcast_fusion.2
  277.1 6.2 %scatter_fusion = f32[96,126,128]{2,1,0:T(8,128)} fusion(f32[96,126,128]{2,1,0:T(8,128)} %get-tuple-element.156, s32[32]{0:T(128)S(1)} %get-tuple-element.143, f32[32,126,128]{2,1,0:T(8,128)S(1)} %copy.45), kind=kCustom, calls=%fused_computation.1.clone.clone.1 | custom fusion | flops 516096 | bytes 6193280 | tf_op jit(solution)/shard_map/while/body/eval_jaxpr/scatter-add | solution.py:44
  283.3 6.6 %fusion.7 = (bf16[96,126,128]{2,0,1:T(8,128)(2,1)S(1)}, f32[96,126,128]{2,0,1:T(8,128)S(1)}) fusion(f32[96,126,128]{2,1,0:T(8,128)} %get-tuple-element.47), kind=kLoop, calls=%fused_computation.23 | loop fusion | flops 1548288 | bytes 15482880 | tf_op jit(solution)/shard_map/convert.4
  290.3 7.7 %collective-permute-start = (bf16[32,126,128]{2,0,1:T(8,128)(2,1)S(1)}, bf16[32,126,128]{2,0,1:T(8,128)(2,1)S(1)}, u32[]{:S(2)}, u32[]{:S(2)}) collective-permute-start(bf16[32,126,128]{2,0,1:T(8,128)(2,1)S(1)} %get-tuple-element.96), channel_id=1, source_target_pairs={{1,0},{2,1},{3,2},{4,3},{5,4},{6,5},{7,6},{8,7},{9,8},{10,9},{11,1... | collective-permute-start | bytes 3096584 | tf_op jit(solution)/shard_map/ppermute | solution.py:13
  299.9 20.5 %collective-permute-done = bf16[32,126,128]{2,0,1:T(8,128)(2,1)S(1)} collective-permute-done((bf16[32,126,128]{2,0,1:T(8,128)(2,1)S(1)}, bf16[32,126,128]{2,0,1:T(8,128)(2,1)S(1)}, u32[]{:S(2)}, u32[]{:S(2)}) %collective-permute-start) | collective-permute-done | bytes 1032224 | tf_op jit(solution)/shard_map/ppermute | solution.py:13
  320.3 8.3 %collective-permute-done.1 = bf16[32,126,128]{2,0,1:T(8,128)(2,1)S(1)} collective-permute-done((bf16[32,126,128]{2,0,1:T(8,128)(2,1)S(1)}, bf16[32,126,128]{2,0,1:T(8,128)(2,1)S(1)}, u32[]{:S(2)}, u32[]{:S(2)}) %collective-permute-start.1) | collective-permute-done | bytes 1032224 | tf_op jit(solution)/shard_map/ppermute | solution.py:13
  (94 shorter events, 83.9 us)
Async XLA Ops:
  1.5 10.7 %all-to-all-start.1 = ((bf16[2,1,64,128]{3,0,1,2:T(2,128)(2,1)}), bf16[2,1,64,128]{3,0,1,2:T(2,128)(2,1)S(1)}, u32[]{:S(2)}, u32[]{:S(2)}) async-start(bf16[2,1,64,128]{3,0,1,2:T(2,128)(2,1)} %copy_convert_fusion), calls=%async_computation.1 | async-start | bytes 65536 | tf_op jit(solution)/shard_map/all_to_all | solution.py:23
  12.3 10.2 %all-to-all-start = ((bf16[2,1,64,125,128]{4,3,1,0,2:T(8,128)(2,1)}), bf16[2,1,64,125,128]{4,3,1,0,2:T(8,128)(2,1)}, u32[]{:S(2)}, u32[]{:S(2)}) async-start(bf16[2,1,64,125,128]{4,3,1,0,2:T(8,128)(2,1)} %copy.34), calls=%async_computation | async-start | bytes 8388608 | tf_op jit(solution)/shard_map/all_to_all | solution.py:22
  27.7 0.7 copy-start
  290.3 30.1 %collective-permute-start = (bf16[32,126,128]{2,0,1:T(8,128)(2,1)S(1)}, bf16[32,126,128]{2,0,1:T(8,128)(2,1)S(1)}, u32[]{:S(2)}, u32[]{:S(2)}) collective-permute-start(bf16[32,126,128]{2,0,1:T(8,128)(2,1)S(1)} %get-tuple-element.96), channel_id=1, source_target_pairs={{1,0},{2,1},{3,2},{4,3},{5,4},{6,5},{7,6},{8,7},{9,8},{10,9},{11,1... | collective-permute-start | bytes 3096584 | tf_op jit(solution)/shard_map/ppermute | solution.py:13
  297.9 30.7 %collective-permute-start.1 = (bf16[32,126,128]{2,0,1:T(8,128)(2,1)S(1)}, bf16[32,126,128]{2,0,1:T(8,128)(2,1)S(1)}, u32[]{:S(2)}, u32[]{:S(2)}) collective-permute-start(bf16[32,126,128]{2,0,1:T(8,128)(2,1)S(1)} %get-tuple-element.97), channel_id=1, source_target_pairs={{0,1},{1,2},{2,3},{3,4},{4,5},{5,6},{6,7},{7,8},{8,9},{9,10},{10,1... | collective-permute-start | bytes 3096584 | tf_op jit(solution)/shard_map/ppermute | solution.py:13
where the time goes:
time: 335 us; the launch traced here: 330 us
  other arithmetic  126 us (38%)
  local copies, waits for them, and re-layouts  85.8 us (26%)
  matrix products  35.6 us (11%)
  waiting for transfers between devices  33.1 us (10%)
  loops' own time  31.4 us (9%)
  starting transfers between devices  18.6 us (6%)
    scatter-add x16, other arithmetic, add_pairs(): return (extended.at[targets].add(contrib), None)  99.2 us
    dot_general x16, matrix products, add_pairs(): jnp.einsum('bgs,bst->bgt', source, matrices, preferred_element_type=jnp.f...  35.6 us
    dot_general x16, local copies, waits for them, and re-layouts, add_pairs(): jnp.einsum('bgs,bst->bgt', source, matrices, preferred_element_type=jnp.f...  32.1 us
    gather x16, local copies, waits for them, and re-layouts, add_pairs(): matrices = tables[table_ids[:, which]]  31.6 us
    another operation x1, loops' own time, per_device(): lax.scan(add_pairs, start_buffer, jnp.arange(PB, dtype=jnp.int32))  31.4 us
    ppermute x2, waiting for transfers between devices, passed_along(): lax.ppermute(value, axis, [(source, source + steps) for source in range(f...  28.8 us
    select_n x16, other arithmetic, add_pairs(): return (extended.at[targets].add(contrib), None)  11.5 us
    ppermute x2, starting transfers between devices, passed_along(): lax.ppermute(value, axis, [(source, source + steps) for source in range(f...  9.58 us
  transfers between devices with their start and end apart: 4, of which 3 were waited for; matrix products, arithmetic and copies ran while one was open for 2% of the time, Pallas kernels for 0%

commit v1 on v0

v1 whole, which is shorter than its diff:
```python
import functools

import jax
import jax.numpy as jnp
from jax import lax
from jax.experimental import pallas as pl
from jax.experimental.pallas import tpu as pltpu
from jax.sharding import PartitionSpec as P


OWN = 32
G = 125
ROWS = 128
W = 128
PB = 16
CH = 8
NCH = OWN // CH
U = 4
LIST = 640
DUMMY = OWN << 16
COPY_ALIASED = False
MIB = 1 << 20


HBM = pl.BlockSpec(memory_space=pltpu.HBM)
VMEM = pl.BlockSpec(memory_space=pltpu.VMEM)
SMEM = pl.BlockSpec(memory_space=pltpu.SMEM)


def on_chip(shape, dtype):
    return pltpu.VMEM(shape, dtype)


def in_vmem(x):
    return pltpu.with_memory_space_constraint(x, pltpu.VMEM)


def in_hbm(x):
    return pltpu.with_memory_space_constraint(x, pltpu.HBM)


def params(mib):
    return pltpu.CompilerParams(vmem_limit_bytes=mib * MIB)


def cost(flops, nbytes):
    return pl.CostEstimate(flops=flops, bytes_accessed=nbytes, transcendentals=0)


def shifted(value, axis, steps):
    count = lax.axis_size(axis)
    first, last = (max(0, -steps), min(count, count - steps))
    return lax.ppermute(value, axis, [(source, source + steps) for source in range(first, last)])


OUTER = ((0, 0), (24, 8))
INNER = ((8, 0), (16, 8))


def fetch(kern, buf, sems, base, pieces):
    copies = [
        pltpu.make_async_copy(
            kern.at[:, 0, :, pl.ds(base + first, CH)],
            buf.at[:, :, pl.ds(place, CH)],
            sems.at[n],
        )
        for n, (first, place) in enumerate(pieces)
    ]
    for copy in copies:
        copy.start()
    return copies


def two_events(buf, place, out):
    total = buf[0, :, place : place + CH].astype(jnp.float32)
    total = total + buf[1, :, place : place + CH].astype(jnp.float32)
    out[0:G, place : place + CH] = total.astype(jnp.bfloat16)


def put_counts(cbuf, pieces, out):
    for first, place in pieces:
        total = cbuf[0, first : first + CH] + cbuf[1, first : first + CH]
        out[G, place : place + CH] = total.astype(jnp.float32).astype(jnp.bfloat16)


def send_outer_kernel(kern, counts, out, buf, cbuf, sems, csem):
    base = (1 - lax.axis_index("event")) * OWN
    copies = fetch(kern, buf, sems, base, OUTER)
    ccopy = pltpu.make_async_copy(counts.at[:, 0, pl.ds(base, OWN)], cbuf, csem)
    ccopy.start()
    for copy, (_, place) in zip(copies, OUTER):
        copy.wait()
        two_events(buf, place, out)
    ccopy.wait()
    put_counts(cbuf, OUTER, out)


def send_inner_kernel(
    kern, counts, off, tab, out, own_outer, own_inner, own_l, prev_l, next_l,
    buf, cbuf, sems, csem,
):
    me = lax.axis_index("event")
    other = 1 - me
    outer = fetch(kern, buf.at[0], sems.at[0], me * OWN, OUTER)
    others = fetch(kern, buf.at[1], sems.at[1], other * OWN, INNER)
    inner = fetch(kern, buf.at[2], sems.at[2], me * OWN, INNER)
    ccopies = [
        pltpu.make_async_copy(counts.at[:, 0, pl.ds(side * OWN, OWN)], cbuf.at[n], csem.at[n])
        for n, side in enumerate((me, other))
    ]
    for copy in ccopies:
        copy.start()

    first = 8
    lists = (prev_l, own_l, next_l)
    for ref in lists:
        ref[0] = first
    fill = (jnp.int32(first),) * 3
    for c in range(NCH):

        def block(j, fill):
            b = c * CH + j
            prev_n, own_n, next_n = fill
            for k in range(PB):
                x = b + off[0, 0, k, b]
                code = j | (tab[0, 0, k, b] << 8) | ((x & (OWN - 1)) << 16)
                for ref, n in zip(lists, (prev_n, own_n, next_n)):
                    ref[n] = code
                part = x >> 5
                prev_n = prev_n + (part == 0).astype(jnp.int32)
                own_n = own_n + (part == 1).astype(jnp.int32)
                next_n = next_n + (part == 2).astype(jnp.int32)
            return prev_n, own_n, next_n

        fill = lax.fori_loop(0, CH, block, fill)
        padded = []
        for ref, n in zip(lists, fill):
            for u in range(U - 1):
                ref[n + u] = DUMMY
            n = (n + (U - 1)) & ~(U - 1)
            ref[c + 1] = n
            padded.append(n)
        fill = tuple(padded)

    for copy in ccopies:
        copy.wait()
    for which, (copies, pieces, dst, side) in enumerate(
        ((outer, OUTER, own_outer, 0), (others, INNER, out, 1), (inner, INNER, own_inner, 0))
    ):
        for copy, (_, place) in zip(copies, pieces):
            copy.wait()
            two_events(buf.at[which], place, dst)
        put_counts(cbuf.at[side], pieces, dst)


def source_kernel(pieces, own, got, vol, low, high):
    for (first, place), dst in zip(pieces, (low, high)):
        span = slice(place, place + CH)
        v = vol[0, first : first + CH]
        hits = own[G, span].astype(jnp.float32) + got[G, span].astype(jnp.float32)
        factor = v.astype(jnp.float32) / jnp.sqrt(1.0 + hits)
        total = own[0:G, span].astype(jnp.float32) + got[0:G, span].astype(jnp.float32)
        dst[0:G] = (total * factor[None]).astype(jnp.bfloat16)
        dst[G] = v


def by_block(source, dst):
    x = source[...].astype(jnp.float32)
    x = jnp.concatenate([x, jnp.zeros((ROWS - G - 1, CH, W), jnp.float32)], axis=0)
    dst[...] = jnp.transpose(x, (1, 0, 2)).astype(jnp.bfloat16)


def add_terms(lst, c, source, tables, acc):
    start = lst[c]
    steps = (lst[c + 1] - start) >> 2

    def step(i, carry):
        at = start + i * U
        for u in range(U):
            code = lst[at + u]
            term = jnp.dot(
                source[code & (CH - 1)],
                tables[(code >> 8) & 31],
                preferred_element_type=jnp.float32,
            )
            x = code >> 16
            acc[x] = acc[x] + term
        return carry

    lax.fori_loop(0, steps, step, 0)


def own_kernel(lst, s0, s1, s2, s3, tables, acc, mats):
    def clear(i, carry):
        acc[i] = jnp.zeros((ROWS, W), jnp.float32)
        return carry

    lax.fori_loop(0, OWN + 1, clear, 0)
    for c, source in enumerate((s0, s1, s2, s3)):
        by_block(source, mats.at[c])
        add_terms(lst, c, mats.at[c], tables, acc)


def received_terms(step, next_l, prev_l, from_next, from_prev, tables, acc, mats):
    by_block(from_next, mats.at[0])
    by_block(from_prev, mats.at[1])
    add_terms(next_l, step, mats.at[0], tables, acc)
    add_terms(prev_l, NCH - 1 - step, mats.at[1], tables, acc)


def chunk_kernel(step, next_l, prev_l, from_next, from_prev, tables, acc_in, acc, mats):
    if COPY_ALIASED:
        acc[...] = acc_in[...]
    received_terms(step, next_l, prev_l, from_next, from_prev, tables, acc, mats)


def last_kernel(next_l, prev_l, from_next, from_prev, tables, acc_in, out, acc, mats, stage, sem):
    if COPY_ALIASED:
        acc[...] = acc_in[...]
    received_terms(NCH - 1, next_l, prev_l, from_next, from_prev, tables, acc, mats)
    for c in range(NCH):
        span = slice(c * CH, c * CH + CH)
        scale = 1.0 / acc[span, G : G + 1]
        result = jnp.transpose(acc[span] * scale, (1, 0, 2))
        stage[:, span] = result[0:G].astype(jnp.bfloat16)
    copy = pltpu.make_async_copy(stage, out.at[0], sem)
    copy.start()
    copy.wait()


def per_device(kernels, counts, volume, tables, pair_offset, pair_table):
    bf16, f32, i32 = jnp.bfloat16, jnp.float32, jnp.int32
    dma = pltpu.SemaphoreType.DMA
    half = 2 * CH
    kernels = in_hbm(jnp.transpose(kernels, (0, 1, 3, 2, 4)))
    pair_offset = jnp.transpose(pair_offset, (0, 1, 3, 2))
    pair_table = jnp.transpose(pair_table, (0, 1, 3, 2))
    swap = [(0, 1), (1, 0)]

    to_outer = pl.pallas_call(
        send_outer_kernel,
        out_shape=on_chip((G + 1, half, W), bf16),
        in_specs=[HBM, HBM],
        out_specs=VMEM,
        scratch_shapes=[
            pltpu.VMEM((2, G, half, W), bf16),
            pltpu.VMEM((2, OWN, W), i32),
            dma((2,)),
            dma,
        ],
        compiler_params=params(8),
        cost_estimate=cost(1 << 20, 1 << 20),
        name="send_outer",
    )(kernels, counts)
    got_outer = lax.ppermute(to_outer, "event", swap)

    to_inner, own_outer, own_inner, own_l, prev_l, next_l = pl.pallas_call(
        send_inner_kernel,
        out_shape=[on_chip((G + 1, half, W), bf16)] * 3
        + [jax.ShapeDtypeStruct((LIST,), i32)] * 3,
        in_specs=[HBM, HBM, SMEM, SMEM],
        out_specs=[VMEM] * 3 + [SMEM] * 3,
        scratch_shapes=[
            pltpu.VMEM((3, 2, G, half, W), bf16),
            pltpu.VMEM((2, 2, OWN, W), i32),
            dma((3, 2)),
            dma((2,)),
        ],
        compiler_params=params(8),
        cost_estimate=cost(1 << 20, 6 << 20),
        name="send_inner",
    )(kernels, counts, pair_offset, pair_table)
    got_inner = lax.ppermute(to_inner, "event", swap)

    def source(pieces, own, got):
        return pl.pallas_call(
            functools.partial(source_kernel, pieces),
            out_shape=[on_chip((G + 1, CH, W), bf16)] * 2,
            in_specs=[VMEM] * 3,
            out_specs=[VMEM] * 2,
            compiler_params=params(4),
            cost_estimate=cost(1 << 20, 1 << 20),
        )(own, in_vmem(got), volume)

    def moved(value, steps):
        return shifted(value, "dom", steps)

    s0, s3 = source(OUTER, own_outer, got_outer)
    next_0 = moved(s0, -1)
    prev_0 = moved(s3, 1)
    s1, s2 = source(INNER, own_inner, got_inner)
    lists_next = moved(prev_l, -1)
    lists_prev = moved(next_l, 1)
    from_next = [next_0] + [moved(s, -1) for s in (s1, s2, s3)]
    from_prev = [prev_0] + [moved(s, 1) for s in (s2, s1, s0)]

    acc_shape = on_chip((OWN + 1, ROWS, W), f32)
    term = 2 * ROWS * W * W
    acc = pl.pallas_call(
        own_kernel,
        out_shape=acc_shape,
        in_specs=[SMEM] + [VMEM] * 5,
        out_specs=VMEM,
        scratch_shapes=[pltpu.VMEM((NCH, CH, ROWS, W), bf16)],
        compiler_params=params(4),
        cost_estimate=cost(256 * term, 16 << 20),
        name="own_terms",
    )(own_l, s0, s1, s2, s3, tables)
    mats = pltpu.VMEM((2, CH, ROWS, W), bf16)
    for step in range(NCH - 1):
        acc = pl.pallas_call(
            functools.partial(chunk_kernel, step),
            out_shape=acc_shape,
            in_specs=[SMEM, SMEM] + [VMEM] * 4,
            out_specs=VMEM,
            scratch_shapes=[mats],
            input_output_aliases={5: 0},
            compiler_params=params(4),
            cost_estimate=cost(64 * term, 4 << 20),
        )(lists_next, lists_prev, in_vmem(from_next[step]), in_vmem(from_prev[step]), tables, acc)
    out, _ = pl.pallas_call(
        last_kernel,
        out_shape=[jax.ShapeDtypeStruct((1, G, OWN, W), bf16), acc_shape],
        in_specs=[SMEM, SMEM] + [VMEM] * 4,
        out_specs=[HBM, VMEM],
        input_output_aliases={5: 1},
        scratch_shapes=[mats, pltpu.VMEM((G, OWN, W), bf16), dma],
        compiler_params=params(4),
        cost_estimate=cost(16 * term, 4 << 20),
        name="terms_last",
    )(lists_next, lists_prev, in_vmem(from_next[-1]), in_vmem(from_prev[-1]), tables, acc)
    return jnp.transpose(out, (0, 2, 1, 3))


def solution(mesh):
    in_specs = (
        P("event", "dom", None, None, None),
        P("event", "dom", None, None),
        P("dom", "event", None),
        P(),
        P("dom", "event", None, None),
        P("dom", "event", None, None),
    )
    return jax.shard_map(
        per_device,
        mesh=mesh,
        in_specs=in_specs,
        out_specs=P("dom", "event", None, None),
        check_vma=False,
    )
```

time: 335 us -> 106 us (0.32)
  the two profiles are of different devices: /device:TPU:320 before, /device:TPU:254 now
where the time goes in v1:
time: 106 us; the launch traced here: 105 us
  starting transfers between devices  53.2 us (50%)
  Pallas kernels  38.2 us (36%)
  waiting for transfers between devices  12.6 us (12%)
    ppermute x10, starting transfers between devices, shifted(): lax.ppermute(value, axis, [(source, source + steps) for source in range(f...  48.9 us
    pallas_call x1, Pallas kernels, per_device(): pl.pallas_call(own_kernel, out_shape=acc_shape, in_specs=[SMEM] + [VMEM]...  14 us
    pallas_call x3, Pallas kernels, per_device(): pl.pallas_call(functools.partial(chunk_kernel, step), out_shape=acc_shape...  13.3 us
    ppermute x10, waiting for transfers between devices, shifted(): lax.ppermute(value, axis, [(source, source + steps) for source in range(f...  12.6 us
    pallas_call x1, Pallas kernels, per_device(): pl.pallas_call(send_inner_kernel, out_shape=[on_chip((G + 1, half, W), bf...  6.11 us
    pallas_call x1, Pallas kernels, per_device(): pl.pallas_call(last_kernel, out_shape=[jax.ShapeDtypeStruct((1, G, OWN, W...  3.1 us
    ppermute x1, starting transfers between devices, per_device(): got_inner = lax.ppermute(to_inner, 'event', swap)  2.41 us
  transfers between devices with their start and end apart: 12, of which 2 were waited for; matrix products, arithmetic and copies ran while one was open for 0% of the time, Pallas kernels for 32%

profile of v1, /device:TPU:254, one launch (start us, length us, event | category | flops | bytes accessed | tf_op | source)
XLA Modules:
  0.0 105.2 jit_solution(9237901738303490865)
XLA Ops:
  0.0 0.0 copy-start.1
  0.0 0.8 copy-done.1
  0.8 0.0 copy-start.3
  0.8 0.0 copy-start.4
  0.8 1.3 %send_outer.1 = bf16[126,16,128]{2,1,0:T(8,128)(2,1)S(1)} custom-call(bf16[2,1,125,64,128]{4,3,2,1,0:T(8,128)(2,1)} %bitcast.6, s32[2,1,64,128]{3,2,1,0:T(8,128)S(1)} %copy-done.1), custom_call_target="tpu_custom_call" | custom-call | flops 1048576 | bytes 1048576 | tf_op jit(solution)/shard_map/send_outer/pallas_call | solution.py:240
  2.2 0.0 copy-start.2
  2.2 1.9 %collective-permute-start.2 = (bf16[126,16,128]{2,1,0:T(8,128)(2,1)S(1)}, bf16[126,16,128]{2,1,0:T(8,128)(2,1)S(1)}, u32[]{:S(2)}, u32[]{:S(2)}) collective-permute-start(bf16[126,16,128]{2,1,0:T(8,128)(2,1)S(1)} %send_outer.1), channel_id=1, source_target_pairs={{0,256},{256,0},{1,257},{257,1},{2,258},{258,2},{3,259},{259,3},{4... | collective-permute-start | bytes 1548296 | tf_op jit(solution)/shard_map/ppermute | solution.py:255
  4.1 0.0 copy-done.3
  4.1 0.0 copy-done.4
  4.1 0.0 copy-start
  4.2 6.1 %send_inner.1 = (bf16[126,16,128]{2,1,0:T(8,128)(2,1)S(1)}, bf16[126,16,128]{2,1,0:T(8,128)(2,1)S(1)}, bf16[126,16,128]{2,1,0:T(8,128)(2,1)S(1)}, s32[640]{0:T(1...) custom-call(bf16[2,1,125,64,128]{4,3,2,1,0:T(8,128)(2,1)} %bitcast.7, s32[2,1,64,128]{3,2,1,0:T(8,128)S(1)} %copy-done.1, ...), custom_call_target="tpu_custom_call" | custom-call | flops 1048576 | bytes 6291456 | tf_op jit(solution)/shard_map/send_inner/pallas_call | solution.py:257
  10.3 2.4 %collective-permute-start.5 = (bf16[126,16,128]{2,1,0:T(8,128)(2,1)S(1)}, bf16[126,16,128]{2,1,0:T(8,128)(2,1)S(1)}, u32[]{:S(2)}, u32[]{:S(2)}) collective-permute-start(bf16[126,16,128]{2,1,0:T(8,128)(2,1)S(1)} %get-tuple-element.22), channel_id=1, source_target_pairs={{0,256},{256,0},{1,257},{257,1},{2,258},{258,2},{3,259},{259,3},{4... | collective-permute-start | bytes 1548296 | tf_op jit(solution)/shard_map/ppermute | solution.py:273
  12.7 0.0 collective-permute-done.2.got
  12.7 0.0 copy-done.2
  12.7 0.2 shard_map.64
  12.9 2.7 %collective-permute-start.10 = (bf16[126,8,128]{2,1,0:T(8,128)(2,1)S(1)}, bf16[126,8,128]{2,1,0:T(8,128)(2,1)S(1)}, u32[]{:S(2)}, u32[]{:S(2)}) collective-permute-start(bf16[126,8,128]{2,1,0:T(8,128)(2,1)S(1)} %get-tuple-element.20.s0), channel_id=1, source_target_pairs={{1,0},{2,1},{3,2},{4,3},{5,4},{6,5},{7,6},{8,7},{9,8},{10,9},{11,1... | collective-permute-start | bytes 774152 | tf_op jit(solution)/shard_map/ppermute | solution.py:53
  15.6 8.5 %collective-permute-start.11 = (bf16[126,8,128]{2,1,0:T(8,128)(2,1)S(1)}, bf16[126,8,128]{2,1,0:T(8,128)(2,1)S(1)}, u32[]{:S(2)}, u32[]{:S(2)}) collective-permute-start(bf16[126,8,128]{2,1,0:T(8,128)(2,1)S(1)} %get-tuple-element.19.s3), channel_id=1, source_target_pairs={{0,1},{1,2},{2,3},{3,4},{4,5},{5,6},{6,7},{7,8},{8,9},{9,10},{10,1... | collective-permute-start | bytes 774152 | tf_op jit(solution)/shard_map/ppermute | solution.py:53
  24.2 0.0 collective-permute-done.5.got
  24.2 0.2 shard_map.65
  24.3 1.9 %collective-permute-start.8 = (bf16[126,8,128]{2,1,0:T(8,128)(2,1)S(1)}, bf16[126,8,128]{2,1,0:T(8,128)(2,1)S(1)}, u32[]{:S(2)}, u32[]{:S(2)}) collective-permute-start(bf16[126,8,128]{2,1,0:T(8,128)(2,1)S(1)} %get-tuple-element.24.s1), channel_id=1, source_target_pairs={{1,0},{2,1},{3,2},{4,3},{5,4},{6,5},{7,6},{8,7},{9,8},{10,9},{11,1... | collective-permute-start | bytes 774152 | tf_op jit(solution)/shard_map/ppermute | solution.py:53
  26.3 9.4 %collective-permute-start.9 = (bf16[126,8,128]{2,1,0:T(8,128)(2,1)S(1)}, bf16[126,8,128]{2,1,0:T(8,128)(2,1)S(1)}, u32[]{:S(2)}, u32[]{:S(2)}) collective-permute-start(bf16[126,8,128]{2,1,0:T(8,128)(2,1)S(1)} %get-tuple-element.23.s2), channel_id=1, source_target_pairs={{0,1},{1,2},{2,3},{3,4},{4,5},{5,6},{6,7},{7,8},{8,9},{9,10},{10,1... | collective-permute-start | bytes 774152 | tf_op jit(solution)/shard_map/ppermute | solution.py:53
  35.6 1.9 %collective-permute-start = (s32[640]{0:T(1024)S(1)}, s32[640]{0:T(1024)S(1)}, u32[]{:S(2)}, u32[]{:S(2)}) collective-permute-start(s32[640]{0:T(1024)S(1)} %get-tuple-element.16), channel_id=1, source_target_pairs={{1,0},{2,1},{3,2},{4,3},{5,4},{6,5},{7,6},{8,7},{9,8},{10,9},{11,1... | collective-permute-start | bytes 7688 | tf_op jit(solution)/shard_map/ppermute | solution.py:53
  37.6 9.0 %collective-permute-done.next_l = s32[640]{0:T(1024)S(1)} collective-permute-done((s32[640]{0:T(1024)S(1)}, s32[640]{0:T(1024)S(1)}, u32[]{:S(2)}, u32[]{:S(2)}) %collective-permute-start) | collective-permute-done | bytes 2592 | tf_op jit(solution)/shard_map/ppermute | solution.py:53
  46.6 1.9 %collective-permute-start.1 = (s32[640]{0:T(1024)S(1)}, s32[640]{0:T(1024)S(1)}, u32[]{:S(2)}, u32[]{:S(2)}) collective-permute-start(s32[640]{0:T(1024)S(1)} %get-tuple-element.17), channel_id=1, source_target_pairs={{0,1},{1,2},{2,3},{3,4},{4,5},{5,6},{6,7},{7,8},{8,9},{9,10},{10,1... | collective-permute-start | bytes 7688 | tf_op jit(solution)/shard_map/ppermute | solution.py:53
  48.5 3.6 %collective-permute-done.1.prev_l = s32[640]{0:T(1024)S(1)} collective-permute-done((s32[640]{0:T(1024)S(1)}, s32[640]{0:T(1024)S(1)}, u32[]{:S(2)}, u32[]{:S(2)}) %collective-permute-start.1) | collective-permute-done | bytes 2592 | tf_op jit(solution)/shard_map/ppermute | solution.py:53
  52.1 1.9 %collective-permute-start.6 = (bf16[126,8,128]{2,1,0:T(8,128)(2,1)S(1)}, bf16[126,8,128]{2,1,0:T(8,128)(2,1)S(1)}, u32[]{:S(2)}, u32[]{:S(2)}) collective-permute-start(bf16[126,8,128]{2,1,0:T(8,128)(2,1)S(1)} %get-tuple-element.23.s2), channel_id=1, source_target_pairs={{1,0},{2,1},{3,2},{4,3},{5,4},{6,5},{7,6},{8,7},{9,8},{10,9},{11,1... | collective-permute-start | bytes 774152 | tf_op jit(solution)/shard_map/ppermute | solution.py:53
  54.0 0.0 collective-permute-done.10.from_next
  54.0 9.4 %collective-permute-start.7 = (bf16[126,8,128]{2,1,0:T(8,128)(2,1)S(1)}, bf16[126,8,128]{2,1,0:T(8,128)(2,1)S(1)}, u32[]{:S(2)}, u32[]{:S(2)}) collective-permute-start(bf16[126,8,128]{2,1,0:T(8,128)(2,1)S(1)} %get-tuple-element.24.s1), channel_id=1, source_target_pairs={{0,1},{1,2},{2,3},{3,4},{4,5},{5,6},{6,7},{7,8},{8,9},{9,10},{10,1... | collective-permute-start | bytes 774152 | tf_op jit(solution)/shard_map/ppermute | solution.py:53
  63.3 0.0 collective-permute-done.11.from_prev
  63.4 1.9 %collective-permute-start.3 = (bf16[126,8,128]{2,1,0:T(8,128)(2,1)S(1)}, bf16[126,8,128]{2,1,0:T(8,128)(2,1)S(1)}, u32[]{:S(2)}, u32[]{:S(2)}) collective-permute-start(bf16[126,8,128]{2,1,0:T(8,128)(2,1)S(1)} %get-tuple-element.19.s3), channel_id=1, source_target_pairs={{1,0},{2,1},{3,2},{4,3},{5,4},{6,5},{7,6},{8,7},{9,8},{10,9},{11,1... | collective-permute-start | bytes 774152 | tf_op jit(solution)/shard_map/ppermute | solution.py:53
  65.3 0.0 collective-permute-done.8.from_next
  65.3 9.4 %collective-permute-start.4 = (bf16[126,8,128]{2,1,0:T(8,128)(2,1)S(1)}, bf16[126,8,128]{2,1,0:T(8,128)(2,1)S(1)}, u32[]{:S(2)}, u32[]{:S(2)}) collective-permute-start(bf16[126,8,128]{2,1,0:T(8,128)(2,1)S(1)} %get-tuple-element.20.s0), channel_id=1, source_target_pairs={{0,1},{1,2},{2,3},{3,4},{4,5},{5,6},{6,7},{7,8},{8,9},{9,10},{10,1... | collective-permute-start | bytes 774152 | tf_op jit(solution)/shard_map/ppermute | solution.py:53
  74.7 0.0 copy-done
  74.7 14.0 %own_terms.1.acc_in = f32[33,128,128]{2,1,0:T(8,128)S(1)} custom-call(s32[640]{0:T(1024)S(1)} %get-tuple-element.25.lst, bf16[126,8,128]{2,1,0:T(8,128)(2,1)S(1)} %get-tuple-element.20.s0, bf16[126,8,128]{2,1,0:T(8,128)(2,1)S(1)} %get-tuple-element.24.s1, bf16[126,8,128]{2,1,0:T(8,128)(2,1)S(1)} %get-tuple-element.23.s2, ...), custom_call_target="tpu_custom_call" | custom-call | flops 1073741824 | bytes 16777216 | tf_op jit(solution)/shard_map/own_terms/pallas_call | solution.py:299
  88.7 5.5 %shard_map.66.acc_in = f32[33,128,128]{2,1,0:T(8,128)S(1)} custom-call(s32[640]{0:T(1024)S(1)} %collective-permute-done.next_l, s32[640]{0:T(1024)S(1)} %collective-permute-done.1.prev_l, bf16[126,8,128]{2,1,0:T(8,128)(2,1)S(1)} %collective-permute-done.10.from_next, ...), custom_call_target="tpu_custom_call", output_to_operand_aliasing={{}: (5, {})} | custom-call | flops 268435456 | bytes 4194304 | tf_op jit(solution)/shard_map/pallas_call | solution.py:311
  94.1 0.0 collective-permute-done.9.from_prev
  94.2 4.6 %shard_map.67.acc_in = f32[33,128,128]{2,1,0:T(8,128)S(1)} custom-call(s32[640]{0:T(1024)S(1)} %collective-permute-done.next_l, s32[640]{0:T(1024)S(1)} %collective-permute-done.1.prev_l, bf16[126,8,128]{2,1,0:T(8,128)(2,1)S(1)} %collective-permute-done.8.from_next, ...), custom_call_target="tpu_custom_call", output_to_operand_aliasing={{}: (5, {})} | custom-call | flops 268435456 | bytes 4194304 | tf_op jit(solution)/shard_map/pallas_call | solution.py:311
  98.7 0.0 collective-permute-done.6.from_next
  98.7 0.0 collective-permute-done.7.from_prev
  98.8 3.3 %shard_map.68.acc_in = f32[33,128,128]{2,1,0:T(8,128)S(1)} custom-call(s32[640]{0:T(1024)S(1)} %collective-permute-done.next_l, s32[640]{0:T(1024)S(1)} %collective-permute-done.1.prev_l, bf16[126,8,128]{2,1,0:T(8,128)(2,1)S(1)} %collective-permute-done.6.from_next, ...), custom_call_target="tpu_custom_call", output_to_operand_aliasing={{}: (5, {})} | custom-call | flops 268435456 | bytes 4194304 | tf_op jit(solution)/shard_map/pallas_call | solution.py:311
  102.0 0.0 collective-permute-done.3.from_next
  102.0 0.0 collective-permute-done.4.from_prev
  102.1 3.1 %terms_last.1 = (bf16[1,125,32,128]{3,2,1,0:T(8,128)(2,1)}, f32[33,128,128]{2,1,0:T(8,128)S(1)}) custom-call(s32[640]{0:T(1024)S(1)} %collective-permute-done.next_l, s32[640]{0:T(1024)S(1)} %collective-permute-done.1.prev_l, bf16[126,8,128]{2,1,0:T(8,128)(2,1)S(1)} %collective-permute-done.3.from_next, ...), custom_call_target="tpu_custom_call", output_to_operand_aliasing={{1}: (5, {})} | custom-call | flops 67108864 | bytes 4194304 | tf_op jit(solution)/shard_map/terms_last/pallas_call | solution.py:321
Async XLA Ops:
  0.0 0.8 copy-start.1
  0.8 3.3 %copy-start.3 = (s32[1,1,32,16]{2,3,1,0:T(8,128)S(1)}, s32[1,1,32,16]{2,3,1,0:T(8,128)}, u32[]{:S(2)}) copy-start(s32[1,1,32,16]{2,3,1,0:T(8,128)} %param.10) | copy-start | bytes 6148
  0.8 3.3 %copy-start.4 = (s32[1,1,32,16]{2,3,1,0:T(8,128)S(1)}, s32[1,1,32,16]{2,3,1,0:T(8,128)}, u32[]{:S(2)}) copy-start(s32[1,1,32,16]{2,3,1,0:T(8,128)} %param.11) | copy-start | bytes 6148
  2.2 10.5 %copy-start.2 = (bf16[1,32,128]{2,1,0:T(8,128)(2,1)S(1)}, bf16[1,32,128]{2,1,0:T(8,128)(2,1)}, u32[]{:S(2)}) copy-start(bf16[1,32,128]{2,1,0:T(8,128)(2,1)} %vol.3) | copy-start | bytes 24580
  2.2 10.5 %collective-permute-start.2 = (bf16[126,16,128]{2,1,0:T(8,128)(2,1)S(1)}, bf16[126,16,128]{2,1,0:T(8,128)(2,1)S(1)}, u32[]{:S(2)}, u32[]{:S(2)}) collective-permute-start(bf16[126,16,128]{2,1,0:T(8,128)(2,1)S(1)} %send_outer.1), channel_id=1, source_target_pairs={{0,256},{256,0},{1,257},{257,1},{2,258},{258,2},{3,259},{259,3},{4... | collective-permute-start | bytes 1548296 | tf_op jit(solution)/shard_map/ppermute | solution.py:255
  4.1 70.5 %copy-start = (bf16[32,128,128]{2,1,0:T(8,128)(2,1)S(1)}, bf16[32,128,128]{2,1,0:T(8,128)(2,1)}, u32[]{:S(2)}) copy-start(bf16[32,128,128]{2,1,0:T(8,128)(2,1)} %tables.9) | copy-start | bytes 3145732
  10.3 13.9 %collective-permute-start.5 = (bf16[126,16,128]{2,1,0:T(8,128)(2,1)S(1)}, bf16[126,16,128]{2,1,0:T(8,128)(2,1)S(1)}, u32[]{:S(2)}, u32[]{:S(2)}) collective-permute-start(bf16[126,16,128]{2,1,0:T(8,128)(2,1)S(1)} %get-tuple-element.22), channel_id=1, source_target_pairs={{0,256},{256,0},{1,257},{257,1},{2,258},{258,2},{3,259},{259,3},{4... | collective-permute-start | bytes 1548296 | tf_op jit(solution)/shard_map/ppermute | solution.py:273
  12.9 41.1 %collective-permute-start.10 = (bf16[126,8,128]{2,1,0:T(8,128)(2,1)S(1)}, bf16[126,8,128]{2,1,0:T(8,128)(2,1)S(1)}, u32[]{:S(2)}, u32[]{:S(2)}) collective-permute-start(bf16[126,8,128]{2,1,0:T(8,128)(2,1)S(1)} %get-tuple-element.20.s0), channel_id=1, source_target_pairs={{1,0},{2,1},{3,2},{4,3},{5,4},{6,5},{7,6},{8,7},{9,8},{10,9},{11,1... | collective-permute-start | bytes 774152 | tf_op jit(solution)/shard_map/ppermute | solution.py:53
  15.6 47.7 %collective-permute-start.11 = (bf16[126,8,128]{2,1,0:T(8,128)(2,1)S(1)}, bf16[126,8,128]{2,1,0:T(8,128)(2,1)S(1)}, u32[]{:S(2)}, u32[]{:S(2)}) collective-permute-start(bf16[126,8,128]{2,1,0:T(8,128)(2,1)S(1)} %get-tuple-element.19.s3), channel_id=1, source_target_pairs={{0,1},{1,2},{2,3},{3,4},{4,5},{5,6},{6,7},{7,8},{8,9},{9,10},{10,1... | collective-permute-start | bytes 774152 | tf_op jit(solution)/shard_map/ppermute | solution.py:53
  24.3 40.9 %collective-permute-start.8 = (bf16[126,8,128]{2,1,0:T(8,128)(2,1)S(1)}, bf16[126,8,128]{2,1,0:T(8,128)(2,1)S(1)}, u32[]{:S(2)}, u32[]{:S(2)}) collective-permute-start(bf16[126,8,128]{2,1,0:T(8,128)(2,1)S(1)} %get-tuple-element.24.s1), channel_id=1, source_target_pairs={{1,0},{2,1},{3,2},{4,3},{5,4},{6,5},{7,6},{8,7},{9,8},{10,9},{11,1... | collective-permute-start | bytes 774152 | tf_op jit(solution)/shard_map/ppermute | solution.py:53
  26.3 67.9 %collective-permute-start.9 = (bf16[126,8,128]{2,1,0:T(8,128)(2,1)S(1)}, bf16[126,8,128]{2,1,0:T(8,128)(2,1)S(1)}, u32[]{:S(2)}, u32[]{:S(2)}) collective-permute-start(bf16[126,8,128]{2,1,0:T(8,128)(2,1)S(1)} %get-tuple-element.23.s2), channel_id=1, source_target_pairs={{0,1},{1,2},{2,3},{3,4},{4,5},{5,6},{6,7},{7,8},{8,9},{9,10},{10,1... | collective-permute-start | bytes 774152 | tf_op jit(solution)/shard_map/ppermute | solution.py:53
  35.6 10.9 %collective-permute-start = (s32[640]{0:T(1024)S(1)}, s32[640]{0:T(1024)S(1)}, u32[]{:S(2)}, u32[]{:S(2)}) collective-permute-start(s32[640]{0:T(1024)S(1)} %get-tuple-element.16), channel_id=1, source_target_pairs={{1,0},{2,1},{3,2},{4,3},{5,4},{6,5},{7,6},{8,7},{9,8},{10,9},{11,1... | collective-permute-start | bytes 7688 | tf_op jit(solution)/shard_map/ppermute | solution.py:53
  46.6 5.5 %collective-permute-start.1 = (s32[640]{0:T(1024)S(1)}, s32[640]{0:T(1024)S(1)}, u32[]{:S(2)}, u32[]{:S(2)}) collective-permute-start(s32[640]{0:T(1024)S(1)} %get-tuple-element.17), channel_id=1, source_target_pairs={{0,1},{1,2},{2,3},{3,4},{4,5},{5,6},{6,7},{7,8},{8,9},{9,10},{10,1... | collective-permute-start | bytes 7688 | tf_op jit(solution)/shard_map/ppermute | solution.py:53
  52.1 46.7 %collective-permute-start.6 = (bf16[126,8,128]{2,1,0:T(8,128)(2,1)S(1)}, bf16[126,8,128]{2,1,0:T(8,128)(2,1)S(1)}, u32[]{:S(2)}, u32[]{:S(2)}) collective-permute-start(bf16[126,8,128]{2,1,0:T(8,128)(2,1)S(1)} %get-tuple-element.23.s2), channel_id=1, source_target_pairs={{1,0},{2,1},{3,2},{4,3},{5,4},{6,5},{7,6},{8,7},{9,8},{10,9},{11,1... | collective-permute-start | bytes 774152 | tf_op jit(solution)/shard_map/ppermute | solution.py:53
  54.0 44.8 %collective-permute-start.7 = (bf16[126,8,128]{2,1,0:T(8,128)(2,1)S(1)}, bf16[126,8,128]{2,1,0:T(8,128)(2,1)S(1)}, u32[]{:S(2)}, u32[]{:S(2)}) collective-permute-start(bf16[126,8,128]{2,1,0:T(8,128)(2,1)S(1)} %get-tuple-element.24.s1), channel_id=1, source_target_pairs={{0,1},{1,2},{2,3},{3,4},{4,5},{5,6},{6,7},{7,8},{8,9},{9,10},{10,1... | collective-permute-start | bytes 774152 | tf_op jit(solution)/shard_map/ppermute | solution.py:53
  63.4 38.7 %collective-permute-start.3 = (bf16[126,8,128]{2,1,0:T(8,128)(2,1)S(1)}, bf16[126,8,128]{2,1,0:T(8,128)(2,1)S(1)}, u32[]{:S(2)}, u32[]{:S(2)}) collective-permute-start(bf16[126,8,128]{2,1,0:T(8,128)(2,1)S(1)} %get-tuple-element.19.s3), channel_id=1, source_target_pairs={{1,0},{2,1},{3,2},{4,3},{5,4},{6,5},{7,6},{8,7},{9,8},{10,9},{11,1... | collective-permute-start | bytes 774152 | tf_op jit(solution)/shard_map/ppermute | solution.py:53
  65.3 36.8 %collective-permute-start.4 = (bf16[126,8,128]{2,1,0:T(8,128)(2,1)S(1)}, bf16[126,8,128]{2,1,0:T(8,128)(2,1)S(1)}, u32[]{:S(2)}, u32[]{:S(2)}) collective-permute-start(bf16[126,8,128]{2,1,0:T(8,128)(2,1)S(1)} %get-tuple-element.20.s0), channel_id=1, source_target_pairs={{0,1},{1,2},{2,3},{3,4},{4,5},{5,6},{6,7},{7,8},{8,9},{9,10},{10,1... | collective-permute-start | bytes 774152 | tf_op jit(solution)/shard_map/ppermute | solution.py:53

commit v2 on v0

v2 whole, which is shorter than its diff:
```python
import jax
import jax.numpy as jnp
from jax import lax
from jax.experimental import pallas as pl
from jax.experimental.pallas import tpu as pltpu
from jax.sharding import PartitionSpec as P


OWN = 32
HALF = OWN // 2
G = 125
ADJ = G + 1
ROWS = 128
W = 128
PB = 16
K = 4
T = 4
LIST = OWN + 8
OWN_LANE = 2 * OWN
MIB = 1 << 20
COPY_ALIASED = False


HBM = pl.BlockSpec(memory_space=pltpu.HBM)
VMEM = pl.BlockSpec(memory_space=pltpu.VMEM)
SMEM = pl.BlockSpec(memory_space=pltpu.SMEM)


def on_chip(shape, dtype):
    return pltpu.VMEM(shape, dtype)


def in_vmem(x):
    return pltpu.with_memory_space_constraint(x, pltpu.VMEM)


def in_hbm(x):
    return pltpu.with_memory_space_constraint(x, pltpu.HBM)


def params(mib):
    return pltpu.CompilerParams(vmem_limit_bytes=mib * MIB)


def cost(flops, nbytes):
    return pl.CostEstimate(flops=flops, bytes_accessed=nbytes, transcendentals=0)


def partial_sums(kern, counts, base, out, buf, cbuf, sems, csem):
    copies = []
    for n in range(2):
        copies.append(
            pltpu.make_async_copy(
                kern.at[:, 0, :, pl.ds(base + n * HALF, HALF)],
                buf.at[:, :, pl.ds(n * HALF, HALF)],
                sems.at[n],
            )
        )
    ccopy = pltpu.make_async_copy(counts.at[:, 0, pl.ds(base, OWN)], cbuf, csem)
    for copy in copies + [ccopy]:
        copy.start()
    yield
    ccopy.wait()
    out[G] = (cbuf[0] + cbuf[1]).astype(jnp.float32).astype(jnp.bfloat16)
    for n, copy in enumerate(copies):
        copy.wait()
        span = slice(n * HALF, (n + 1) * HALF)
        total = buf[0, :, span].astype(jnp.float32) + buf[1, :, span].astype(jnp.float32)
        out[0:G, span] = total.astype(jnp.bfloat16)


def send_kernel(kern, counts, out, *scratch):
    base = (1 - lax.axis_index("event")) * OWN
    for _ in partial_sums(kern, counts, base, out, *scratch):
        pass


def keep_kernel(kern, counts, off, tab, out, adj, *scratch):
    steps = partial_sums(kern, counts, lax.axis_index("event") * OWN, out, *scratch)
    next(steps)
    odd = lax.rem(lax.axis_index("dom"), 2)
    b = lax.broadcasted_iota(jnp.int32, (PB, OWN), 1)
    x = off[0, 0] + b
    part = x >> 5
    group = jnp.where(part == 1, 2, jnp.where(part == 0, odd, 1 - odd))
    lane = (x & (OWN - 1)) + group * OWN
    value = (tab[0, 0] + 1).astype(jnp.float32)
    spot = lax.broadcasted_iota(jnp.int32, (3 * OWN, OWN), 0)
    turned = jnp.zeros((3 * OWN, OWN), jnp.float32)
    for k in range(PB):
        turned = turned + jnp.where(spot == lane[k : k + 1], value[k : k + 1], 0.0)
    wide = jnp.concatenate([turned, jnp.zeros((OWN, OWN), jnp.float32)], axis=0)
    wide = jnp.concatenate([wide, jnp.zeros((W, W - OWN), jnp.float32)], axis=1)
    adj[...] = jnp.transpose(wide, (1, 0))[0:OWN]
    for _ in steps:
        pass


def source_kernel(own, got, vol, adj, first, second):
    odd = lax.rem(lax.axis_index("dom"), 2)
    for dst, half in ((first, odd), (second, 1 - odd)):
        span = pl.ds(pl.multiple_of(half * HALF, HALF), HALF)
        v = vol[0, span].astype(jnp.float32)
        hits = own[G, span].astype(jnp.float32) + got[G, span].astype(jnp.float32)
        factor = v / jnp.sqrt(1.0 + hits)
        total = own[0:G, span].astype(jnp.float32) + got[0:G, span].astype(jnp.float32)
        rows = [total * factor[None], v[None], adj[span][None]]
        rows.append(jnp.zeros((ROWS - ADJ - 1, HALF, W), jnp.float32))
        block = jnp.concatenate(rows, axis=0)
        dst[...] = jnp.transpose(block, (1, 0, 2)).astype(jnp.bfloat16)


def make_lists(p, q, p_lane, q_lane, lanes, codes, sem):
    adj = []
    for ref, lane in ((p, p_lane), (q, q_lane)):
        a = ref[:, ADJ].astype(jnp.float32)
        adj.append(pltpu.roll(a, (W - lane) % W, 1) if lane else a)
    adj = jnp.concatenate(adj, axis=0)
    there = adj > 0.5
    ones = jnp.where(there, 1.0, 0.0)
    row = lax.broadcasted_iota(jnp.int32, (OWN, OWN), 0)
    col = lax.broadcasted_iota(jnp.int32, (OWN, OWN), 1)
    below = jnp.where(col < row, 1.0, 0.0)
    rank = jnp.dot(
        below.astype(jnp.bfloat16), ones.astype(jnp.bfloat16), preferred_element_type=jnp.float32
    )
    rank = jnp.where(there, rank, -1.0)
    source = lax.broadcasted_iota(jnp.int32, (OWN, W), 0).astype(jnp.float32)
    code = source + 1.0 + 64.0 * (adj - 1.0)
    for r in range(OWN):
        picked = jnp.sum(jnp.where(rank == float(r), code, 0.0), axis=0, keepdims=True)
        lanes[r : r + 1] = picked.astype(jnp.int32)
    lanes[OWN : OWN + 1] = jnp.sum(ones, axis=0, keepdims=True).astype(jnp.int32)
    copy = pltpu.make_async_copy(lanes, codes, sem)
    copy.start()
    return copy


def term_group(codes, g, x, mats, tables):
    left, right = [], []
    for j in range(K):
        code = codes[g * K + j, x]
        left.append(mats[code & 63])
        right.append(tables[code >> 6])
    return jnp.dot(
        jnp.concatenate(left, axis=1),
        jnp.concatenate(right, axis=0),
        preferred_element_type=jnp.float32,
    )


def add_terms(codes, mats, tables, acc, fresh):
    def targets(t, carry):
        xs = [t * T + u for u in range(T)]
        most = codes[OWN, xs[0]]
        for x in xs[1:]:
            most = jnp.maximum(most, codes[OWN, x])
        if fresh:
            for x in xs:
                acc[x] = term_group(codes, 0, x, mats, tables)

        def group(g, carry):
            for x in xs:
                acc[x] = acc[x] + term_group(codes, g, x, mats, tables)
            return carry

        lax.fori_loop(1 if fresh else 0, (most + (K - 1)) >> 2, group, 0)
        return carry

    lax.fori_loop(0, OWN // T, targets, 0)


def gather_terms(p, q, p_lane, q_lane, tables, acc, mats, lanes, codes, sem, fresh=False):
    copy = make_lists(p, q, p_lane, q_lane, lanes, codes, sem)
    mats[0] = jnp.zeros((ROWS, W), jnp.bfloat16)
    mats[1 : 1 + HALF] = p[...]
    mats[1 + HALF : 1 + OWN] = q[...]
    copy.wait()
    add_terms(codes, mats, tables, acc, fresh)


def own_kernel(first, second, tables, acc, *scratch):
    gather_terms(first, second, OWN_LANE, OWN_LANE, tables, acc, *scratch, fresh=True)


def chunk_kernel(from_b, from_a, tables, acc_in, acc, *scratch):
    if COPY_ALIASED:
        acc[...] = acc_in[...]
    gather_terms(from_b, from_a, 0, OWN, tables, acc, *scratch)


def last_kernel(from_b, from_a, tables, acc_in, out, acc, stage, osem, *scratch):
    if COPY_ALIASED:
        acc[...] = acc_in[...]
    gather_terms(from_b, from_a, 0, OWN, tables, acc, *scratch)
    for c in range(OWN // 8):
        span = slice(c * 8, c * 8 + 8)
        scale = 1.0 / acc[span, G : G + 1]
        result = jnp.transpose(acc[span] * scale, (1, 0, 2))
        stage[:, span] = result[0:G].astype(jnp.bfloat16)
    copy = pltpu.make_async_copy(stage, out.at[0], osem)
    copy.start()
    copy.wait()


def per_device(kernels, counts, volume, tables, pair_offset, pair_table):
    bf16, f32, i32 = jnp.bfloat16, jnp.float32, jnp.int32
    dma = pltpu.SemaphoreType.DMA
    kernels = in_hbm(jnp.transpose(kernels, (0, 1, 3, 2, 4)))
    counts = in_hbm(counts)
    pair_offset = jnp.transpose(pair_offset, (0, 1, 3, 2))
    pair_table = jnp.transpose(pair_table, (0, 1, 3, 2))
    sums = on_chip((G + 1, OWN, W), bf16)
    scratch = [
        pltpu.VMEM((2, G, OWN, W), bf16),
        pltpu.VMEM((2, OWN, W), i32),
        dma((2,)),
        dma,
    ]

    to_other = pl.pallas_call(
        send_kernel,
        out_shape=sums,
        in_specs=[HBM, HBM],
        out_specs=VMEM,
        scratch_shapes=scratch,
        compiler_params=params(6),
        cost_estimate=cost(1 << 20, 4 << 20),
        name="send",
    )(kernels, counts)
    got = lax.ppermute(to_other, "event", [(0, 1), (1, 0)])
    own, adj = pl.pallas_call(
        keep_kernel,
        out_shape=[sums, on_chip((OWN, W), f32)],
        in_specs=[HBM, HBM, VMEM, VMEM],
        out_specs=[VMEM, VMEM],
        scratch_shapes=scratch,
        compiler_params=params(6),
        cost_estimate=cost(1 << 20, 4 << 20),
        name="keep",
    )(kernels, counts, pair_offset, pair_table)
    first, second = pl.pallas_call(
        source_kernel,
        out_shape=[on_chip((HALF, ROWS, W), bf16)] * 2,
        in_specs=[VMEM] * 4,
        out_specs=[VMEM] * 2,
        compiler_params=params(6),
        cost_estimate=cost(1 << 20, 4 << 20),
        name="source",
    )(own, in_vmem(got), volume, adj)

    count = lax.axis_size("dom")

    def swapped(value, start):
        pairs = [(a, a + 1) for a in range(start, count - 1, 2)]
        pairs = pairs + [(b, a) for a, b in pairs]
        return lax.ppermute(value, "dom", pairs)

    b0 = swapped(first, 1)
    a0 = swapped(second, 0)
    b1 = swapped(second, 1)
    a1 = swapped(first, 0)

    acc_shape = on_chip((OWN, ROWS, W), f32)
    term = 2 * ROWS * W * W
    lists = [
        pltpu.VMEM((OWN + 1, ROWS, W), bf16),
        pltpu.VMEM((LIST, W), i32),
        pltpu.SMEM((LIST, W), i32),
        dma,
    ]
    acc = pl.pallas_call(
        own_kernel,
        out_shape=acc_shape,
        in_specs=[VMEM] * 3,
        out_specs=VMEM,
        scratch_shapes=lists,
        compiler_params=params(6),
        cost_estimate=cost(256 * term, 16 << 20),
        name="own_terms",
    )(first, second, tables)
    acc = pl.pallas_call(
        chunk_kernel,
        out_shape=acc_shape,
        in_specs=[VMEM] * 4,
        out_specs=VMEM,
        scratch_shapes=lists,
        input_output_aliases={3: 0},
        compiler_params=params(6),
        cost_estimate=cost(192 * term, 12 << 20),
        name="chunk_terms",
    )(in_vmem(b0), in_vmem(a0), tables, acc)
    out, _ = pl.pallas_call(
        last_kernel,
        out_shape=[jax.ShapeDtypeStruct((1, G, OWN, W), bf16), acc_shape],
        in_specs=[VMEM] * 4,
        out_specs=[HBM, VMEM],
        scratch_shapes=[pltpu.VMEM((G, OWN, W), bf16), dma] + lists,
        input_output_aliases={3: 1},
        compiler_params=params(6),
        cost_estimate=cost(64 * term, 4 << 20),
        name="last_terms",
    )(in_vmem(b1), in_vmem(a1), tables, acc)
    return jnp.transpose(out, (0, 2, 1, 3))


def solution(mesh):
    in_specs = (
        P("event", "dom", None, None, None),
        P("event", "dom", None, None),
        P("dom", "event", None),
        P(),
        P("dom", "event", None, None),
        P("dom", "event", None, None),
    )
    return jax.shard_map(
        per_device,
        mesh=mesh,
        in_specs=in_specs,
        out_specs=P("dom", "event", None, None),
        check_vma=False,
    )
```

time: 335 us -> 48.7 us (0.15)
  the two profiles are of different devices: /device:TPU:320 before, /device:TPU:256 now
where the time goes in v2:
time: 48.7 us; the launch traced here: 48.4 us
  Pallas kernels  24.6 us (51%)
  starting transfers between devices  18.5 us (38%)
  waiting for transfers between devices  5.11 us (10%)
    ppermute x4, starting transfers between devices, swapped(): return lax.ppermute(value, 'dom', pairs)  16.6 us
    pallas_call x1, Pallas kernels, per_device(): pl.pallas_call(own_kernel, out_shape=acc_shape, in_specs=[VMEM] * 3, out_...  7.99 us
    pallas_call x1, Pallas kernels, per_device(): pl.pallas_call(chunk_kernel, out_shape=acc_shape, in_specs=[VMEM] * 4, ou...  6.68 us
    pallas_call x1, Pallas kernels, per_device(): pl.pallas_call(last_kernel, out_shape=[jax.ShapeDtypeStruct((1, G, OWN, W...  5.81 us
    ppermute x4, waiting for transfers between devices, swapped(): return lax.ppermute(value, 'dom', pairs)  4.33 us
    ppermute x1, starting transfers between devices, per_device(): got = lax.ppermute(to_other, 'event', [(0, 1), (1, 0)])  1.92 us
    pallas_call x1, Pallas kernels, per_device(): pl.pallas_call(keep_kernel, out_shape=[sums, on_chip((OWN, W), f32)], in_...  1.79 us
    pallas_call x1, Pallas kernels, per_device(): pl.pallas_call(send_kernel, out_shape=sums, in_specs=[HBM, HBM], out_spec...  1.71 us
  transfers between devices with their start and end apart: 5, of which 3 were waited for; matrix products, arithmetic and copies ran while one was open for 0% of the time, Pallas kernels for 34%

profile of v2, /device:TPU:256, one launch (start us, length us, event | category | flops | bytes accessed | tf_op | source)
XLA Modules:
  0.0 48.4 jit_solution(15191954805356345506)
XLA Ops:
  0.0 0.0 copy-start.1
  0.0 0.0 copy-start.2
  0.0 1.7 %send.1 = bf16[126,32,128]{2,1,0:T(8,128)(2,1)S(1)} custom-call(bf16[2,1,125,64,128]{4,3,2,1,0:T(8,128)(2,1)} %bitcast.6, s32[2,1,64,128]{3,2,1,0:T(8,128)} %counts.3), custom_call_target="tpu_custom_call" | custom-call | flops 1048576 | bytes 4194304 | tf_op jit(solution)/shard_map/send/pallas_call | solution.py:221
  1.7 0.0 copy-start.3
  1.7 1.9 %collective-permute-start = (bf16[126,32,128]{2,1,0:T(8,128)(2,1)S(1)}, bf16[126,32,128]{2,1,0:T(8,128)(2,1)S(1)}, u32[]{:S(2)}, u32[]{:S(2)}) collective-permute-start(bf16[126,32,128]{2,1,0:T(8,128)(2,1)S(1)} %send.1), channel_id=1, source_target_pairs={{0,256},{256,0},{1,257},{257,1},{2,258},{258,2},{3,259},{259,3},{4... | collective-permute-start | bytes 3096584 | tf_op jit(solution)/shard_map/ppermute | solution.py:231
  3.7 0.0 copy-done.1
  3.7 0.0 copy-done.2
  3.7 0.0 copy-start
  3.7 1.8 %keep.1 = (bf16[126,32,128]{2,1,0:T(8,128)(2,1)S(1)}, f32[32,128]{1,0:T(8,128)S(1)}) custom-call(bf16[2,1,125,64,128]{4,3,2,1,0:T(8,128)(2,1)} %bitcast.7, s32[2,1,64,128]{3,2,1,0:T(8,128)} %counts.3, s32[1,1,16,32]{3,2,1,0:T(8,128)S(1)} %bitcast.4, s32[1,1,16,32]{3,2,1,0:T(8,128)S(1)} %bitcast.5), custom_call_target="tpu_custom_call" | custom-call | flops 1048576 | bytes 4194304 | tf_op jit(solution)/shard_map/keep/pallas_call | solution.py:232
  5.5 0.8 %collective-permute-done.got = bf16[126,32,128]{2,1,0:T(8,128)(2,1)S(1)} collective-permute-done((bf16[126,32,128]{2,1,0:T(8,128)(2,1)S(1)}, bf16[126,32,128]{2,1,0:T(8,128)(2,1)S(1)}, u32[]{:S(2)}, u32[]{:S(2)}) %collective-permute-start) | collective-permute-done | bytes 1032224 | tf_op jit(solution)/shard_map/ppermute | solution.py:231
  6.3 0.0 copy-done.3
  6.3 0.7 %source.1 = (bf16[16,128,128]{2,1,0:T(8,128)(2,1)S(1)}, bf16[16,128,128]{2,1,0:T(8,128)(2,1)S(1)}) custom-call(bf16[126,32,128]{2,1,0:T(8,128)(2,1)S(1)} %get-tuple-element.10.own, bf16[126,32,128]{2,1,0:T(8,128)(2,1)S(1)} %collective-permute-done.got, bf16[1,32,128]{2,1,0:T(8,128)(2,1)S(1)} %copy-done.3, f32[32,128]{1,0:T(8,128)S(1)} %get-tuple-element.11.adj), custom_call_target="tpu_custom_call" | custom-call | flops 1048576 | bytes 4194304 | tf_op jit(solution)/shard_map/source/pallas_call | solution.py:242
  7.0 3.4 %collective-permute-start.4 = (bf16[16,128,128]{2,1,0:T(8,128)(2,1)S(1)}, bf16[16,128,128]{2,1,0:T(8,128)(2,1)S(1)}, u32[]{:S(2)}, u32[]{:S(2)}) collective-permute-start(bf16[16,128,128]{2,1,0:T(8,128)(2,1)S(1)} %get-tuple-element.12.second), channel_id=1, source_target_pairs={{0,1},{2,3},{4,5},{6,7},{8,9},{10,11},{12,13},{14,15},{16,17},{18,... | collective-permute-start | bytes 1572872 | tf_op jit(solution)/shard_map/ppermute | solution.py:257
  10.4 6.0 %collective-permute-start.3 = (bf16[16,128,128]{2,1,0:T(8,128)(2,1)S(1)}, bf16[16,128,128]{2,1,0:T(8,128)(2,1)S(1)}, u32[]{:S(2)}, u32[]{:S(2)}) collective-permute-start(bf16[16,128,128]{2,1,0:T(8,128)(2,1)S(1)} %get-tuple-element.13.first), channel_id=1, source_target_pairs={{1,2},{3,4},{5,6},{7,8},{9,10},{11,12},{13,14},{15,16},{17,18},{19... | collective-permute-start | bytes 1572872 | tf_op jit(solution)/shard_map/ppermute | solution.py:257
  16.4 5.3 %collective-permute-start.1 = (bf16[16,128,128]{2,1,0:T(8,128)(2,1)S(1)}, bf16[16,128,128]{2,1,0:T(8,128)(2,1)S(1)}, u32[]{:S(2)}, u32[]{:S(2)}) collective-permute-start(bf16[16,128,128]{2,1,0:T(8,128)(2,1)S(1)} %get-tuple-element.12.second), channel_id=1, source_target_pairs={{1,2},{3,4},{5,6},{7,8},{9,10},{11,12},{13,14},{15,16},{17,18},{19... | collective-permute-start | bytes 1572872 | tf_op jit(solution)/shard_map/ppermute | solution.py:257
  21.6 1.9 %collective-permute-start.2 = (bf16[16,128,128]{2,1,0:T(8,128)(2,1)S(1)}, bf16[16,128,128]{2,1,0:T(8,128)(2,1)S(1)}, u32[]{:S(2)}, u32[]{:S(2)}) collective-permute-start(bf16[16,128,128]{2,1,0:T(8,128)(2,1)S(1)} %get-tuple-element.13.first), channel_id=1, source_target_pairs={{0,1},{2,3},{4,5},{6,7},{8,9},{10,11},{12,13},{14,15},{16,17},{18,... | collective-permute-start | bytes 1572872 | tf_op jit(solution)/shard_map/ppermute | solution.py:257
  23.6 0.0 copy-done
  23.6 8.0 %own_terms.1.acc_in = f32[32,128,128]{2,1,0:T(8,128)S(1)} custom-call(bf16[16,128,128]{2,1,0:T(8,128)(2,1)S(1)} %get-tuple-element.13.first, bf16[16,128,128]{2,1,0:T(8,128)(2,1)S(1)} %get-tuple-element.12.second, bf16[32,128,128]{2,1,0:T(8,128)(2,1)S(1)} %copy-done), custom_call_target="tpu_custom_call" | custom-call | flops 1073741824 | bytes 16777216 | tf_op jit(solution)/shard_map/own_terms/pallas_call | solution.py:272
  31.6 0.0 collective-permute-done.4.from_a
  31.6 0.9 %collective-permute-done.3.from_b = bf16[16,128,128]{2,1,0:T(8,128)(2,1)S(1)} collective-permute-done((bf16[16,128,128]{2,1,0:T(8,128)(2,1)S(1)}, bf16[16,128,128]{2,1,0:T(8,128)(2,1)S(1)}, u32[]{:S(2)}, u32[]{:S(2)}) %collective-permute-start.3) | collective-permute-done | bytes 524320 | tf_op jit(solution)/shard_map/ppermute | solution.py:257
  32.5 6.7 %chunk_terms.1.acc_in = f32[32,128,128]{2,1,0:T(8,128)S(1)} custom-call(bf16[16,128,128]{2,1,0:T(8,128)(2,1)S(1)} %collective-permute-done.3.from_b, bf16[16,128,128]{2,1,0:T(8,128)(2,1)S(1)} %collective-permute-done.4.from_a, bf16[32,128,128]{2,1,0:T(8,128)(2,1)S(1)} %copy-done, f32[32,128,128]{2,1,0:T(8,128)S(1)} %own_terms.1.acc_in), custom_call_target="tpu_custom_call", output_to_operand_aliasing={{}: (3, {})} | custom-call | flops 805306368 | bytes 12582912 | tf_op jit(solution)/shard_map/chunk_terms/pallas_call | solution.py:282
  39.2 3.4 %collective-permute-done.1.from_b = bf16[16,128,128]{2,1,0:T(8,128)(2,1)S(1)} collective-permute-done((bf16[16,128,128]{2,1,0:T(8,128)(2,1)S(1)}, bf16[16,128,128]{2,1,0:T(8,128)(2,1)S(1)}, u32[]{:S(2)}, u32[]{:S(2)}) %collective-permute-start.1) | collective-permute-done | bytes 524320 | tf_op jit(solution)/shard_map/ppermute | solution.py:257
  42.6 0.0 collective-permute-done.2.from_a
  42.6 5.8 %last_terms.1 = (bf16[1,125,32,128]{3,2,1,0:T(8,128)(2,1)}, f32[32,128,128]{2,1,0:T(8,128)S(1)}) custom-call(bf16[16,128,128]{2,1,0:T(8,128)(2,1)S(1)} %collective-permute-done.1.from_b, bf16[16,128,128]{2,1,0:T(8,128)(2,1)S(1)} %collective-permute-done.2.from_a, bf16[32,128,128]{2,1,0:T(8,128)(2,1)S(1)} %copy-done, ...), custom_call_target="tpu_custom_call", output_to_operand_aliasing={{1}: (3, {})} | custom-call | flops 268435456 | bytes 4194304 | tf_op jit(solution)/shard_map/last_terms/pallas_call | solution.py:293
Async XLA Ops:
  0.0 3.7 %copy-start.1 = (s32[1,1,32,16]{2,3,1,0:T(8,128)S(1)}, s32[1,1,32,16]{2,3,1,0:T(8,128)}, u32[]{:S(2)}) copy-start(s32[1,1,32,16]{2,3,1,0:T(8,128)} %param.10) | copy-start | bytes 6148
  0.0 3.7 %copy-start.2 = (s32[1,1,32,16]{2,3,1,0:T(8,128)S(1)}, s32[1,1,32,16]{2,3,1,0:T(8,128)}, u32[]{:S(2)}) copy-start(s32[1,1,32,16]{2,3,1,0:T(8,128)} %param.11) | copy-start | bytes 6148
  1.7 4.5 %copy-start.3 = (bf16[1,32,128]{2,1,0:T(8,128)(2,1)S(1)}, bf16[1,32,128]{2,1,0:T(8,128)(2,1)}, u32[]{:S(2)}) copy-start(bf16[1,32,128]{2,1,0:T(8,128)(2,1)} %vol.1) | copy-start | bytes 24580
  1.7 4.5 %collective-permute-start = (bf16[126,32,128]{2,1,0:T(8,128)(2,1)S(1)}, bf16[126,32,128]{2,1,0:T(8,128)(2,1)S(1)}, u32[]{:S(2)}, u32[]{:S(2)}) collective-permute-start(bf16[126,32,128]{2,1,0:T(8,128)(2,1)S(1)} %send.1), channel_id=1, source_target_pairs={{0,256},{256,0},{1,257},{257,1},{2,258},{258,2},{3,259},{259,3},{4... | collective-permute-start | bytes 3096584 | tf_op jit(solution)/shard_map/ppermute | solution.py:231
  3.7 19.9 %copy-start = (bf16[32,128,128]{2,1,0:T(8,128)(2,1)S(1)}, bf16[32,128,128]{2,1,0:T(8,128)(2,1)}, u32[]{:S(2)}) copy-start(bf16[32,128,128]{2,1,0:T(8,128)(2,1)} %tables.5) | copy-start | bytes 3145732
  7.0 24.6 %collective-permute-start.4 = (bf16[16,128,128]{2,1,0:T(8,128)(2,1)S(1)}, bf16[16,128,128]{2,1,0:T(8,128)(2,1)S(1)}, u32[]{:S(2)}, u32[]{:S(2)}) collective-permute-start(bf16[16,128,128]{2,1,0:T(8,128)(2,1)S(1)} %get-tuple-element.12.second), channel_id=1, source_target_pairs={{0,1},{2,3},{4,5},{6,7},{8,9},{10,11},{12,13},{14,15},{16,17},{18,... | collective-permute-start | bytes 1572872 | tf_op jit(solution)/shard_map/ppermute | solution.py:257
  10.4 22.1 %collective-permute-start.3 = (bf16[16,128,128]{2,1,0:T(8,128)(2,1)S(1)}, bf16[16,128,128]{2,1,0:T(8,128)(2,1)S(1)}, u32[]{:S(2)}, u32[]{:S(2)}) collective-permute-start(bf16[16,128,128]{2,1,0:T(8,128)(2,1)S(1)} %get-tuple-element.13.first), channel_id=1, source_target_pairs={{1,2},{3,4},{5,6},{7,8},{9,10},{11,12},{13,14},{15,16},{17,18},{19... | collective-permute-start | bytes 1572872 | tf_op jit(solution)/shard_map/ppermute | solution.py:257
  16.4 26.2 %collective-permute-start.1 = (bf16[16,128,128]{2,1,0:T(8,128)(2,1)S(1)}, bf16[16,128,128]{2,1,0:T(8,128)(2,1)S(1)}, u32[]{:S(2)}, u32[]{:S(2)}) collective-permute-start(bf16[16,128,128]{2,1,0:T(8,128)(2,1)S(1)} %get-tuple-element.12.second), channel_id=1, source_target_pairs={{1,2},{3,4},{5,6},{7,8},{9,10},{11,12},{13,14},{15,16},{17,18},{19... | collective-permute-start | bytes 1572872 | tf_op jit(solution)/shard_map/ppermute | solution.py:257
  21.6 21.0 %collective-permute-start.2 = (bf16[16,128,128]{2,1,0:T(8,128)(2,1)S(1)}, bf16[16,128,128]{2,1,0:T(8,128)(2,1)S(1)}, u32[]{:S(2)}, u32[]{:S(2)}) collective-permute-start(bf16[16,128,128]{2,1,0:T(8,128)(2,1)S(1)} %get-tuple-element.13.first), channel_id=1, source_target_pairs={{0,1},{2,3},{4,5},{6,7},{8,9},{10,11},{12,13},{14,15},{16,17},{18,... | collective-permute-start | bytes 1572872 | tf_op jit(solution)/shard_map/ppermute | solution.py:257

commit v3 on v2

v3 whole, which is shorter than its diff:
```python
import jax
import jax.numpy as jnp
from jax import lax
from jax.experimental import pallas as pl
from jax.experimental.pallas import tpu as pltpu
from jax.sharding import PartitionSpec as P


OWN = 32
HALF = OWN // 2
G = 125
ADJ = G + 1
ROWS = 128
W = 128
PB = 16
U = 8
PAIR_ROWS = 3
OWN_LANE = 2 * OWN
MIB = 1 << 20
COPY_ALIASED = False


HBM = pl.BlockSpec(memory_space=pltpu.HBM)
VMEM = pl.BlockSpec(memory_space=pltpu.VMEM)
SMEM = pl.BlockSpec(memory_space=pltpu.SMEM)


def on_chip(shape, dtype):
    return pltpu.VMEM(shape, dtype)


def in_vmem(x):
    return pltpu.with_memory_space_constraint(x, pltpu.VMEM)


def in_hbm(x):
    return pltpu.with_memory_space_constraint(x, pltpu.HBM)


def params(mib):
    return pltpu.CompilerParams(vmem_limit_bytes=mib * MIB)


def cost(flops, nbytes):
    return pl.CostEstimate(flops=flops, bytes_accessed=nbytes, transcendentals=0)


PIECES = ((0, 32), (32, 32), (64, 32), (96, 29))


def partial_sums(kern, counts, base, out, buf, cbuf, sems, csem):
    copies = []
    for n, (first, size) in enumerate(PIECES):
        span = pl.ds(first, size)
        copies.append(
            pltpu.make_async_copy(
                kern.at[:, 0, span, pl.ds(base, OWN)], buf.at[:, span], sems.at[n]
            )
        )
    ccopy = pltpu.make_async_copy(counts.at[:, 0, pl.ds(base, OWN)], cbuf, csem)
    for copy in copies + [ccopy]:
        copy.start()
    yield
    for copy, (first, size) in zip(copies, PIECES):
        copy.wait()
        span = slice(first, first + size)
        total = buf[0, span].astype(jnp.float32) + buf[1, span].astype(jnp.float32)
        out[span] = total.astype(jnp.bfloat16)
    ccopy.wait()
    out[G] = (cbuf[0] + cbuf[1]).astype(jnp.float32).astype(jnp.bfloat16)


def send_kernel(kern, counts, out, *scratch):
    base = (1 - lax.axis_index("event")) * OWN
    for _ in partial_sums(kern, counts, base, out, *scratch):
        pass


def keep_kernel(kern, counts, off, tab, out, adj, *scratch):
    steps = partial_sums(kern, counts, lax.axis_index("event") * OWN, out, *scratch)
    next(steps)
    odd = lax.rem(lax.axis_index("dom"), 2)
    b = lax.broadcasted_iota(jnp.int32, (PB, OWN), 1)
    x = off[0, 0] + b
    part = x >> 5
    group = jnp.where(part == 1, 2, jnp.where(part == 0, odd, 1 - odd))
    lane = (x & (OWN - 1)) + group * OWN
    value = (tab[0, 0] + 1).astype(jnp.float32)
    spot = lax.broadcasted_iota(jnp.int32, (3 * OWN, OWN), 0)
    turned = jnp.zeros((3 * OWN, OWN), jnp.float32)
    for k in range(PB):
        turned = turned + jnp.where(spot == lane[k : k + 1], value[k : k + 1], 0.0)
    wide = jnp.concatenate([turned, jnp.zeros((OWN, OWN), jnp.float32)], axis=0)
    wide = jnp.concatenate([wide, jnp.zeros((W, W - OWN), jnp.float32)], axis=1)
    adj[...] = jnp.transpose(wide, (1, 0))[0:OWN]
    for _ in steps:
        pass


def source_kernel(own, got, vol, adj, first, second):
    odd = lax.rem(lax.axis_index("dom"), 2)
    for dst, half in ((first, odd), (second, 1 - odd)):
        span = pl.ds(pl.multiple_of(half * HALF, HALF), HALF)
        v = vol[0, span].astype(jnp.float32)
        hits = own[G, span].astype(jnp.float32) + got[G, span].astype(jnp.float32)
        factor = v / jnp.sqrt(1.0 + hits)
        total = own[0:G, span].astype(jnp.float32) + got[0:G, span].astype(jnp.float32)
        rest = pl.ds(pl.multiple_of((1 - half) * HALF, HALF), HALF)
        rows = [total * factor[None], v[None], adj[span][None], adj[rest][None]]
        block = jnp.concatenate(rows, axis=0)
        dst[...] = jnp.transpose(block, (1, 0, 2)).astype(jnp.bfloat16)


def neighbours(ref, row, lane):
    a = ref[:, row].astype(jnp.float32)
    return pltpu.roll(a, W - lane, 1) if lane else a


def make_lists(adj, lists):
    n = adj.shape[0]
    f32, bf16 = jnp.float32, jnp.bfloat16
    there = adj > 0.5
    ones = jnp.where(there, 1.0, 0.0)

    def triangle(m, strict):
        row = lax.broadcasted_iota(jnp.int32, (m, m), 0)
        col = lax.broadcasted_iota(jnp.int32, (m, m), 1)
        return jnp.where(col < row if strict else col <= row, 1.0, 0.0).astype(bf16)

    rank = jnp.dot(triangle(n, True), ones.astype(bf16), preferred_element_type=f32)
    rank = jnp.where(there, rank, -1.0)
    source = lax.broadcasted_iota(jnp.int32, (n, W), 0).astype(f32)
    code = source + 1.0 + 64.0 * (adj - 1.0)
    for r in range(n):
        picked = jnp.sum(jnp.where(rank == float(r), code, 0.0), axis=0, keepdims=True)
        lists[r : r + 1] = picked.astype(jnp.int32)
    terms = lax.dot_general(
        ones.astype(bf16), jnp.ones((n, W), bf16), (((0,), (0,)), ((), ())),
        preferred_element_type=f32,
    )[0:OWN]
    pairs = ((terms.astype(jnp.int32) + 1) >> 1).astype(f32)
    end = jnp.dot(triangle(OWN, False), pairs.astype(bf16), preferred_element_type=f32)
    lane = lax.broadcasted_iota(jnp.int32, (OWN, W), 1).astype(f32)
    for q in range(PAIR_ROWS):
        place = lane + float(q * W)
        past = end <= place
        target = jnp.sum(jnp.where(past, 1.0, 0.0), axis=0, keepdims=True)
        base = jnp.sum(jnp.where(past, pairs, 0.0), axis=0, keepdims=True)
        first = jnp.minimum(2.0 * (place[0:1] - base), float(n - 2))
        lists[n + q : n + q + 1] = (target + 256.0 * first).astype(jnp.int32)
    lists[n + PAIR_ROWS : n + PAIR_ROWS + 1] = end[OWN - 1 : OWN].astype(jnp.int32)


def list_rows(n):
    return n + 8


def add_terms(blocks, lists, tables, acc, mats, codes, sem):
    n = HALF * len(blocks)
    copy = pltpu.make_async_copy(lists, codes, sem)
    copy.start()
    mats[0] = jnp.zeros((ROWS, W), jnp.bfloat16)
    for i, ref in enumerate(blocks):
        mats[1 + i * HALF : 1 + (i + 1) * HALF] = ref[...]
    copy.wait()

    def step(i, carry):
        for u in range(U):
            at = i * U + u
            entry = codes[n + (at >> 7), at & (W - 1)]
            x, r = entry & 255, entry >> 8
            two = [codes[r + j, x] for j in range(2)]
            term = jnp.dot(
                jnp.concatenate([mats[c & 63] for c in two], axis=1),
                jnp.concatenate([tables[c >> 6] for c in two], axis=0),
                preferred_element_type=jnp.float32,
            )
            acc[x] = acc[x] + term
        return carry

    lax.fori_loop(0, (codes[n + PAIR_ROWS, 0] + (U - 1)) >> 3, step, 0)


def own_kernel(first, second, tables, acc, lists, *scratch):
    adj = [neighbours(first, ADJ, OWN_LANE), neighbours(second, ADJ, OWN_LANE)]
    make_lists(jnp.concatenate(adj, axis=0), lists)

    def clear(i, carry):
        acc[i] = jnp.zeros((ROWS, W), jnp.float32)
        return carry

    lax.fori_loop(0, OWN + 1, clear, 0)
    add_terms((first, second), lists, tables, acc, *scratch)


def chunk_kernel(from_b, from_a, tables, acc_in, acc, lists_a, lists_b, lists, *scratch):
    if COPY_ALIASED:
        acc[...] = acc_in[...]
    adj = [neighbours(from_b, ADJ, 0), neighbours(from_a, ADJ, OWN)]
    make_lists(jnp.concatenate(adj, axis=0), lists)
    make_lists(neighbours(from_a, ADJ + 1, OWN), lists_a)
    make_lists(neighbours(from_b, ADJ + 1, 0), lists_b)
    add_terms((from_b, from_a), lists, tables, acc, *scratch)


def finish(half, acc, out, stage, sems):
    copies = []
    for c in range(HALF // 8):
        first = pl.multiple_of(half * HALF + c * 8, 8)
        span = pl.ds(first, 8)
        scale = 1.0 / acc[span, G : G + 1]
        result = jnp.transpose(acc[span] * scale, (1, 0, 2))
        stage[c] = result[0:G].astype(jnp.bfloat16)
        copies.append(pltpu.make_async_copy(stage.at[c], out.at[0, :, span], sems.at[c]))
        copies[-1].start()
    for copy in copies:
        copy.wait()


def last_a_kernel(from_a, lists, tables, acc_in, out, acc, stage, sems, *scratch):
    if COPY_ALIASED:
        acc[...] = acc_in[...]
    add_terms((from_a,), lists, tables, acc, *scratch)
    finish(1 - lax.rem(lax.axis_index("dom"), 2), acc, out, stage, sems)


def last_b_kernel(from_b, lists, tables, acc_in, out_in, out, acc, stage, sems, *scratch):
    if COPY_ALIASED:
        acc[...] = acc_in[...]
        pltpu.sync_copy(out_in, out)
    add_terms((from_b,), lists, tables, acc, *scratch)
    finish(lax.rem(lax.axis_index("dom"), 2), acc, out, stage, sems)


def per_device(kernels, counts, volume, tables, pair_offset, pair_table):
    bf16, f32, i32 = jnp.bfloat16, jnp.float32, jnp.int32
    dma = pltpu.SemaphoreType.DMA
    kernels = in_hbm(jnp.transpose(kernels, (0, 1, 3, 2, 4)))
    counts = in_hbm(counts)
    pair_offset = jnp.transpose(pair_offset, (0, 1, 3, 2))
    pair_table = jnp.transpose(pair_table, (0, 1, 3, 2))
    sums = on_chip((G + 1, OWN, W), bf16)
    scratch = [
        pltpu.VMEM((2, G, OWN, W), bf16),
        pltpu.VMEM((2, OWN, W), i32),
        dma((len(PIECES),)),
        dma,
    ]

    to_other = pl.pallas_call(
        send_kernel,
        out_shape=sums,
        in_specs=[HBM, HBM],
        out_specs=VMEM,
        scratch_shapes=scratch,
        compiler_params=params(6),
        cost_estimate=cost(1 << 20, 4 << 20),
        name="send",
    )(kernels, counts)
    got = lax.ppermute(to_other, "event", [(0, 1), (1, 0)])
    own, adj = pl.pallas_call(
        keep_kernel,
        out_shape=[sums, on_chip((OWN, W), f32)],
        in_specs=[HBM, HBM, VMEM, VMEM],
        out_specs=[VMEM, VMEM],
        scratch_shapes=scratch,
        compiler_params=params(6),
        cost_estimate=cost(1 << 20, 4 << 20),
        name="keep",
    )(kernels, counts, pair_offset, pair_table)
    first, second = pl.pallas_call(
        source_kernel,
        out_shape=[on_chip((HALF, ROWS, W), bf16)] * 2,
        in_specs=[VMEM] * 4,
        out_specs=[VMEM] * 2,
        compiler_params=params(6),
        cost_estimate=cost(1 << 20, 4 << 20),
        name="source",
    )(own, in_vmem(got), volume, adj)

    count = lax.axis_size("dom")

    def swapped(value, start):
        pairs = [(a, a + 1) for a in range(start, count - 1, 2)]
        pairs = pairs + [(b, a) for a, b in pairs]
        return lax.ppermute(value, "dom", pairs)

    a0 = swapped(second, 0)
    b0 = swapped(first, 1)
    a1 = swapped(first, 0)
    b1 = swapped(second, 1)

    acc_shape = on_chip((OWN + 1, ROWS, W), f32)
    out_shape = jax.ShapeDtypeStruct((1, G, OWN, W), bf16)
    term = 2 * ROWS * W * W

    def lists(n):
        return (list_rows(n), W)

    def work(n):
        return [pltpu.VMEM((n + 1, ROWS, W), bf16), pltpu.SMEM(lists(n), i32), dma]

    stage = [pltpu.VMEM((HALF // 8, G, 8, W), bf16), dma((HALF // 8,))]
    acc = pl.pallas_call(
        own_kernel,
        out_shape=acc_shape,
        in_specs=[VMEM] * 3,
        out_specs=VMEM,
        scratch_shapes=[pltpu.VMEM(lists(OWN), i32)] + work(OWN),
        compiler_params=params(6),
        cost_estimate=cost(256 * term, 16 << 20),
        name="own_terms",
    )(first, second, tables)
    acc, lists_a, lists_b = pl.pallas_call(
        chunk_kernel,
        out_shape=[acc_shape] + [on_chip(lists(HALF), i32)] * 2,
        in_specs=[VMEM] * 4,
        out_specs=[VMEM] * 3,
        scratch_shapes=[pltpu.VMEM(lists(OWN), i32)] + work(OWN),
        input_output_aliases={3: 0},
        compiler_params=params(6),
        cost_estimate=cost(192 * term, 12 << 20),
        name="chunk_terms",
    )(in_vmem(b0), in_vmem(a0), tables, acc)
    out, acc = pl.pallas_call(
        last_a_kernel,
        out_shape=[out_shape, acc_shape],
        in_specs=[VMEM] * 4,
        out_specs=[HBM, VMEM],
        scratch_shapes=stage + work(HALF),
        input_output_aliases={3: 1},
        compiler_params=params(6),
        cost_estimate=cost(32 * term, 2 << 20),
        name="last_a",
    )(in_vmem(a1), lists_a, tables, acc)
    out, _ = pl.pallas_call(
        last_b_kernel,
        out_shape=[out_shape, acc_shape],
        in_specs=[VMEM] * 4 + [HBM],
        out_specs=[HBM, VMEM],
        scratch_shapes=stage + work(HALF),
        input_output_aliases={3: 1, 4: 0},
        compiler_params=params(6),
        cost_estimate=cost(32 * term, 2 << 20),
        name="last_b",
    )(in_vmem(b1), lists_b, tables, acc, out)
    return jnp.transpose(out, (0, 2, 1, 3))


def solution(mesh):
    in_specs = (
        P("event", "dom", None, None, None),
        P("event", "dom", None, None),
        P("dom", "event", None),
        P(),
        P("dom", "event", None, None),
        P("dom", "event", None, None),
    )
    return jax.shard_map(
        per_device,
        mesh=mesh,
        in_specs=in_specs,
        out_specs=P("dom", "event", None, None),
        check_vma=False,
    )
```

time: 48.7 us -> 45.5 us (0.934)
  Pallas kernels: 24.6 us -> 21.8 us
    pallas_call x2 -> x3, Pallas kernels: 12.5 us -> 10.7 us  [the longest x1 5.43 us: per_device(): pl.pallas_call(chunk_kernel, out_shape=[acc_shape] + [on_chip(lists(HALF)...]
    pallas_call x1, Pallas kernels: 7.99 us -> 7.02 us  [per_device(): pl.pallas_call(own_kernel, out_shape=acc_shape, in_specs=[VMEM] * 3, out_...]
  transfers between devices with their start and end apart: 5 -> 5, of which waited for: 3 -> 3; matrix products, arithmetic and copies ran while one was open for 0% -> 0% of each run, Pallas kernels for 34% -> 37%
where the time goes in v3:
time: 45.5 us; the launch traced here: 45.2 us
  Pallas kernels  21.8 us (48%)
  starting transfers between devices  18.5 us (41%)
  waiting for transfers between devices  4.74 us (10%)
    ppermute x4, starting transfers between devices, swapped(): return lax.ppermute(value, 'dom', pairs)  16.6 us
    pallas_call x1, Pallas kernels, per_device(): pl.pallas_call(own_kernel, out_shape=acc_shape, in_specs=[VMEM] * 3, out_...  7.02 us
    pallas_call x1, Pallas kernels, per_device(): pl.pallas_call(chunk_kernel, out_shape=[acc_shape] + [on_chip(lists(HALF)...  5.43 us
    ppermute x4, waiting for transfers between devices, swapped(): return lax.ppermute(value, 'dom', pairs)  3.9 us
    pallas_call x1, Pallas kernels, per_device(): pl.pallas_call(last_a_kernel, out_shape=[out_shape, acc_shape], in_specs=...  2.63 us
    pallas_call x1, Pallas kernels, per_device(): pl.pallas_call(last_b_kernel, out_shape=[out_shape, acc_shape], in_specs=...  2.63 us
    ppermute x1, starting transfers between devices, per_device(): got = lax.ppermute(to_other, 'event', [(0, 1), (1, 0)])  1.92 us
    pallas_call x1, Pallas kernels, per_device(): pl.pallas_call(keep_kernel, out_shape=[sums, on_chip((OWN, W), f32)], in_...  1.72 us
  transfers between devices with their start and end apart: 5, of which 3 were waited for; matrix products, arithmetic and copies ran while one was open for 0% of the time, Pallas kernels for 37%

profile of v3, /device:TPU:256, one launch (start us, length us, event | category | flops | bytes accessed | tf_op | source)
XLA Modules:
  0.0 45.2 jit_solution(12292474099069096149)
XLA Ops:
  0.0 0.0 copy-start.1
  0.0 0.0 copy-start.2
  0.0 1.6 %send.1 = bf16[126,32,128]{2,1,0:T(8,128)(2,1)S(1)} custom-call(bf16[2,1,125,64,128]{4,3,2,1,0:T(8,128)(2,1)} %bitcast.6, s32[2,1,64,128]{3,2,1,0:T(8,128)} %counts.3), custom_call_target="tpu_custom_call" | custom-call | flops 1048576 | bytes 4194304 | tf_op jit(solution)/shard_map/send/pallas_call | solution.py:250
  1.7 0.0 copy-start.3
  1.7 1.9 %collective-permute-start = (bf16[126,32,128]{2,1,0:T(8,128)(2,1)S(1)}, bf16[126,32,128]{2,1,0:T(8,128)(2,1)S(1)}, u32[]{:S(2)}, u32[]{:S(2)}) collective-permute-start(bf16[126,32,128]{2,1,0:T(8,128)(2,1)S(1)} %send.1), channel_id=1, source_target_pairs={{0,256},{256,0},{1,257},{257,1},{2,258},{258,2},{3,259},{259,3},{4... | collective-permute-start | bytes 3096584 | tf_op jit(solution)/shard_map/ppermute | solution.py:260
  3.6 0.0 copy-done.1
  3.6 0.0 copy-done.2
  3.6 0.0 copy-start
  3.6 1.7 %keep.1 = (bf16[126,32,128]{2,1,0:T(8,128)(2,1)S(1)}, f32[32,128]{1,0:T(8,128)S(1)}) custom-call(bf16[2,1,125,64,128]{4,3,2,1,0:T(8,128)(2,1)} %bitcast.7, s32[2,1,64,128]{3,2,1,0:T(8,128)} %counts.3, s32[1,1,16,32]{3,2,1,0:T(8,128)S(1)} %bitcast.4, s32[1,1,16,32]{3,2,1,0:T(8,128)S(1)} %bitcast.5), custom_call_target="tpu_custom_call" | custom-call | flops 1048576 | bytes 4194304 | tf_op jit(solution)/shard_map/keep/pallas_call | solution.py:261
  5.4 0.8 %collective-permute-done.got = bf16[126,32,128]{2,1,0:T(8,128)(2,1)S(1)} collective-permute-done((bf16[126,32,128]{2,1,0:T(8,128)(2,1)S(1)}, bf16[126,32,128]{2,1,0:T(8,128)(2,1)S(1)}, u32[]{:S(2)}, u32[]{:S(2)}) %collective-permute-start) | collective-permute-done | bytes 1032224 | tf_op jit(solution)/shard_map/ppermute | solution.py:260
  6.2 0.0 copy-done.3
  6.2 0.7 %source.1 = (bf16[16,128,128]{2,1,0:T(8,128)(2,1)S(1)}, bf16[16,128,128]{2,1,0:T(8,128)(2,1)S(1)}) custom-call(bf16[126,32,128]{2,1,0:T(8,128)(2,1)S(1)} %get-tuple-element.15.own, bf16[126,32,128]{2,1,0:T(8,128)(2,1)S(1)} %collective-permute-done.got, bf16[1,32,128]{2,1,0:T(8,128)(2,1)S(1)} %copy-done.3, f32[32,128]{1,0:T(8,128)S(1)} %get-tuple-element.16.adj), custom_call_target="tpu_custom_call" | custom-call | flops 1048576 | bytes 4194304 | tf_op jit(solution)/shard_map/source/pallas_call | solution.py:271
  6.9 3.4 %collective-permute-start.3 = (bf16[16,128,128]{2,1,0:T(8,128)(2,1)S(1)}, bf16[16,128,128]{2,1,0:T(8,128)(2,1)S(1)}, u32[]{:S(2)}, u32[]{:S(2)}) collective-permute-start(bf16[16,128,128]{2,1,0:T(8,128)(2,1)S(1)} %get-tuple-element.17.second), channel_id=1, source_target_pairs={{0,1},{2,3},{4,5},{6,7},{8,9},{10,11},{12,13},{14,15},{16,17},{18,... | collective-permute-start | bytes 1572872 | tf_op jit(solution)/shard_map/ppermute | solution.py:286
  10.3 6.0 %collective-permute-start.2 = (bf16[16,128,128]{2,1,0:T(8,128)(2,1)S(1)}, bf16[16,128,128]{2,1,0:T(8,128)(2,1)S(1)}, u32[]{:S(2)}, u32[]{:S(2)}) collective-permute-start(bf16[16,128,128]{2,1,0:T(8,128)(2,1)S(1)} %get-tuple-element.18.first), channel_id=1, source_target_pairs={{1,2},{3,4},{5,6},{7,8},{9,10},{11,12},{13,14},{15,16},{17,18},{19... | collective-permute-start | bytes 1572872 | tf_op jit(solution)/shard_map/ppermute | solution.py:286
  16.3 1.9 %collective-permute-start.4 = (bf16[16,128,128]{2,1,0:T(8,128)(2,1)S(1)}, bf16[16,128,128]{2,1,0:T(8,128)(2,1)S(1)}, u32[]{:S(2)}, u32[]{:S(2)}) collective-permute-start(bf16[16,128,128]{2,1,0:T(8,128)(2,1)S(1)} %get-tuple-element.18.first), channel_id=1, source_target_pairs={{0,1},{2,3},{4,5},{6,7},{8,9},{10,11},{12,13},{14,15},{16,17},{18,... | collective-permute-start | bytes 1572872 | tf_op jit(solution)/shard_map/ppermute | solution.py:286
  18.2 5.3 %collective-permute-start.1 = (bf16[16,128,128]{2,1,0:T(8,128)(2,1)S(1)}, bf16[16,128,128]{2,1,0:T(8,128)(2,1)S(1)}, u32[]{:S(2)}, u32[]{:S(2)}) collective-permute-start(bf16[16,128,128]{2,1,0:T(8,128)(2,1)S(1)} %get-tuple-element.17.second), channel_id=1, source_target_pairs={{1,2},{3,4},{5,6},{7,8},{9,10},{11,12},{13,14},{15,16},{17,18},{19... | collective-permute-start | bytes 1572872 | tf_op jit(solution)/shard_map/ppermute | solution.py:286
  23.5 0.0 copy-done
  23.5 7.0 %own_terms.1.acc_in = f32[33,128,128]{2,1,0:T(8,128)S(1)} custom-call(bf16[16,128,128]{2,1,0:T(8,128)(2,1)S(1)} %get-tuple-element.18.first, bf16[16,128,128]{2,1,0:T(8,128)(2,1)S(1)} %get-tuple-element.17.second, bf16[32,128,128]{2,1,0:T(8,128)(2,1)S(1)} %copy-done), custom_call_target="tpu_custom_call" | custom-call | flops 1073741824 | bytes 16777216 | tf_op jit(solution)/shard_map/own_terms/pallas_call | solution.py:304
  30.5 0.0 collective-permute-done.3.from_a
  30.6 1.9 %collective-permute-done.2.from_b = bf16[16,128,128]{2,1,0:T(8,128)(2,1)S(1)} collective-permute-done((bf16[16,128,128]{2,1,0:T(8,128)(2,1)S(1)}, bf16[16,128,128]{2,1,0:T(8,128)(2,1)S(1)}, u32[]{:S(2)}, u32[]{:S(2)}) %collective-permute-start.2) | collective-permute-done | bytes 524320 | tf_op jit(solution)/shard_map/ppermute | solution.py:286
  32.4 5.4 %chunk_terms.1 = (f32[33,128,128]{2,1,0:T(8,128)S(1)}, s32[24,128]{1,0:T(8,128)S(1)}, s32[24,128]{1,0:T(8,128)S(1)}) custom-call(bf16[16,128,128]{2,1,0:T(8,128)(2,1)S(1)} %collective-permute-done.2.from_b, bf16[16,128,128]{2,1,0:T(8,128)(2,1)S(1)} %collective-permute-done.3.from_a, ...), custom_call_target="tpu_custom_call", output_to_operand_aliasing={{0}: (3, {})} | custom-call | flops 805306368 | bytes 12582912 | tf_op jit(solution)/shard_map/chunk_terms/pallas_call | solution.py:314
  37.9 0.0 collective-permute-done.4.from_a
  37.9 2.6 %last_a.1 = (bf16[1,125,32,128]{3,2,1,0:T(8,128)(2,1)}, f32[33,128,128]{2,1,0:T(8,128)S(1)}) custom-call(bf16[16,128,128]{2,1,0:T(8,128)(2,1)S(1)} %collective-permute-done.4.from_a, s32[24,128]{1,0:T(8,128)S(1)} %get-tuple-element.20.lists, bf16[32,128,128]{2,1,0:T(8,128)(2,1)S(1)} %copy-done, ...), custom_call_target="tpu_custom_call", output_to_operand_aliasing={{1}: (3, {})} | custom-call | flops 134217728 | bytes 2097152 | tf_op jit(solution)/shard_map/last_a/pallas_call | solution.py:325
  40.5 2.0 %collective-permute-done.1.from_b = bf16[16,128,128]{2,1,0:T(8,128)(2,1)S(1)} collective-permute-done((bf16[16,128,128]{2,1,0:T(8,128)(2,1)S(1)}, bf16[16,128,128]{2,1,0:T(8,128)(2,1)S(1)}, u32[]{:S(2)}, u32[]{:S(2)}) %collective-permute-start.1) | collective-permute-done | bytes 524320 | tf_op jit(solution)/shard_map/ppermute | solution.py:286
  42.5 2.6 %last_b.1 = (bf16[1,125,32,128]{3,2,1,0:T(8,128)(2,1)}, f32[33,128,128]{2,1,0:T(8,128)S(1)}) custom-call(bf16[16,128,128]{2,1,0:T(8,128)(2,1)S(1)} %collective-permute-done.1.from_b, s32[24,128]{1,0:T(8,128)S(1)} %get-tuple-element.19.lists, bf16[32,128,128]{2,1,0:T(8,128)(2,1)S(1)} %copy-done, ...), custom_call_target="tpu_custom_call", output_to_operand_aliasing={{1}: (3, {}), {0}: (4, {})} | custom-call | flops 134217728 | bytes 2097152 | tf_op jit(solution)/shard_map/last_b/pallas_call | solution.py:336
Async XLA Ops:
  0.0 3.6 %copy-start.1 = (s32[1,1,32,16]{2,3,1,0:T(8,128)S(1)}, s32[1,1,32,16]{2,3,1,0:T(8,128)}, u32[]{:S(2)}) copy-start(s32[1,1,32,16]{2,3,1,0:T(8,128)} %param.10) | copy-start | bytes 6148
  0.0 3.6 %copy-start.2 = (s32[1,1,32,16]{2,3,1,0:T(8,128)S(1)}, s32[1,1,32,16]{2,3,1,0:T(8,128)}, u32[]{:S(2)}) copy-start(s32[1,1,32,16]{2,3,1,0:T(8,128)} %param.11) | copy-start | bytes 6148
  1.7 4.5 %copy-start.3 = (bf16[1,32,128]{2,1,0:T(8,128)(2,1)S(1)}, bf16[1,32,128]{2,1,0:T(8,128)(2,1)}, u32[]{:S(2)}) copy-start(bf16[1,32,128]{2,1,0:T(8,128)(2,1)} %vol.1) | copy-start | bytes 24580
  1.7 4.5 %collective-permute-start = (bf16[126,32,128]{2,1,0:T(8,128)(2,1)S(1)}, bf16[126,32,128]{2,1,0:T(8,128)(2,1)S(1)}, u32[]{:S(2)}, u32[]{:S(2)}) collective-permute-start(bf16[126,32,128]{2,1,0:T(8,128)(2,1)S(1)} %send.1), channel_id=1, source_target_pairs={{0,256},{256,0},{1,257},{257,1},{2,258},{258,2},{3,259},{259,3},{4... | collective-permute-start | bytes 3096584 | tf_op jit(solution)/shard_map/ppermute | solution.py:260
  3.6 19.9 %copy-start = (bf16[32,128,128]{2,1,0:T(8,128)(2,1)S(1)}, bf16[32,128,128]{2,1,0:T(8,128)(2,1)}, u32[]{:S(2)}) copy-start(bf16[32,128,128]{2,1,0:T(8,128)(2,1)} %tables.7) | copy-start | bytes 3145732
  6.9 23.7 %collective-permute-start.3 = (bf16[16,128,128]{2,1,0:T(8,128)(2,1)S(1)}, bf16[16,128,128]{2,1,0:T(8,128)(2,1)S(1)}, u32[]{:S(2)}, u32[]{:S(2)}) collective-permute-start(bf16[16,128,128]{2,1,0:T(8,128)(2,1)S(1)} %get-tuple-element.17.second), channel_id=1, source_target_pairs={{0,1},{2,3},{4,5},{6,7},{8,9},{10,11},{12,13},{14,15},{16,17},{18,... | collective-permute-start | bytes 1572872 | tf_op jit(solution)/shard_map/ppermute | solution.py:286
  10.3 22.1 %collective-permute-start.2 = (bf16[16,128,128]{2,1,0:T(8,128)(2,1)S(1)}, bf16[16,128,128]{2,1,0:T(8,128)(2,1)S(1)}, u32[]{:S(2)}, u32[]{:S(2)}) collective-permute-start(bf16[16,128,128]{2,1,0:T(8,128)(2,1)S(1)} %get-tuple-element.18.first), channel_id=1, source_target_pairs={{1,2},{3,4},{5,6},{7,8},{9,10},{11,12},{13,14},{15,16},{17,18},{19... | collective-permute-start | bytes 1572872 | tf_op jit(solution)/shard_map/ppermute | solution.py:286
  16.3 21.6 %collective-permute-start.4 = (bf16[16,128,128]{2,1,0:T(8,128)(2,1)S(1)}, bf16[16,128,128]{2,1,0:T(8,128)(2,1)S(1)}, u32[]{:S(2)}, u32[]{:S(2)}) collective-permute-start(bf16[16,128,128]{2,1,0:T(8,128)(2,1)S(1)} %get-tuple-element.18.first), channel_id=1, source_target_pairs={{0,1},{2,3},{4,5},{6,7},{8,9},{10,11},{12,13},{14,15},{16,17},{18,... | collective-permute-start | bytes 1572872 | tf_op jit(solution)/shard_map/ppermute | solution.py:286
  18.2 24.3 %collective-permute-start.1 = (bf16[16,128,128]{2,1,0:T(8,128)(2,1)S(1)}, bf16[16,128,128]{2,1,0:T(8,128)(2,1)S(1)}, u32[]{:S(2)}, u32[]{:S(2)}) collective-permute-start(bf16[16,128,128]{2,1,0:T(8,128)(2,1)S(1)} %get-tuple-element.17.second), channel_id=1, source_target_pairs={{1,2},{3,4},{5,6},{7,8},{9,10},{11,12},{13,14},{15,16},{17,18},{19... | collective-permute-start | bytes 1572872 | tf_op jit(solution)/shard_map/ppermute | solution.py:286

commit v4 on v3

--- a/solution.py
+++ b/solution.py
@@ -1,3 +1,5 @@
+import functools
+
 import jax
 import jax.numpy as jnp
 from jax import lax
@@ -15,7 +17,7 @@
 PB = 16
 U = 8
 PAIR_ROWS = 3
-OWN_LANE = 2 * OWN
+PREV_LANE, OWN_LANE, NEXT_LANE = 0, OWN, 2 * OWN
 MIB = 1 << 20
 COPY_ALIASED = False
 
@@ -41,11 +43,17 @@
     return pltpu.CompilerParams(vmem_limit_bytes=mib * MIB)
 
 
+def shifted(value, axis, steps):
+    count = lax.axis_size(axis)
+    first, last = (max(0, -steps), min(count, count - steps))
+    return lax.ppermute(value, axis, [(source, source + steps) for source in range(first, last)])
+
+
 def cost(flops, nbytes):
     return pl.CostEstimate(flops=flops, bytes_accessed=nbytes, transcendentals=0)
 
 
-PIECES = ((0, 32), (32, 32), (64, 32), (96, 29))
+PIECES = tuple((first, min(16, G - first)) for first in range(0, G, 16))
 
 
 def partial_sums(kern, counts, base, out, buf, cbuf, sems, csem):
@@ -79,12 +87,8 @@
 def keep_kernel(kern, counts, off, tab, out, adj, *scratch):
     steps = partial_sums(kern, counts, lax.axis_index("event") * OWN, out, *scratch)
     next(steps)
-    odd = lax.rem(lax.axis_index("dom"), 2)
     b = lax.broadcasted_iota(jnp.int32, (PB, OWN), 1)
-    x = off[0, 0] + b
-    part = x >> 5
-    group = jnp.where(part == 1, 2, jnp.where(part == 0, odd, 1 - odd))
-    lane = (x & (OWN - 1)) + group * OWN
+    lane = off[0, 0] + b
     value = (tab[0, 0] + 1).astype(jnp.float32)
     spot = lax.broadcasted_iota(jnp.int32, (3 * OWN, OWN), 0)
     turned = jnp.zeros((3 * OWN, OWN), jnp.float32)
@@ -97,18 +101,16 @@
         pass
 
 
-def source_kernel(own, got, vol, adj, first, second):
-    odd = lax.rem(lax.axis_index("dom"), 2)
-    for dst, half in ((first, odd), (second, 1 - odd)):
-        span = pl.ds(pl.multiple_of(half * HALF, HALF), HALF)
-        v = vol[0, span].astype(jnp.float32)
-        hits = own[G, span].astype(jnp.float32) + got[G, span].astype(jnp.float32)
-        factor = v / jnp.sqrt(1.0 + hits)
-        total = own[0:G, span].astype(jnp.float32) + got[0:G, span].astype(jnp.float32)
-        rest = pl.ds(pl.multiple_of((1 - half) * HALF, HALF), HALF)
-        rows = [total * factor[None], v[None], adj[span][None], adj[rest][None]]
-        block = jnp.concatenate(rows, axis=0)
-        dst[...] = jnp.transpose(block, (1, 0, 2)).astype(jnp.bfloat16)
+def source_kernel(half, own, got, vol, adj, dst):
+    span = slice(half * HALF, (half + 1) * HALF)
+    rest = slice((1 - half) * HALF, (2 - half) * HALF)
+    v = vol[0, span].astype(jnp.float32)
+    hits = own[G, span].astype(jnp.float32) + got[G, span].astype(jnp.float32)
+    factor = v / jnp.sqrt(1.0 + hits)
+    total = own[0:G, span].astype(jnp.float32) + got[0:G, span].astype(jnp.float32)
+    rows = [total * factor[None], v[None], adj[span][None], adj[rest][None]]
+    block = jnp.concatenate(rows, axis=0)
+    dst[...] = jnp.transpose(block, (1, 0, 2)).astype(jnp.bfloat16)
 
 
 def neighbours(ref, row, lane):
@@ -181,8 +183,8 @@
     lax.fori_loop(0, (codes[n + PAIR_ROWS, 0] + (U - 1)) >> 3, step, 0)
 
 
-def own_kernel(first, second, tables, acc, lists, *scratch):
-    adj = [neighbours(first, ADJ, OWN_LANE), neighbours(second, ADJ, OWN_LANE)]
+def own_kernel(low, high, tables, acc, lists, *scratch):
+    adj = [neighbours(low, ADJ, OWN_LANE), neighbours(high, ADJ, OWN_LANE)]
     make_lists(jnp.concatenate(adj, axis=0), lists)
 
     def clear(i, carry):
@@ -190,24 +192,23 @@
         return carry
 
     lax.fori_loop(0, OWN + 1, clear, 0)
-    add_terms((first, second), lists, tables, acc, *scratch)
-
-
-def chunk_kernel(from_b, from_a, tables, acc_in, acc, lists_a, lists_b, lists, *scratch):
+    add_terms((low, high), lists, tables, acc, *scratch)
+
+
+def chunk_kernel(from_next, from_prev, tables, acc_in, acc, lists_n, lists_p, lists, *scratch):
     if COPY_ALIASED:
         acc[...] = acc_in[...]
-    adj = [neighbours(from_b, ADJ, 0), neighbours(from_a, ADJ, OWN)]
+    adj = [neighbours(from_next, ADJ, PREV_LANE), neighbours(from_prev, ADJ, NEXT_LANE)]
     make_lists(jnp.concatenate(adj, axis=0), lists)
-    make_lists(neighbours(from_a, ADJ + 1, OWN), lists_a)
-    make_lists(neighbours(from_b, ADJ + 1, 0), lists_b)
-    add_terms((from_b, from_a), lists, tables, acc, *scratch)
+    make_lists(neighbours(from_next, ADJ + 1, PREV_LANE), lists_n)
+    make_lists(neighbours(from_prev, ADJ + 1, NEXT_LANE), lists_p)
+    add_terms((from_next, from_prev), lists, tables, acc, *scratch)
 
 
 def finish(half, acc, out, stage, sems):
     copies = []
     for c in range(HALF // 8):
-        first = pl.multiple_of(half * HALF + c * 8, 8)
-        span = pl.ds(first, 8)
+        span = slice(half * HALF + c * 8, half * HALF + c * 8 + 8)
         scale = 1.0 / acc[span, G : G + 1]
         result = jnp.transpose(acc[span] * scale, (1, 0, 2))
         stage[c] = result[0:G].astype(jnp.bfloat16)
@@ -217,19 +218,19 @@
         copy.wait()
 
 
-def last_a_kernel(from_a, lists, tables, acc_in, out, acc, stage, sems, *scratch):
+def last_n_kernel(source, lists, tables, acc_in, out, acc, stage, sems, *scratch):
     if COPY_ALIASED:
         acc[...] = acc_in[...]
-    add_terms((from_a,), lists, tables, acc, *scratch)
-    finish(1 - lax.rem(lax.axis_index("dom"), 2), acc, out, stage, sems)
-
-
-def last_b_kernel(from_b, lists, tables, acc_in, out_in, out, acc, stage, sems, *scratch):
+    add_terms((source,), lists, tables, acc, *scratch)
+    finish(1, acc, out, stage, sems)
+
+
+def last_p_kernel(source, lists, tables, acc_in, out_in, out, acc, stage, sems, *scratch):
     if COPY_ALIASED:
         acc[...] = acc_in[...]
         pltpu.sync_copy(out_in, out)
-    add_terms((from_b,), lists, tables, acc, *scratch)
-    finish(lax.rem(lax.axis_index("dom"), 2), acc, out, stage, sems)
+    add_terms((source,), lists, tables, acc, *scratch)
+    finish(0, acc, out, stage, sems)
 
 
 def per_device(kernels, counts, volume, tables, pair_offset, pair_table):
@@ -268,27 +269,26 @@
         cost_estimate=cost(1 << 20, 4 << 20),
         name="keep",
     )(kernels, counts, pair_offset, pair_table)
-    first, second = pl.pallas_call(
-        source_kernel,
-        out_shape=[on_chip((HALF, ROWS, W), bf16)] * 2,
-        in_specs=[VMEM] * 4,
-        out_specs=[VMEM] * 2,
-        compiler_params=params(6),
-        cost_estimate=cost(1 << 20, 4 << 20),
-        name="source",
-    )(own, in_vmem(got), volume, adj)
-
-    count = lax.axis_size("dom")
-
-    def swapped(value, start):
-        pairs = [(a, a + 1) for a in range(start, count - 1, 2)]
-        pairs = pairs + [(b, a) for a, b in pairs]
-        return lax.ppermute(value, "dom", pairs)
-
-    a0 = swapped(second, 0)
-    b0 = swapped(first, 1)
-    a1 = swapped(first, 0)
-    b1 = swapped(second, 1)
+
+    def source(half):
+        return pl.pallas_call(
+            functools.partial(source_kernel, half),
+            out_shape=on_chip((HALF, ROWS, W), bf16),
+            in_specs=[VMEM] * 4,
+            out_specs=VMEM,
+            compiler_params=params(6),
+            cost_estimate=cost(1 << 20, 2 << 20),
+        )(own, in_vmem(got), volume, adj)
+
+    def moved(value, steps):
+        return in_vmem(shifted(value, "dom", steps))
+
+    high = source(1)
+    p0 = moved(high, 1)
+    low = source(0)
+    n0 = moved(low, -1)
+    p1 = moved(low, 1)
+    n1 = moved(high, -1)
 
     acc_shape = on_chip((OWN + 1, ROWS, W), f32)
     out_shape = jax.ShapeDtypeStruct((1, G, OWN, W), bf16)
@@ -310,8 +310,8 @@
         compiler_params=params(6),
         cost_estimate=cost(256 * term, 16 << 20),
         name="own_terms",
-    )(first, second, tables)
-    acc, lists_a, lists_b = pl.pallas_call(
+    )(low, high, tables)
+    acc, lists_n, lists_p = pl.pallas_call(
         chunk_kernel,
         out_shape=[acc_shape] + [on_chip(lists(HALF), i32)] * 2,
         in_specs=[VMEM] * 4,
@@ -321,9 +321,9 @@
         compiler_params=params(6),
         cost_estimate=cost(192 * term, 12 << 20),
         name="chunk_terms",
-    )(in_vmem(b0), in_vmem(a0), tables, acc)
+    )(n0, p0, tables, acc)
     out, acc = pl.pallas_call(
-        last_a_kernel,
+        last_n_kernel,
         out_shape=[out_shape, acc_shape],
         in_specs=[VMEM] * 4,
         out_specs=[HBM, VMEM],
@@ -331,10 +331,10 @@
         input_output_aliases={3: 1},
         compiler_params=params(6),
         cost_estimate=cost(32 * term, 2 << 20),
-        name="last_a",
-    )(in_vmem(a1), lists_a, tables, acc)
+        name="last_n",
+    )(n1, lists_n, tables, acc)
     out, _ = pl.pallas_call(
-        last_b_kernel,
+        last_p_kernel,
         out_shape=[out_shape, acc_shape],
         in_specs=[VMEM] * 4 + [HBM],
         out_specs=[HBM, VMEM],
@@ -342,8 +342,8 @@
         input_output_aliases={3: 1, 4: 0},
         compiler_params=params(6),
         cost_estimate=cost(32 * term, 2 << 20),
-        name="last_b",
-    )(in_vmem(b1), lists_b, tables, acc, out)
+        name="last_p",
+    )(p1, lists_p, tables, acc, out)
     return jnp.transpose(out, (0, 2, 1, 3))
 
 

time: 45.5 us -> 48.7 us (1.070)
  starting transfers between devices: 18.5 us -> 21.8 us
    ppermute x4, starting transfers between devices: 16.6 us -> 19.9 us  [shifted(): lax.ppermute(value, axis, [(source, source + steps) for source in range(f...]
    pallas_call x3 -> x4, Pallas kernels: 5.94 us -> 5.96 us  [the longest x1 2.63 us: per_device(): pl.pallas_call(last_n_kernel, out_shape=[out_shape, acc_shape], in_specs=...]
  transfers between devices with their start and end apart: 5 -> 5, of which waited for: 3 -> 3; matrix products, arithmetic and copies ran while one was open for 0% -> 0% of each run, Pallas kernels for 37% -> 35%
where the time goes in v4:
time: 48.7 us; the launch traced here: 48.4 us
  starting transfers between devices  21.8 us (45%)
  Pallas kernels  21.7 us (45%)
  waiting for transfers between devices  4.83 us (10%)
    ppermute x4, starting transfers between devices, shifted(): lax.ppermute(value, axis, [(source, source + steps) for source in range(f...  19.9 us
    pallas_call x1, Pallas kernels, per_device(): pl.pallas_call(own_kernel, out_shape=acc_shape, in_specs=[VMEM] * 3, out_...  7.01 us
    pallas_call x1, Pallas kernels, per_device(): pl.pallas_call(chunk_kernel, out_shape=[acc_shape] + [on_chip(lists(HALF)...  5.44 us
    ppermute x4, waiting for transfers between devices, shifted(): lax.ppermute(value, axis, [(source, source + steps) for source in range(f...  3.89 us
    pallas_call x1, Pallas kernels, per_device(): pl.pallas_call(last_n_kernel, out_shape=[out_shape, acc_shape], in_specs=...  2.63 us
    pallas_call x1, Pallas kernels, per_device(): pl.pallas_call(last_p_kernel, out_shape=[out_shape, acc_shape], in_specs=...  2.63 us
    ppermute x1, starting transfers between devices, per_device(): got = lax.ppermute(to_other, 'event', [(0, 1), (1, 0)])  1.92 us
    pallas_call x1, Pallas kernels, per_device(): pl.pallas_call(send_kernel, out_shape=sums, in_specs=[HBM, HBM], out_spec...  1.64 us
  transfers between devices with their start and end apart: 5, of which 3 were waited for; matrix products, arithmetic and copies ran while one was open for 0% of the time, Pallas kernels for 35%

profile of v4, /device:TPU:256, one launch (start us, length us, event | category | flops | bytes accessed | tf_op | source)
XLA Modules:
  0.0 48.4 jit_solution(6684542901370645454)
XLA Ops:
  0.0 0.0 copy-start.2
  0.0 0.0 copy-start.3
  0.0 1.6 %send.1 = bf16[126,32,128]{2,1,0:T(8,128)(2,1)S(1)} custom-call(bf16[2,1,125,64,128]{4,3,2,1,0:T(8,128)(2,1)} %bitcast.6, s32[2,1,64,128]{3,2,1,0:T(8,128)} %counts.3), custom_call_target="tpu_custom_call" | custom-call | flops 1048576 | bytes 4194304 | tf_op jit(solution)/shard_map/send/pallas_call | solution.py:251
  1.7 0.0 copy-start.1
  1.7 1.9 %collective-permute-start = (bf16[126,32,128]{2,1,0:T(8,128)(2,1)S(1)}, bf16[126,32,128]{2,1,0:T(8,128)(2,1)S(1)}, u32[]{:S(2)}, u32[]{:S(2)}) collective-permute-start(bf16[126,32,128]{2,1,0:T(8,128)(2,1)S(1)} %send.1), channel_id=1, source_target_pairs={{0,256},{256,0},{1,257},{257,1},{2,258},{258,2},{3,259},{259,3},{4... | collective-permute-start | bytes 3096584 | tf_op jit(solution)/shard_map/ppermute | solution.py:261
  3.6 0.0 copy-done.2
  3.6 0.0 copy-done.3
  3.6 1.6 %keep.1 = (bf16[126,32,128]{2,1,0:T(8,128)(2,1)S(1)}, f32[32,128]{1,0:T(8,128)S(1)}) custom-call(bf16[2,1,125,64,128]{4,3,2,1,0:T(8,128)(2,1)} %bitcast.7, s32[2,1,64,128]{3,2,1,0:T(8,128)} %counts.3, s32[1,1,16,32]{3,2,1,0:T(8,128)S(1)} %bitcast.4, s32[1,1,16,32]{3,2,1,0:T(8,128)S(1)} %bitcast.5), custom_call_target="tpu_custom_call" | custom-call | flops 1048576 | bytes 4194304 | tf_op jit(solution)/shard_map/keep/pallas_call | solution.py:262
  5.3 0.9 %collective-permute-done.got = bf16[126,32,128]{2,1,0:T(8,128)(2,1)S(1)} collective-permute-done((bf16[126,32,128]{2,1,0:T(8,128)(2,1)S(1)}, bf16[126,32,128]{2,1,0:T(8,128)(2,1)S(1)}, u32[]{:S(2)}, u32[]{:S(2)}) %collective-permute-start) | collective-permute-done | bytes 1032224 | tf_op jit(solution)/shard_map/ppermute | solution.py:261
  6.2 0.0 copy-done.1
  6.2 0.0 copy-start
  6.2 0.3 shard_map.64.low
  6.6 6.7 %collective-permute-start.2 = (bf16[16,128,128]{2,1,0:T(8,128)(2,1)S(1)}, bf16[16,128,128]{2,1,0:T(8,128)(2,1)S(1)}, u32[]{:S(2)}, u32[]{:S(2)}) collective-permute-start(bf16[16,128,128]{2,1,0:T(8,128)(2,1)S(1)} %shard_map.64.low), channel_id=1, source_target_pairs={{1,0},{2,1},{3,2},{4,3},{5,4},{6,5},{7,6},{8,7},{9,8},{10,9},{11,1... | collective-permute-start | bytes 1572872 | tf_op jit(solution)/shard_map/ppermute | solution.py:49
  13.2 0.3 shard_map.65.high
  13.6 1.9 %collective-permute-start.3 = (bf16[16,128,128]{2,1,0:T(8,128)(2,1)S(1)}, bf16[16,128,128]{2,1,0:T(8,128)(2,1)S(1)}, u32[]{:S(2)}, u32[]{:S(2)}) collective-permute-start(bf16[16,128,128]{2,1,0:T(8,128)(2,1)S(1)} %shard_map.65.high), channel_id=1, source_target_pairs={{0,1},{1,2},{2,3},{3,4},{4,5},{5,6},{6,7},{7,8},{8,9},{9,10},{10,1... | collective-permute-start | bytes 1572872 | tf_op jit(solution)/shard_map/ppermute | solution.py:49
  15.5 9.4 %collective-permute-start.4 = (bf16[16,128,128]{2,1,0:T(8,128)(2,1)S(1)}, bf16[16,128,128]{2,1,0:T(8,128)(2,1)S(1)}, u32[]{:S(2)}, u32[]{:S(2)}) collective-permute-start(bf16[16,128,128]{2,1,0:T(8,128)(2,1)S(1)} %shard_map.65.high), channel_id=1, source_target_pairs={{1,0},{2,1},{3,2},{4,3},{5,4},{6,5},{7,6},{8,7},{9,8},{10,9},{11,1... | collective-permute-start | bytes 1572872 | tf_op jit(solution)/shard_map/ppermute | solution.py:49
  24.9 1.9 %collective-permute-start.1 = (bf16[16,128,128]{2,1,0:T(8,128)(2,1)S(1)}, bf16[16,128,128]{2,1,0:T(8,128)(2,1)S(1)}, u32[]{:S(2)}, u32[]{:S(2)}) collective-permute-start(bf16[16,128,128]{2,1,0:T(8,128)(2,1)S(1)} %shard_map.64.low), channel_id=1, source_target_pairs={{0,1},{1,2},{2,3},{3,4},{4,5},{5,6},{6,7},{7,8},{8,9},{9,10},{10,1... | collective-permute-start | bytes 1572872 | tf_op jit(solution)/shard_map/ppermute | solution.py:49
  26.8 0.0 copy-done
  26.8 7.0 %own_terms.1.acc_in = f32[33,128,128]{2,1,0:T(8,128)S(1)} custom-call(bf16[16,128,128]{2,1,0:T(8,128)(2,1)S(1)} %shard_map.64.low, bf16[16,128,128]{2,1,0:T(8,128)(2,1)S(1)} %shard_map.65.high, bf16[32,128,128]{2,1,0:T(8,128)(2,1)S(1)} %copy-done), custom_call_target="tpu_custom_call" | custom-call | flops 1073741824 | bytes 16777216 | tf_op jit(solution)/shard_map/own_terms/pallas_call | solution.py:304
  33.8 0.0 collective-permute-done.2.from_next
  33.8 1.3 %collective-permute-done.3.from_prev = bf16[16,128,128]{2,1,0:T(8,128)(2,1)S(1)} collective-permute-done((bf16[16,128,128]{2,1,0:T(8,128)(2,1)S(1)}, bf16[16,128,128]{2,1,0:T(8,128)(2,1)S(1)}, u32[]{:S(2)}, u32[]{:S(2)}) %collective-permute-start.3) | collective-permute-done | bytes 524320 | tf_op jit(solution)/shard_map/ppermute | solution.py:49
  35.1 5.4 %chunk_terms.1 = (f32[33,128,128]{2,1,0:T(8,128)S(1)}, s32[24,128]{1,0:T(8,128)S(1)}, s32[24,128]{1,0:T(8,128)S(1)}) custom-call(bf16[16,128,128]{2,1,0:T(8,128)(2,1)S(1)} %collective-permute-done.2.from_next, bf16[16,128,128]{2,1,0:T(8,128)(2,1)S(1)} %collective-permute-done.3.from_prev, ...), custom_call_target="tpu_custom_call", output_to_operand_aliasing={{0}: (3, {})} | custom-call | flops 805306368 | bytes 12582912 | tf_op jit(solution)/shard_map/chunk_terms/pallas_call | solution.py:314
  40.5 0.0 collective-permute-done.4.source
  40.5 2.6 %last_n.1 = (bf16[1,125,32,128]{3,2,1,0:T(8,128)(2,1)}, f32[33,128,128]{2,1,0:T(8,128)S(1)}) custom-call(bf16[16,128,128]{2,1,0:T(8,128)(2,1)S(1)} %collective-permute-done.4.source, s32[24,128]{1,0:T(8,128)S(1)} %get-tuple-element.16.lists, bf16[32,128,128]{2,1,0:T(8,128)(2,1)S(1)} %copy-done, ...), custom_call_target="tpu_custom_call", output_to_operand_aliasing={{1}: (3, {})} | custom-call | flops 134217728 | bytes 2097152 | tf_op jit(solution)/shard_map/last_n/pallas_call | solution.py:325
  43.2 2.6 %collective-permute-done.1.source = bf16[16,128,128]{2,1,0:T(8,128)(2,1)S(1)} collective-permute-done((bf16[16,128,128]{2,1,0:T(8,128)(2,1)S(1)}, bf16[16,128,128]{2,1,0:T(8,128)(2,1)S(1)}, u32[]{:S(2)}, u32[]{:S(2)}) %collective-permute-start.1) | collective-permute-done | bytes 524320 | tf_op jit(solution)/shard_map/ppermute | solution.py:49
  45.8 2.6 %last_p.1 = (bf16[1,125,32,128]{3,2,1,0:T(8,128)(2,1)}, f32[33,128,128]{2,1,0:T(8,128)S(1)}) custom-call(bf16[16,128,128]{2,1,0:T(8,128)(2,1)S(1)} %collective-permute-done.1.source, s32[24,128]{1,0:T(8,128)S(1)} %get-tuple-element.15.lists, bf16[32,128,128]{2,1,0:T(8,128)(2,1)S(1)} %copy-done, ...), custom_call_target="tpu_custom_call", output_to_operand_aliasing={{1}: (3, {}), {0}: (4, {})} | custom-call | flops 134217728 | bytes 2097152 | tf_op jit(solution)/shard_map/last_p/pallas_call | solution.py:336
Async XLA Ops:
  0.0 3.6 %copy-start.2 = (s32[1,1,32,16]{2,3,1,0:T(8,128)S(1)}, s32[1,1,32,16]{2,3,1,0:T(8,128)}, u32[]{:S(2)}) copy-start(s32[1,1,32,16]{2,3,1,0:T(8,128)} %param.10) | copy-start | bytes 6148
  0.0 3.6 %copy-start.3 = (s32[1,1,32,16]{2,3,1,0:T(8,128)S(1)}, s32[1,1,32,16]{2,3,1,0:T(8,128)}, u32[]{:S(2)}) copy-start(s32[1,1,32,16]{2,3,1,0:T(8,128)} %param.11) | copy-start | bytes 6148
  1.7 4.5 %copy-start.1 = (bf16[1,32,128]{2,1,0:T(8,128)(2,1)S(1)}, bf16[1,32,128]{2,1,0:T(8,128)(2,1)}, u32[]{:S(2)}) copy-start(bf16[1,32,128]{2,1,0:T(8,128)(2,1)} %vol.3) | copy-start | bytes 24580
  1.7 4.5 %collective-permute-start = (bf16[126,32,128]{2,1,0:T(8,128)(2,1)S(1)}, bf16[126,32,128]{2,1,0:T(8,128)(2,1)S(1)}, u32[]{:S(2)}, u32[]{:S(2)}) collective-permute-start(bf16[126,32,128]{2,1,0:T(8,128)(2,1)S(1)} %send.1), channel_id=1, source_target_pairs={{0,256},{256,0},{1,257},{257,1},{2,258},{258,2},{3,259},{259,3},{4... | collective-permute-start | bytes 3096584 | tf_op jit(solution)/shard_map/ppermute | solution.py:261
  6.2 20.6 %copy-start = (bf16[32,128,128]{2,1,0:T(8,128)(2,1)S(1)}, bf16[32,128,128]{2,1,0:T(8,128)(2,1)}, u32[]{:S(2)}) copy-start(bf16[32,128,128]{2,1,0:T(8,128)(2,1)} %tables.7) | copy-start | bytes 3145732
  6.6 27.3 %collective-permute-start.2 = (bf16[16,128,128]{2,1,0:T(8,128)(2,1)S(1)}, bf16[16,128,128]{2,1,0:T(8,128)(2,1)S(1)}, u32[]{:S(2)}, u32[]{:S(2)}) collective-permute-start(bf16[16,128,128]{2,1,0:T(8,128)(2,1)S(1)} %shard_map.64.low), channel_id=1, source_target_pairs={{1,0},{2,1},{3,2},{4,3},{5,4},{6,5},{7,6},{8,7},{9,8},{10,9},{11,1... | collective-permute-start | bytes 1572872 | tf_op jit(solution)/shard_map/ppermute | solution.py:49
  13.6 21.5 %collective-permute-start.3 = (bf16[16,128,128]{2,1,0:T(8,128)(2,1)S(1)}, bf16[16,128,128]{2,1,0:T(8,128)(2,1)S(1)}, u32[]{:S(2)}, u32[]{:S(2)}) collective-permute-start(bf16[16,128,128]{2,1,0:T(8,128)(2,1)S(1)} %shard_map.65.high), channel_id=1, source_target_pairs={{0,1},{1,2},{2,3},{3,4},{4,5},{5,6},{6,7},{7,8},{8,9},{9,10},{10,1... | collective-permute-start | bytes 1572872 | tf_op jit(solution)/shard_map/ppermute | solution.py:49
  15.5 25.0 %collective-permute-start.4 = (bf16[16,128,128]{2,1,0:T(8,128)(2,1)S(1)}, bf16[16,128,128]{2,1,0:T(8,128)(2,1)S(1)}, u32[]{:S(2)}, u32[]{:S(2)}) collective-permute-start(bf16[16,128,128]{2,1,0:T(8,128)(2,1)S(1)} %shard_map.65.high), channel_id=1, source_target_pairs={{1,0},{2,1},{3,2},{4,3},{5,4},{6,5},{7,6},{8,7},{9,8},{10,9},{11,1... | collective-permute-start | bytes 1572872 | tf_op jit(solution)/shard_map/ppermute | solution.py:49
  24.9 21.0 %collective-permute-start.1 = (bf16[16,128,128]{2,1,0:T(8,128)(2,1)S(1)}, bf16[16,128,128]{2,1,0:T(8,128)(2,1)S(1)}, u32[]{:S(2)}, u32[]{:S(2)}) collective-permute-start(bf16[16,128,128]{2,1,0:T(8,128)(2,1)S(1)} %shard_map.64.low), channel_id=1, source_target_pairs={{0,1},{1,2},{2,3},{3,4},{4,5},{5,6},{6,7},{7,8},{8,9},{9,10},{10,1... | collective-permute-start | bytes 1572872 | tf_op jit(solution)/shard_map/ppermute | solution.py:49

commit v5 on v3

--- a/solution.py
+++ b/solution.py
@@ -1,3 +1,5 @@
+import functools
+
 import jax
 import jax.numpy as jnp
 from jax import lax
@@ -45,7 +47,7 @@
     return pl.CostEstimate(flops=flops, bytes_accessed=nbytes, transcendentals=0)
 
 
-PIECES = ((0, 32), (32, 32), (64, 32), (96, 29))
+PIECES = tuple((first, min(16, G - first)) for first in range(0, G, 16))
 
 
 def partial_sums(kern, counts, base, out, buf, cbuf, sems, csem):
@@ -97,18 +99,18 @@
         pass
 
 
-def source_kernel(own, got, vol, adj, first, second):
+def source_kernel(leaves_first, own, got, vol, adj, dst):
     odd = lax.rem(lax.axis_index("dom"), 2)
-    for dst, half in ((first, odd), (second, 1 - odd)):
-        span = pl.ds(pl.multiple_of(half * HALF, HALF), HALF)
-        v = vol[0, span].astype(jnp.float32)
-        hits = own[G, span].astype(jnp.float32) + got[G, span].astype(jnp.float32)
-        factor = v / jnp.sqrt(1.0 + hits)
-        total = own[0:G, span].astype(jnp.float32) + got[0:G, span].astype(jnp.float32)
-        rest = pl.ds(pl.multiple_of((1 - half) * HALF, HALF), HALF)
-        rows = [total * factor[None], v[None], adj[span][None], adj[rest][None]]
-        block = jnp.concatenate(rows, axis=0)
-        dst[...] = jnp.transpose(block, (1, 0, 2)).astype(jnp.bfloat16)
+    half = odd if leaves_first else 1 - odd
+    span = pl.ds(pl.multiple_of(half * HALF, HALF), HALF)
+    rest = pl.ds(pl.multiple_of((1 - half) * HALF, HALF), HALF)
+    v = vol[0, span].astype(jnp.float32)
+    hits = own[G, span].astype(jnp.float32) + got[G, span].astype(jnp.float32)
+    factor = v / jnp.sqrt(1.0 + hits)
+    total = own[0:G, span].astype(jnp.float32) + got[0:G, span].astype(jnp.float32)
+    rows = [total * factor[None], v[None], adj[span][None], adj[rest][None]]
+    block = jnp.concatenate(rows, axis=0)
+    dst[...] = jnp.transpose(block, (1, 0, 2)).astype(jnp.bfloat16)
 
 
 def neighbours(ref, row, lane):
@@ -217,19 +219,19 @@
         copy.wait()
 
 
-def last_a_kernel(from_a, lists, tables, acc_in, out, acc, stage, sems, *scratch):
+def last_b_kernel(from_b, lists, tables, acc_in, out, acc, stage, sems, *scratch):
     if COPY_ALIASED:
         acc[...] = acc_in[...]
-    add_terms((from_a,), lists, tables, acc, *scratch)
-    finish(1 - lax.rem(lax.axis_index("dom"), 2), acc, out, stage, sems)
-
-
-def last_b_kernel(from_b, lists, tables, acc_in, out_in, out, acc, stage, sems, *scratch):
+    add_terms((from_b,), lists, tables, acc, *scratch)
+    finish(lax.rem(lax.axis_index("dom"), 2), acc, out, stage, sems)
+
+
+def last_a_kernel(from_a, lists, tables, acc_in, out_in, out, acc, stage, sems, *scratch):
     if COPY_ALIASED:
         acc[...] = acc_in[...]
         pltpu.sync_copy(out_in, out)
-    add_terms((from_b,), lists, tables, acc, *scratch)
-    finish(lax.rem(lax.axis_index("dom"), 2), acc, out, stage, sems)
+    add_terms((from_a,), lists, tables, acc, *scratch)
+    finish(1 - lax.rem(lax.axis_index("dom"), 2), acc, out, stage, sems)
 
 
 def per_device(kernels, counts, volume, tables, pair_offset, pair_table):
@@ -268,27 +270,30 @@
         cost_estimate=cost(1 << 20, 4 << 20),
         name="keep",
     )(kernels, counts, pair_offset, pair_table)
-    first, second = pl.pallas_call(
-        source_kernel,
-        out_shape=[on_chip((HALF, ROWS, W), bf16)] * 2,
-        in_specs=[VMEM] * 4,
-        out_specs=[VMEM] * 2,
-        compiler_params=params(6),
-        cost_estimate=cost(1 << 20, 4 << 20),
-        name="source",
-    )(own, in_vmem(got), volume, adj)
+
+    def source(leaves_first):
+        return pl.pallas_call(
+            functools.partial(source_kernel, leaves_first),
+            out_shape=on_chip((HALF, ROWS, W), bf16),
+            in_specs=[VMEM] * 4,
+            out_specs=VMEM,
+            compiler_params=params(6),
+            cost_estimate=cost(1 << 20, 2 << 20),
+        )(own, in_vmem(got), volume, adj)
 
     count = lax.axis_size("dom")
 
     def swapped(value, start):
         pairs = [(a, a + 1) for a in range(start, count - 1, 2)]
         pairs = pairs + [(b, a) for a, b in pairs]
-        return lax.ppermute(value, "dom", pairs)
-
+        return in_vmem(lax.ppermute(value, "dom", pairs))
+
+    first = source(True)
+    b0 = swapped(first, 1)
+    second = source(False)
     a0 = swapped(second, 0)
-    b0 = swapped(first, 1)
+    b1 = swapped(second, 1)
     a1 = swapped(first, 0)
-    b1 = swapped(second, 1)
 
     acc_shape = on_chip((OWN + 1, ROWS, W), f32)
     out_shape = jax.ShapeDtypeStruct((1, G, OWN, W), bf16)
@@ -321,9 +326,9 @@
         compiler_params=params(6),
         cost_estimate=cost(192 * term, 12 << 20),
         name="chunk_terms",
-    )(in_vmem(b0), in_vmem(a0), tables, acc)
+    )(b0, a0, tables, acc)
     out, acc = pl.pallas_call(
-        last_a_kernel,
+        last_b_kernel,
         out_shape=[out_shape, acc_shape],
         in_specs=[VMEM] * 4,
         out_specs=[HBM, VMEM],
@@ -331,10 +336,10 @@
         input_output_aliases={3: 1},
         compiler_params=params(6),
         cost_estimate=cost(32 * term, 2 << 20),
-        name="last_a",
-    )(in_vmem(a1), lists_a, tables, acc)
+        name="last_b",
+    )(b1, lists_b, tables, acc)
     out, _ = pl.pallas_call(
-        last_b_kernel,
+        last_a_kernel,
         out_shape=[out_shape, acc_shape],
         in_specs=[VMEM] * 4 + [HBM],
         out_specs=[HBM, VMEM],
@@ -342,8 +347,8 @@
         input_output_aliases={3: 1, 4: 0},
         compiler_params=params(6),
         cost_estimate=cost(32 * term, 2 << 20),
-        name="last_b",
-    )(in_vmem(b1), lists_b, tables, acc, out)
+        name="last_a",
+    )(a1, lists_a, tables, acc, out)
     return jnp.transpose(out, (0, 2, 1, 3))
 
 

time: 45.5 us -> 44.7 us (0.982)
  the two profiles are of different devices: /device:TPU:256 before, /device:TPU:254 now
where the time goes in v5:
time: 44.7 us; the launch traced here: 44.4 us
  Pallas kernels  21.4 us (48%)
  starting transfers between devices  17 us (38%)
  waiting for transfers between devices  5.78 us (13%)
    ppermute x4, starting transfers between devices, swapped(): return in_vmem(lax.ppermute(value, 'dom', pairs))  15.1 us
    pallas_call x1, Pallas kernels, per_device(): pl.pallas_call(own_kernel, out_shape=acc_shape, in_specs=[VMEM] * 3, out_...  7.01 us
    pallas_call x1, Pallas kernels, per_device(): pl.pallas_call(chunk_kernel, out_shape=[acc_shape] + [on_chip(lists(HALF)...  5.13 us
    ppermute x4, waiting for transfers between devices, swapped(): return in_vmem(lax.ppermute(value, 'dom', pairs))  4.83 us
    pallas_call x1, Pallas kernels, per_device(): pl.pallas_call(last_a_kernel, out_shape=[out_shape, acc_shape], in_specs=...  2.63 us
    pallas_call x1, Pallas kernels, per_device(): pl.pallas_call(last_b_kernel, out_shape=[out_shape, acc_shape], in_specs=...  2.63 us
    ppermute x1, starting transfers between devices, per_device(): got = lax.ppermute(to_other, 'event', [(0, 1), (1, 0)])  1.92 us
    pallas_call x1, Pallas kernels, per_device(): pl.pallas_call(send_kernel, out_shape=sums, in_specs=[HBM, HBM], out_spec...  1.64 us
  transfers between devices with their start and end apart: 5, of which 2 were waited for; matrix products, arithmetic and copies ran while one was open for 0% of the time, Pallas kernels for 38%

profile of v5, /device:TPU:254, one launch (start us, length us, event | category | flops | bytes accessed | tf_op | source)
XLA Modules:
  0.0 44.4 jit_solution(692394558365373075)
XLA Ops:
  0.0 0.0 copy-start.2
  0.0 0.0 copy-start.3
  0.0 1.6 %send.1 = bf16[126,32,128]{2,1,0:T(8,128)(2,1)S(1)} custom-call(bf16[2,1,125,64,128]{4,3,2,1,0:T(8,128)(2,1)} %bitcast.6, s32[2,1,64,128]{3,2,1,0:T(8,128)} %counts.3), custom_call_target="tpu_custom_call" | custom-call | flops 1048576 | bytes 4194304 | tf_op jit(solution)/shard_map/send/pallas_call | solution.py:252
  1.7 0.0 copy-start.1
  1.7 1.9 %collective-permute-start = (bf16[126,32,128]{2,1,0:T(8,128)(2,1)S(1)}, bf16[126,32,128]{2,1,0:T(8,128)(2,1)S(1)}, u32[]{:S(2)}, u32[]{:S(2)}) collective-permute-start(bf16[126,32,128]{2,1,0:T(8,128)(2,1)S(1)} %send.1), channel_id=1, source_target_pairs={{0,256},{256,0},{1,257},{257,1},{2,258},{258,2},{3,259},{259,3},{4... | collective-permute-start | bytes 3096584 | tf_op jit(solution)/shard_map/ppermute | solution.py:262
  3.6 0.0 copy-done.2
  3.6 0.0 copy-done.3
  3.6 1.6 %keep.1 = (bf16[126,32,128]{2,1,0:T(8,128)(2,1)S(1)}, f32[32,128]{1,0:T(8,128)S(1)}) custom-call(bf16[2,1,125,64,128]{4,3,2,1,0:T(8,128)(2,1)} %bitcast.7, s32[2,1,64,128]{3,2,1,0:T(8,128)} %counts.3, s32[1,1,16,32]{3,2,1,0:T(8,128)S(1)} %bitcast.4, s32[1,1,16,32]{3,2,1,0:T(8,128)S(1)} %bitcast.5), custom_call_target="tpu_custom_call" | custom-call | flops 1048576 | bytes 4194304 | tf_op jit(solution)/shard_map/keep/pallas_call | solution.py:263
  5.3 0.9 %collective-permute-done.got = bf16[126,32,128]{2,1,0:T(8,128)(2,1)S(1)} collective-permute-done((bf16[126,32,128]{2,1,0:T(8,128)(2,1)S(1)}, bf16[126,32,128]{2,1,0:T(8,128)(2,1)S(1)}, u32[]{:S(2)}, u32[]{:S(2)}) %collective-permute-start) | collective-permute-done | bytes 1032224 | tf_op jit(solution)/shard_map/ppermute | solution.py:262
  6.2 0.0 copy-done.1
  6.2 0.0 copy-start
  6.2 0.3 shard_map.64.first
  6.6 4.6 %collective-permute-start.2 = (bf16[16,128,128]{2,1,0:T(8,128)(2,1)S(1)}, bf16[16,128,128]{2,1,0:T(8,128)(2,1)S(1)}, u32[]{:S(2)}, u32[]{:S(2)}) collective-permute-start(bf16[16,128,128]{2,1,0:T(8,128)(2,1)S(1)} %shard_map.64.first), channel_id=1, source_target_pairs={{1,2},{3,4},{5,6},{7,8},{9,10},{11,12},{13,14},{15,16},{17,18},{19... | collective-permute-start | bytes 1572872 | tf_op jit(solution)/shard_map/ppermute | solution.py:289
  11.2 0.4 shard_map.65.second
  11.5 1.9 %collective-permute-start.3 = (bf16[16,128,128]{2,1,0:T(8,128)(2,1)S(1)}, bf16[16,128,128]{2,1,0:T(8,128)(2,1)S(1)}, u32[]{:S(2)}, u32[]{:S(2)}) collective-permute-start(bf16[16,128,128]{2,1,0:T(8,128)(2,1)S(1)} %shard_map.65.second), channel_id=1, source_target_pairs={{0,1},{2,3},{4,5},{6,7},{8,9},{10,11},{12,13},{14,15},{16,17},{18,... | collective-permute-start | bytes 1572872 | tf_op jit(solution)/shard_map/ppermute | solution.py:289
  13.5 6.7 %collective-permute-start.4 = (bf16[16,128,128]{2,1,0:T(8,128)(2,1)S(1)}, bf16[16,128,128]{2,1,0:T(8,128)(2,1)S(1)}, u32[]{:S(2)}, u32[]{:S(2)}) collective-permute-start(bf16[16,128,128]{2,1,0:T(8,128)(2,1)S(1)} %shard_map.65.second), channel_id=1, source_target_pairs={{1,2},{3,4},{5,6},{7,8},{9,10},{11,12},{13,14},{15,16},{17,18},{19... | collective-permute-start | bytes 1572872 | tf_op jit(solution)/shard_map/ppermute | solution.py:289
  20.1 1.9 %collective-permute-start.1 = (bf16[16,128,128]{2,1,0:T(8,128)(2,1)S(1)}, bf16[16,128,128]{2,1,0:T(8,128)(2,1)S(1)}, u32[]{:S(2)}, u32[]{:S(2)}) collective-permute-start(bf16[16,128,128]{2,1,0:T(8,128)(2,1)S(1)} %shard_map.64.first), channel_id=1, source_target_pairs={{0,1},{2,3},{4,5},{6,7},{8,9},{10,11},{12,13},{14,15},{16,17},{18,... | collective-permute-start | bytes 1572872 | tf_op jit(solution)/shard_map/ppermute | solution.py:289
  22.1 0.0 copy-done
  22.1 7.0 %own_terms.1.acc_in = f32[33,128,128]{2,1,0:T(8,128)S(1)} custom-call(bf16[16,128,128]{2,1,0:T(8,128)(2,1)S(1)} %shard_map.64.first, bf16[16,128,128]{2,1,0:T(8,128)(2,1)S(1)} %shard_map.65.second, bf16[32,128,128]{2,1,0:T(8,128)(2,1)S(1)} %copy-done), custom_call_target="tpu_custom_call" | custom-call | flops 1073741824 | bytes 16777216 | tf_op jit(solution)/shard_map/own_terms/pallas_call | solution.py:309
  29.1 0.0 collective-permute-done.2.from_b
  29.1 0.0 collective-permute-done.3.from_a
  29.1 5.1 %chunk_terms.1 = (f32[33,128,128]{2,1,0:T(8,128)S(1)}, s32[24,128]{1,0:T(8,128)S(1)}, s32[24,128]{1,0:T(8,128)S(1)}) custom-call(bf16[16,128,128]{2,1,0:T(8,128)(2,1)S(1)} %collective-permute-done.2.from_b, bf16[16,128,128]{2,1,0:T(8,128)(2,1)S(1)} %collective-permute-done.3.from_a, ...), custom_call_target="tpu_custom_call", output_to_operand_aliasing={{0}: (3, {})} | custom-call | flops 805306368 | bytes 12582912 | tf_op jit(solution)/shard_map/chunk_terms/pallas_call | solution.py:319
  34.2 4.8 %collective-permute-done.4.from_b = bf16[16,128,128]{2,1,0:T(8,128)(2,1)S(1)} collective-permute-done((bf16[16,128,128]{2,1,0:T(8,128)(2,1)S(1)}, bf16[16,128,128]{2,1,0:T(8,128)(2,1)S(1)}, u32[]{:S(2)}, u32[]{:S(2)}) %collective-permute-start.4) | collective-permute-done | bytes 524320 | tf_op jit(solution)/shard_map/ppermute | solution.py:289
  39.1 2.6 %last_b.1 = (bf16[1,125,32,128]{3,2,1,0:T(8,128)(2,1)}, f32[33,128,128]{2,1,0:T(8,128)S(1)}) custom-call(bf16[16,128,128]{2,1,0:T(8,128)(2,1)S(1)} %collective-permute-done.4.from_b, s32[24,128]{1,0:T(8,128)S(1)} %get-tuple-element.16.lists, bf16[32,128,128]{2,1,0:T(8,128)(2,1)S(1)} %copy-done, ...), custom_call_target="tpu_custom_call", output_to_operand_aliasing={{1}: (3, {})} | custom-call | flops 134217728 | bytes 2097152 | tf_op jit(solution)/shard_map/last_b/pallas_call | solution.py:330
  41.7 0.0 collective-permute-done.1.from_a
  41.7 2.6 %last_a.1 = (bf16[1,125,32,128]{3,2,1,0:T(8,128)(2,1)}, f32[33,128,128]{2,1,0:T(8,128)S(1)}) custom-call(bf16[16,128,128]{2,1,0:T(8,128)(2,1)S(1)} %collective-permute-done.1.from_a, s32[24,128]{1,0:T(8,128)S(1)} %get-tuple-element.15.lists, bf16[32,128,128]{2,1,0:T(8,128)(2,1)S(1)} %copy-done, ...), custom_call_target="tpu_custom_call", output_to_operand_aliasing={{1}: (3, {}), {0}: (4, {})} | custom-call | flops 134217728 | bytes 2097152 | tf_op jit(solution)/shard_map/last_a/pallas_call | solution.py:341
Async XLA Ops:
  0.0 3.6 %copy-start.2 = (s32[1,1,32,16]{2,3,1,0:T(8,128)S(1)}, s32[1,1,32,16]{2,3,1,0:T(8,128)}, u32[]{:S(2)}) copy-start(s32[1,1,32,16]{2,3,1,0:T(8,128)} %param.10) | copy-start | bytes 6148
  0.0 3.6 %copy-start.3 = (s32[1,1,32,16]{2,3,1,0:T(8,128)S(1)}, s32[1,1,32,16]{2,3,1,0:T(8,128)}, u32[]{:S(2)}) copy-start(s32[1,1,32,16]{2,3,1,0:T(8,128)} %param.11) | copy-start | bytes 6148
  1.7 4.5 %copy-start.1 = (bf16[1,32,128]{2,1,0:T(8,128)(2,1)S(1)}, bf16[1,32,128]{2,1,0:T(8,128)(2,1)}, u32[]{:S(2)}) copy-start(bf16[1,32,128]{2,1,0:T(8,128)(2,1)} %vol.3) | copy-start | bytes 24580
  1.7 4.5 %collective-permute-start = (bf16[126,32,128]{2,1,0:T(8,128)(2,1)S(1)}, bf16[126,32,128]{2,1,0:T(8,128)(2,1)S(1)}, u32[]{:S(2)}, u32[]{:S(2)}) collective-permute-start(bf16[126,32,128]{2,1,0:T(8,128)(2,1)S(1)} %send.1), channel_id=1, source_target_pairs={{0,256},{256,0},{1,257},{257,1},{2,258},{258,2},{3,259},{259,3},{4... | collective-permute-start | bytes 3096584 | tf_op jit(solution)/shard_map/ppermute | solution.py:262
  6.2 15.9 %copy-start = (bf16[32,128,128]{2,1,0:T(8,128)(2,1)S(1)}, bf16[32,128,128]{2,1,0:T(8,128)(2,1)}, u32[]{:S(2)}) copy-start(bf16[32,128,128]{2,1,0:T(8,128)(2,1)} %tables.7) | copy-start | bytes 3145732
  6.6 22.5 %collective-permute-start.2 = (bf16[16,128,128]{2,1,0:T(8,128)(2,1)S(1)}, bf16[16,128,128]{2,1,0:T(8,128)(2,1)S(1)}, u32[]{:S(2)}, u32[]{:S(2)}) collective-permute-start(bf16[16,128,128]{2,1,0:T(8,128)(2,1)S(1)} %shard_map.64.first), channel_id=1, source_target_pairs={{1,2},{3,4},{5,6},{7,8},{9,10},{11,12},{13,14},{15,16},{17,18},{19... | collective-permute-start | bytes 1572872 | tf_op jit(solution)/shard_map/ppermute | solution.py:289
  11.5 17.6 %collective-permute-start.3 = (bf16[16,128,128]{2,1,0:T(8,128)(2,1)S(1)}, bf16[16,128,128]{2,1,0:T(8,128)(2,1)S(1)}, u32[]{:S(2)}, u32[]{:S(2)}) collective-permute-start(bf16[16,128,128]{2,1,0:T(8,128)(2,1)S(1)} %shard_map.65.second), channel_id=1, source_target_pairs={{0,1},{2,3},{4,5},{6,7},{8,9},{10,11},{12,13},{14,15},{16,17},{18,... | collective-permute-start | bytes 1572872 | tf_op jit(solution)/shard_map/ppermute | solution.py:289
  13.5 25.6 %collective-permute-start.4 = (bf16[16,128,128]{2,1,0:T(8,128)(2,1)S(1)}, bf16[16,128,128]{2,1,0:T(8,128)(2,1)S(1)}, u32[]{:S(2)}, u32[]{:S(2)}) collective-permute-start(bf16[16,128,128]{2,1,0:T(8,128)(2,1)S(1)} %shard_map.65.second), channel_id=1, source_target_pairs={{1,2},{3,4},{5,6},{7,8},{9,10},{11,12},{13,14},{15,16},{17,18},{19... | collective-permute-start | bytes 1572872 | tf_op jit(solution)/shard_map/ppermute | solution.py:289
  20.1 21.6 %collective-permute-start.1 = (bf16[16,128,128]{2,1,0:T(8,128)(2,1)S(1)}, bf16[16,128,128]{2,1,0:T(8,128)(2,1)S(1)}, u32[]{:S(2)}, u32[]{:S(2)}) collective-permute-start(bf16[16,128,128]{2,1,0:T(8,128)(2,1)S(1)} %shard_map.64.first), channel_id=1, source_target_pairs={{0,1},{2,3},{4,5},{6,7},{8,9},{10,11},{12,13},{14,15},{16,17},{18,... | collective-permute-start | bytes 1572872 | tf_op jit(solution)/shard_map/ppermute | solution.py:289

commit v6 on v5

--- a/solution.py
+++ b/solution.py
@@ -1,5 +1,3 @@
-import functools
-
 import jax
 import jax.numpy as jnp
 from jax import lax
@@ -10,6 +8,8 @@
 
 OWN = 32
 HALF = OWN // 2
+REST = 8
+BIG = OWN - REST
 G = 125
 ADJ = G + 1
 ROWS = 128
@@ -94,23 +94,38 @@
         turned = turned + jnp.where(spot == lane[k : k + 1], value[k : k + 1], 0.0)
     wide = jnp.concatenate([turned, jnp.zeros((OWN, OWN), jnp.float32)], axis=0)
     wide = jnp.concatenate([wide, jnp.zeros((W, W - OWN), jnp.float32)], axis=1)
-    adj[...] = jnp.transpose(wide, (1, 0))[0:OWN]
+    adj[0:OWN] = jnp.transpose(wide, (1, 0))[0:OWN]
+    adj[OWN : 2 * OWN] = jnp.zeros((OWN, W), jnp.float32)
+    adj[OWN + REST : OWN + 2 * REST] = adj[BIG:OWN]
+    adj[OWN + 2 * REST : OWN + 3 * REST] = adj[0:REST]
     for _ in steps:
         pass
 
 
-def source_kernel(leaves_first, own, got, vol, adj, dst):
-    odd = lax.rem(lax.axis_index("dom"), 2)
-    half = odd if leaves_first else 1 - odd
+def weighted_half(half, other, own, got, vol, adj):
     span = pl.ds(pl.multiple_of(half * HALF, HALF), HALF)
-    rest = pl.ds(pl.multiple_of((1 - half) * HALF, HALF), HALF)
     v = vol[0, span].astype(jnp.float32)
     hits = own[G, span].astype(jnp.float32) + got[G, span].astype(jnp.float32)
     factor = v / jnp.sqrt(1.0 + hits)
     total = own[0:G, span].astype(jnp.float32) + got[0:G, span].astype(jnp.float32)
-    rows = [total * factor[None], v[None], adj[span][None], adj[rest][None]]
+    second = adj[pl.ds(pl.multiple_of(other, HALF), HALF)]
+    rows = [total * factor[None], v[None], adj[span][None], second[None]]
     block = jnp.concatenate(rows, axis=0)
-    dst[...] = jnp.transpose(block, (1, 0, 2)).astype(jnp.bfloat16)
+    return jnp.transpose(block, (1, 0, 2)).astype(jnp.bfloat16)
+
+
+def source_b_kernel(own, got, vol, adj, b0):
+    odd = lax.rem(lax.axis_index("dom"), 2)
+    b0[...] = weighted_half(odd, (1 - odd) * HALF, own, got, vol, adj)
+
+
+def source_a_kernel(own, got, vol, adj, b0, b1, a0, a1):
+    odd = lax.rem(lax.axis_index("dom"), 2)
+    half = weighted_half(1 - odd, OWN + (1 - odd) * HALF, own, got, vol, adj)
+    b1[...] = half
+    a0[pl.ds((1 - odd) * REST, HALF)] = half
+    a0[pl.ds(odd * HALF, REST)] = b0[pl.ds((1 - odd) * REST, REST)]
+    a1[...] = b0[pl.ds(odd * REST, REST)]
 
 
 def neighbours(ref, row, lane):
@@ -158,12 +173,14 @@
 
 
 def add_terms(blocks, lists, tables, acc, mats, codes, sem):
-    n = HALF * len(blocks)
+    n = codes.shape[0] - 8
     copy = pltpu.make_async_copy(lists, codes, sem)
     copy.start()
     mats[0] = jnp.zeros((ROWS, W), jnp.bfloat16)
-    for i, ref in enumerate(blocks):
-        mats[1 + i * HALF : 1 + (i + 1) * HALF] = ref[...]
+    at = 1
+    for ref in blocks:
+        mats[at : at + ref.shape[0]] = ref[...]
+        at += ref.shape[0]
     copy.wait()
 
     def step(i, carry):
@@ -195,14 +212,20 @@
     add_terms((first, second), lists, tables, acc, *scratch)
 
 
-def chunk_kernel(from_b, from_a, tables, acc_in, acc, lists_a, lists_b, lists, *scratch):
+def first_b_kernel(b0, tables, acc_in, acc, lists_b, lists, *scratch):
     if COPY_ALIASED:
         acc[...] = acc_in[...]
-    adj = [neighbours(from_b, ADJ, 0), neighbours(from_a, ADJ, OWN)]
-    make_lists(jnp.concatenate(adj, axis=0), lists)
-    make_lists(neighbours(from_a, ADJ + 1, OWN), lists_a)
-    make_lists(neighbours(from_b, ADJ + 1, 0), lists_b)
-    add_terms((from_b, from_a), lists, tables, acc, *scratch)
+    make_lists(neighbours(b0, ADJ, 0), lists)
+    make_lists(neighbours(b0, ADJ + 1, 0), lists_b)
+    add_terms((b0,), lists, tables, acc, *scratch)
+
+
+def first_a_kernel(a0, tables, acc_in, acc, lists_a, lists, *scratch):
+    if COPY_ALIASED:
+        acc[...] = acc_in[...]
+    make_lists(neighbours(a0, ADJ, OWN), lists)
+    make_lists(neighbours(a0, ADJ + 1, OWN)[REST : 2 * REST], lists_a)
+    add_terms((a0,), lists, tables, acc, *scratch)
 
 
 def finish(half, acc, out, stage, sems):
@@ -262,7 +285,7 @@
     got = lax.ppermute(to_other, "event", [(0, 1), (1, 0)])
     own, adj = pl.pallas_call(
         keep_kernel,
-        out_shape=[sums, on_chip((OWN, W), f32)],
+        out_shape=[sums, on_chip((2 * OWN, W), f32)],
         in_specs=[HBM, HBM, VMEM, VMEM],
         out_specs=[VMEM, VMEM],
         scratch_shapes=scratch,
@@ -271,15 +294,8 @@
         name="keep",
     )(kernels, counts, pair_offset, pair_table)
 
-    def source(leaves_first):
-        return pl.pallas_call(
-            functools.partial(source_kernel, leaves_first),
-            out_shape=on_chip((HALF, ROWS, W), bf16),
-            in_specs=[VMEM] * 4,
-            out_specs=VMEM,
-            compiler_params=params(6),
-            cost_estimate=cost(1 << 20, 2 << 20),
-        )(own, in_vmem(got), volume, adj)
+    def blocks(n):
+        return on_chip((n, ROWS, W), bf16)
 
     count = lax.axis_size("dom")
 
@@ -288,12 +304,28 @@
         pairs = pairs + [(b, a) for a, b in pairs]
         return in_vmem(lax.ppermute(value, "dom", pairs))
 
-    first = source(True)
+    first = pl.pallas_call(
+        source_b_kernel,
+        out_shape=blocks(HALF),
+        in_specs=[VMEM] * 4,
+        out_specs=VMEM,
+        compiler_params=params(6),
+        cost_estimate=cost(1 << 20, 2 << 20),
+        name="source_b",
+    )(own, in_vmem(got), volume, adj)
     b0 = swapped(first, 1)
-    second = source(False)
-    a0 = swapped(second, 0)
+    second, to_a, rest = pl.pallas_call(
+        source_a_kernel,
+        out_shape=[blocks(HALF), blocks(BIG), blocks(REST)],
+        in_specs=[VMEM] * 5,
+        out_specs=[VMEM] * 3,
+        compiler_params=params(6),
+        cost_estimate=cost(1 << 20, 2 << 20),
+        name="source_a",
+    )(own, in_vmem(got), volume, adj, first)
+    a0 = swapped(to_a, 0)
     b1 = swapped(second, 1)
-    a1 = swapped(first, 0)
+    a1 = swapped(rest, 0)
 
     acc_shape = on_chip((OWN + 1, ROWS, W), f32)
     out_shape = jax.ShapeDtypeStruct((1, G, OWN, W), bf16)
@@ -316,17 +348,21 @@
         cost_estimate=cost(256 * term, 16 << 20),
         name="own_terms",
     )(first, second, tables)
-    acc, lists_a, lists_b = pl.pallas_call(
-        chunk_kernel,
-        out_shape=[acc_shape] + [on_chip(lists(HALF), i32)] * 2,
-        in_specs=[VMEM] * 4,
-        out_specs=[VMEM] * 3,
-        scratch_shapes=[pltpu.VMEM(lists(OWN), i32)] + work(OWN),
-        input_output_aliases={3: 0},
-        compiler_params=params(6),
-        cost_estimate=cost(192 * term, 12 << 20),
-        name="chunk_terms",
-    )(b0, a0, tables, acc)
+
+    def first_terms(kernel, value, acc, n, second):
+        return pl.pallas_call(
+            kernel,
+            out_shape=[acc_shape, on_chip(lists(second), i32)],
+            in_specs=[VMEM] * 3,
+            out_specs=[VMEM] * 2,
+            scratch_shapes=[pltpu.VMEM(lists(n), i32)] + work(n),
+            input_output_aliases={2: 0},
+            compiler_params=params(6),
+            cost_estimate=cost(96 * term, 6 << 20),
+        )(value, tables, acc)
+
+    acc, lists_b = first_terms(first_b_kernel, b0, acc, HALF, HALF)
+    acc, lists_a = first_terms(first_a_kernel, a0, acc, BIG, REST)
     out, acc = pl.pallas_call(
         last_b_kernel,
         out_shape=[out_shape, acc_shape],
@@ -343,7 +379,7 @@
         out_shape=[out_shape, acc_shape],
         in_specs=[VMEM] * 4 + [HBM],
         out_specs=[HBM, VMEM],
-        scratch_shapes=stage + work(HALF),
+        scratch_shapes=stage + work(REST),
         input_output_aliases={3: 1, 4: 0},
         compiler_params=params(6),
         cost_estimate=cost(32 * term, 2 << 20),

time: 44.7 us -> 47.5 us (1.063)
  the two profiles are of different devices: /device:TPU:254 before, /device:TPU:256 now
where the time goes in v6:
time: 47.5 us; the launch traced here: 47.2 us
  Pallas kernels  22.9 us (48%)
  starting transfers between devices  18.5 us (39%)
  waiting for transfers between devices  5.67 us (12%)
    ppermute x4, starting transfers between devices, swapped(): return in_vmem(lax.ppermute(value, 'dom', pairs))  16.6 us
    pallas_call x2, Pallas kernels, first_terms(): pl.pallas_call(kernel, out_shape=[acc_shape, on_chip(lists(second), i32)]...  7.24 us
    pallas_call x1, Pallas kernels, per_device(): pl.pallas_call(own_kernel, out_shape=acc_shape, in_specs=[VMEM] * 3, out_...  7.01 us
    ppermute x4, waiting for transfers between devices, swapped(): return in_vmem(lax.ppermute(value, 'dom', pairs))  4.72 us
    pallas_call x1, Pallas kernels, per_device(): pl.pallas_call(last_b_kernel, out_shape=[out_shape, acc_shape], in_specs=...  2.63 us
    pallas_call x1, Pallas kernels, per_device(): pl.pallas_call(last_a_kernel, out_shape=[out_shape, acc_shape], in_specs=...  1.96 us
    ppermute x1, starting transfers between devices, per_device(): got = lax.ppermute(to_other, 'event', [(0, 1), (1, 0)])  1.92 us
    pallas_call x1, Pallas kernels, per_device(): pl.pallas_call(send_kernel, out_shape=sums, in_specs=[HBM, HBM], out_spec...  1.64 us
  transfers between devices with their start and end apart: 5, of which 3 were waited for; matrix products, arithmetic and copies ran while one was open for 0% of the time, Pallas kernels for 39%

profile of v6, /device:TPU:256, one launch (start us, length us, event | category | flops | bytes accessed | tf_op | source)
XLA Modules:
  0.0 47.2 jit_solution(18328053329414533694)
XLA Ops:
  0.0 0.0 copy-start.2
  0.0 0.0 copy-start.3
  0.0 1.6 %send.1 = bf16[126,32,128]{2,1,0:T(8,128)(2,1)S(1)} custom-call(bf16[2,1,125,64,128]{4,3,2,1,0:T(8,128)(2,1)} %bitcast.6, s32[2,1,64,128]{3,2,1,0:T(8,128)} %counts.3), custom_call_target="tpu_custom_call" | custom-call | flops 1048576 | bytes 4194304 | tf_op jit(solution)/shard_map/send/pallas_call | solution.py:275
  1.7 0.0 copy-start.1
  1.7 1.9 %collective-permute-start = (bf16[126,32,128]{2,1,0:T(8,128)(2,1)S(1)}, bf16[126,32,128]{2,1,0:T(8,128)(2,1)S(1)}, u32[]{:S(2)}, u32[]{:S(2)}) collective-permute-start(bf16[126,32,128]{2,1,0:T(8,128)(2,1)S(1)} %send.1), channel_id=1, source_target_pairs={{0,256},{256,0},{1,257},{257,1},{2,258},{258,2},{3,259},{259,3},{4... | collective-permute-start | bytes 3096584 | tf_op jit(solution)/shard_map/ppermute | solution.py:285
  3.6 0.0 copy-done.2
  3.6 0.0 copy-done.3
  3.6 1.6 %keep.1 = (bf16[126,32,128]{2,1,0:T(8,128)(2,1)S(1)}, f32[64,128]{1,0:T(8,128)S(1)}) custom-call(bf16[2,1,125,64,128]{4,3,2,1,0:T(8,128)(2,1)} %bitcast.7, s32[2,1,64,128]{3,2,1,0:T(8,128)} %counts.3, s32[1,1,16,32]{3,2,1,0:T(8,128)S(1)} %bitcast.4, s32[1,1,16,32]{3,2,1,0:T(8,128)S(1)} %bitcast.5), custom_call_target="tpu_custom_call" | custom-call | flops 1048576 | bytes 4194304 | tf_op jit(solution)/shard_map/keep/pallas_call | solution.py:286
  5.3 0.9 %collective-permute-done.got = bf16[126,32,128]{2,1,0:T(8,128)(2,1)S(1)} collective-permute-done((bf16[126,32,128]{2,1,0:T(8,128)(2,1)S(1)}, bf16[126,32,128]{2,1,0:T(8,128)(2,1)S(1)}, u32[]{:S(2)}, u32[]{:S(2)}) %collective-permute-start) | collective-permute-done | bytes 1032224 | tf_op jit(solution)/shard_map/ppermute | solution.py:285
  6.2 0.0 copy-done.1
  6.2 0.0 copy-start
  6.2 0.3 source_b.1.b0.first
  6.6 0.4 source_a.1
  7.0 3.4 %collective-permute-start.2 = (bf16[24,128,128]{2,1,0:T(8,128)(2,1)S(1)}, bf16[24,128,128]{2,1,0:T(8,128)(2,1)S(1)}, u32[]{:S(2)}, u32[]{:S(2)}) collective-permute-start(bf16[24,128,128]{2,1,0:T(8,128)(2,1)S(1)} %get-tuple-element.20), channel_id=1, source_target_pairs={{0,1},{2,3},{4,5},{6,7},{8,9},{10,11},{12,13},{14,15},{16,17},{18,... | collective-permute-start | bytes 2359304 | tf_op jit(solution)/shard_map/ppermute | solution.py:305
  10.4 6.0 %collective-permute-start.3 = (bf16[16,128,128]{2,1,0:T(8,128)(2,1)S(1)}, bf16[16,128,128]{2,1,0:T(8,128)(2,1)S(1)}, u32[]{:S(2)}, u32[]{:S(2)}) collective-permute-start(bf16[16,128,128]{2,1,0:T(8,128)(2,1)S(1)} %source_b.1.b0.first), channel_id=1, source_target_pairs={{1,2},{3,4},{5,6},{7,8},{9,10},{11,12},{13,14},{15,16},{17,18},{19... | collective-permute-start | bytes 1572872 | tf_op jit(solution)/shard_map/ppermute | solution.py:305
  16.4 5.3 %collective-permute-start.4 = (bf16[16,128,128]{2,1,0:T(8,128)(2,1)S(1)}, bf16[16,128,128]{2,1,0:T(8,128)(2,1)S(1)}, u32[]{:S(2)}, u32[]{:S(2)}) collective-permute-start(bf16[16,128,128]{2,1,0:T(8,128)(2,1)S(1)} %get-tuple-element.21.second), channel_id=1, source_target_pairs={{1,2},{3,4},{5,6},{7,8},{9,10},{11,12},{13,14},{15,16},{17,18},{19... | collective-permute-start | bytes 1572872 | tf_op jit(solution)/shard_map/ppermute | solution.py:305
  21.7 1.9 %collective-permute-start.1 = (bf16[8,128,128]{2,1,0:T(8,128)(2,1)S(1)}, bf16[8,128,128]{2,1,0:T(8,128)(2,1)S(1)}, u32[]{:S(2)}, u32[]{:S(2)}) collective-permute-start(bf16[8,128,128]{2,1,0:T(8,128)(2,1)S(1)} %get-tuple-element.19), channel_id=1, source_target_pairs={{0,1},{2,3},{4,5},{6,7},{8,9},{10,11},{12,13},{14,15},{16,17},{18,... | collective-permute-start | bytes 786440 | tf_op jit(solution)/shard_map/ppermute | solution.py:305
  23.6 0.0 copy-done
  23.6 7.0 %own_terms.1.acc_in = f32[33,128,128]{2,1,0:T(8,128)S(1)} custom-call(bf16[16,128,128]{2,1,0:T(8,128)(2,1)S(1)} %source_b.1.b0.first, bf16[16,128,128]{2,1,0:T(8,128)(2,1)S(1)} %get-tuple-element.21.second, bf16[32,128,128]{2,1,0:T(8,128)(2,1)S(1)} %copy-done), custom_call_target="tpu_custom_call" | custom-call | flops 1073741824 | bytes 16777216 | tf_op jit(solution)/shard_map/own_terms/pallas_call | solution.py:341
  30.6 1.9 %collective-permute-done.3.b0 = bf16[16,128,128]{2,1,0:T(8,128)(2,1)S(1)} collective-permute-done((bf16[16,128,128]{2,1,0:T(8,128)(2,1)S(1)}, bf16[16,128,128]{2,1,0:T(8,128)(2,1)S(1)}, u32[]{:S(2)}, u32[]{:S(2)}) %collective-permute-start.3) | collective-permute-done | bytes 524320 | tf_op jit(solution)/shard_map/ppermute | solution.py:305
  32.5 3.6 %shard_map.64 = (f32[33,128,128]{2,1,0:T(8,128)S(1)}, s32[24,128]{1,0:T(8,128)S(1)}) custom-call(bf16[16,128,128]{2,1,0:T(8,128)(2,1)S(1)} %collective-permute-done.3.b0, bf16[32,128,128]{2,1,0:T(8,128)(2,1)S(1)} %copy-done, f32[33,128,128]{2,1,0:T(8,128)S(1)} %own_terms.1.acc_in), custom_call_target="tpu_custom_call", output_to_operand_aliasing={{0}: (2, {})} | custom-call | flops 402653184 | bytes 6291456 | tf_op jit(solution)/shard_map/pallas_call | solution.py:353
  36.1 0.0 collective-permute-done.2.a0
  36.1 3.7 %shard_map.65 = (f32[33,128,128]{2,1,0:T(8,128)S(1)}, s32[16,128]{1,0:T(8,128)S(1)}) custom-call(bf16[24,128,128]{2,1,0:T(8,128)(2,1)S(1)} %collective-permute-done.2.a0, bf16[32,128,128]{2,1,0:T(8,128)(2,1)S(1)} %copy-done, f32[33,128,128]{2,1,0:T(8,128)S(1)} %get-tuple-element.22.acc_in), custom_call_target="tpu_custom_call", output_to_operand_aliasing={{0}: (2, {})} | custom-call | flops 402653184 | bytes 6291456 | tf_op jit(solution)/shard_map/pallas_call | solution.py:353
  39.8 2.8 %collective-permute-done.4.from_b = bf16[16,128,128]{2,1,0:T(8,128)(2,1)S(1)} collective-permute-done((bf16[16,128,128]{2,1,0:T(8,128)(2,1)S(1)}, bf16[16,128,128]{2,1,0:T(8,128)(2,1)S(1)}, u32[]{:S(2)}, u32[]{:S(2)}) %collective-permute-start.4) | collective-permute-done | bytes 524320 | tf_op jit(solution)/shard_map/ppermute | solution.py:305
  42.6 2.6 %last_b.1 = (bf16[1,125,32,128]{3,2,1,0:T(8,128)(2,1)}, f32[33,128,128]{2,1,0:T(8,128)S(1)}) custom-call(bf16[16,128,128]{2,1,0:T(8,128)(2,1)S(1)} %collective-permute-done.4.from_b, s32[24,128]{1,0:T(8,128)S(1)} %get-tuple-element.24.lists, bf16[32,128,128]{2,1,0:T(8,128)(2,1)S(1)} %copy-done, ...), custom_call_target="tpu_custom_call", output_to_operand_aliasing={{1}: (3, {})} | custom-call | flops 134217728 | bytes 2097152 | tf_op jit(solution)/shard_map/last_b/pallas_call | solution.py:366
  45.3 0.0 collective-permute-done.1.from_a
  45.3 2.0 %last_a.1 = (bf16[1,125,32,128]{3,2,1,0:T(8,128)(2,1)}, f32[33,128,128]{2,1,0:T(8,128)S(1)}) custom-call(bf16[8,128,128]{2,1,0:T(8,128)(2,1)S(1)} %collective-permute-done.1.from_a, s32[16,128]{1,0:T(8,128)S(1)} %get-tuple-element.23.lists, bf16[32,128,128]{2,1,0:T(8,128)(2,1)S(1)} %copy-done, ...), custom_call_target="tpu_custom_call", output_to_operand_aliasing={{1}: (3, {}), {0}: (4, {})} | custom-call | flops 134217728 | bytes 2097152 | tf_op jit(solution)/shard_map/last_a/pallas_call | solution.py:377
Async XLA Ops:
  0.0 3.6 %copy-start.2 = (s32[1,1,32,16]{2,3,1,0:T(8,128)S(1)}, s32[1,1,32,16]{2,3,1,0:T(8,128)}, u32[]{:S(2)}) copy-start(s32[1,1,32,16]{2,3,1,0:T(8,128)} %param.10) | copy-start | bytes 6148
  0.0 3.6 %copy-start.3 = (s32[1,1,32,16]{2,3,1,0:T(8,128)S(1)}, s32[1,1,32,16]{2,3,1,0:T(8,128)}, u32[]{:S(2)}) copy-start(s32[1,1,32,16]{2,3,1,0:T(8,128)} %param.11) | copy-start | bytes 6148
  1.7 4.5 %copy-start.1 = (bf16[1,32,128]{2,1,0:T(8,128)(2,1)S(1)}, bf16[1,32,128]{2,1,0:T(8,128)(2,1)}, u32[]{:S(2)}) copy-start(bf16[1,32,128]{2,1,0:T(8,128)(2,1)} %vol.3) | copy-start | bytes 24580
  1.7 4.5 %collective-permute-start = (bf16[126,32,128]{2,1,0:T(8,128)(2,1)S(1)}, bf16[126,32,128]{2,1,0:T(8,128)(2,1)S(1)}, u32[]{:S(2)}, u32[]{:S(2)}) collective-permute-start(bf16[126,32,128]{2,1,0:T(8,128)(2,1)S(1)} %send.1), channel_id=1, source_target_pairs={{0,256},{256,0},{1,257},{257,1},{2,258},{258,2},{3,259},{259,3},{4... | collective-permute-start | bytes 3096584 | tf_op jit(solution)/shard_map/ppermute | solution.py:285
  6.2 17.4 %copy-start = (bf16[32,128,128]{2,1,0:T(8,128)(2,1)S(1)}, bf16[32,128,128]{2,1,0:T(8,128)(2,1)}, u32[]{:S(2)}) copy-start(bf16[32,128,128]{2,1,0:T(8,128)(2,1)} %tables.9) | copy-start | bytes 3145732
  7.0 29.1 %collective-permute-start.2 = (bf16[24,128,128]{2,1,0:T(8,128)(2,1)S(1)}, bf16[24,128,128]{2,1,0:T(8,128)(2,1)S(1)}, u32[]{:S(2)}, u32[]{:S(2)}) collective-permute-start(bf16[24,128,128]{2,1,0:T(8,128)(2,1)S(1)} %get-tuple-element.20), channel_id=1, source_target_pairs={{0,1},{2,3},{4,5},{6,7},{8,9},{10,11},{12,13},{14,15},{16,17},{18,... | collective-permute-start | bytes 2359304 | tf_op jit(solution)/shard_map/ppermute | solution.py:305
  10.4 22.1 %collective-permute-start.3 = (bf16[16,128,128]{2,1,0:T(8,128)(2,1)S(1)}, bf16[16,128,128]{2,1,0:T(8,128)(2,1)S(1)}, u32[]{:S(2)}, u32[]{:S(2)}) collective-permute-start(bf16[16,128,128]{2,1,0:T(8,128)(2,1)S(1)} %source_b.1.b0.first), channel_id=1, source_target_pairs={{1,2},{3,4},{5,6},{7,8},{9,10},{11,12},{13,14},{15,16},{17,18},{19... | collective-permute-start | bytes 1572872 | tf_op jit(solution)/shard_map/ppermute | solution.py:305
  16.4 26.2 %collective-permute-start.4 = (bf16[16,128,128]{2,1,0:T(8,128)(2,1)S(1)}, bf16[16,128,128]{2,1,0:T(8,128)(2,1)S(1)}, u32[]{:S(2)}, u32[]{:S(2)}) collective-permute-start(bf16[16,128,128]{2,1,0:T(8,128)(2,1)S(1)} %get-tuple-element.21.second), channel_id=1, source_target_pairs={{1,2},{3,4},{5,6},{7,8},{9,10},{11,12},{13,14},{15,16},{17,18},{19... | collective-permute-start | bytes 1572872 | tf_op jit(solution)/shard_map/ppermute | solution.py:305
  21.7 23.6 %collective-permute-start.1 = (bf16[8,128,128]{2,1,0:T(8,128)(2,1)S(1)}, bf16[8,128,128]{2,1,0:T(8,128)(2,1)S(1)}, u32[]{:S(2)}, u32[]{:S(2)}) collective-permute-start(bf16[8,128,128]{2,1,0:T(8,128)(2,1)S(1)} %get-tuple-element.19), channel_id=1, source_target_pairs={{0,1},{2,3},{4,5},{6,7},{8,9},{10,11},{12,13},{14,15},{16,17},{18,... | collective-permute-start | bytes 786440 | tf_op jit(solution)/shard_map/ppermute | solution.py:305

commit v7 on v5

--- a/solution.py
+++ b/solution.py
@@ -157,13 +157,15 @@
     return n + 8
 
 
-def add_terms(blocks, lists, tables, acc, mats, codes, sem):
+def add_terms(blocks, lists, tables, acc, mats, codes, sem, meanwhile=None):
     n = HALF * len(blocks)
     copy = pltpu.make_async_copy(lists, codes, sem)
     copy.start()
     mats[0] = jnp.zeros((ROWS, W), jnp.bfloat16)
     for i, ref in enumerate(blocks):
         mats[1 + i * HALF : 1 + (i + 1) * HALF] = ref[...]
+    if meanwhile is not None:
+        meanwhile()
     copy.wait()
 
     def step(i, carry):
@@ -215,23 +217,28 @@
         stage[c] = result[0:G].astype(jnp.bfloat16)
         copies.append(pltpu.make_async_copy(stage.at[c], out.at[0, :, span], sems.at[c]))
         copies[-1].start()
-    for copy in copies:
-        copy.wait()
-
-
-def last_b_kernel(from_b, lists, tables, acc_in, out, acc, stage, sems, *scratch):
+    return copies
+
+
+def last_b_kernel(from_b, lists, tables, acc_in, acc, *scratch):
     if COPY_ALIASED:
         acc[...] = acc_in[...]
     add_terms((from_b,), lists, tables, acc, *scratch)
-    finish(lax.rem(lax.axis_index("dom"), 2), acc, out, stage, sems)
-
-
-def last_a_kernel(from_a, lists, tables, acc_in, out_in, out, acc, stage, sems, *scratch):
+
+
+def last_a_kernel(from_a, lists, tables, acc_in, out, acc, stage, sems, *scratch):
     if COPY_ALIASED:
         acc[...] = acc_in[...]
-        pltpu.sync_copy(out_in, out)
-    add_terms((from_a,), lists, tables, acc, *scratch)
-    finish(1 - lax.rem(lax.axis_index("dom"), 2), acc, out, stage, sems)
+    odd = lax.rem(lax.axis_index("dom"), 2)
+    copies = []
+
+    def finish_b():
+        copies.extend(finish(odd, acc, out, stage.at[0], sems.at[0]))
+
+    add_terms((from_a,), lists, tables, acc, *scratch, meanwhile=finish_b)
+    copies.extend(finish(1 - odd, acc, out, stage.at[1], sems.at[1]))
+    for copy in copies:
+        copy.wait()
 
 
 def per_device(kernels, counts, volume, tables, pair_offset, pair_table):
@@ -305,7 +312,7 @@
     def work(n):
         return [pltpu.VMEM((n + 1, ROWS, W), bf16), pltpu.SMEM(lists(n), i32), dma]
 
-    stage = [pltpu.VMEM((HALF // 8, G, 8, W), bf16), dma((HALF // 8,))]
+    stage = [pltpu.VMEM((2, HALF // 8, G, 8, W), bf16), dma((2, HALF // 8))]
     acc = pl.pallas_call(
         own_kernel,
         out_shape=acc_shape,
@@ -327,13 +334,13 @@
         cost_estimate=cost(192 * term, 12 << 20),
         name="chunk_terms",
     )(b0, a0, tables, acc)
-    out, acc = pl.pallas_call(
+    acc = pl.pallas_call(
         last_b_kernel,
-        out_shape=[out_shape, acc_shape],
+        out_shape=acc_shape,
         in_specs=[VMEM] * 4,
-        out_specs=[HBM, VMEM],
-        scratch_shapes=stage + work(HALF),
-        input_output_aliases={3: 1},
+        out_specs=VMEM,
+        scratch_shapes=work(HALF),
+        input_output_aliases={3: 0},
         compiler_params=params(6),
         cost_estimate=cost(32 * term, 2 << 20),
         name="last_b",
@@ -341,14 +348,14 @@
     out, _ = pl.pallas_call(
         last_a_kernel,
         out_shape=[out_shape, acc_shape],
-        in_specs=[VMEM] * 4 + [HBM],
+        in_specs=[VMEM] * 4,
         out_specs=[HBM, VMEM],
         scratch_shapes=stage + work(HALF),
-        input_output_aliases={3: 1, 4: 0},
+        input_output_aliases={3: 1},
         compiler_params=params(6),
         cost_estimate=cost(32 * term, 2 << 20),
         name="last_a",
-    )(a1, lists_a, tables, acc, out)
+    )(a1, lists_a, tables, acc)
     return jnp.transpose(out, (0, 2, 1, 3))
 
 

time: 44.7 us -> 44.2 us (0.989)
  the two profiles are of different devices: /device:TPU:254 before, /device:TPU:448 now
where the time goes in v7:
time: 44.2 us; the launch traced here: 44 us
  Pallas kernels  20.8 us (47%)
  starting transfers between devices  17.2 us (39%)
  waiting for transfers between devices  5.8 us (13%)
    ppermute x4, starting transfers between devices, swapped(): return in_vmem(lax.ppermute(value, 'dom', pairs))  15.3 us
    pallas_call x1, Pallas kernels, per_device(): pl.pallas_call(own_kernel, out_shape=acc_shape, in_specs=[VMEM] * 3, out_...  7.01 us
    pallas_call x1, Pallas kernels, per_device(): pl.pallas_call(chunk_kernel, out_shape=[acc_shape] + [on_chip(lists(HALF)...  5.44 us
    ppermute x4, waiting for transfers between devices, swapped(): return in_vmem(lax.ppermute(value, 'dom', pairs))  4.85 us
    pallas_call x1, Pallas kernels, per_device(): pl.pallas_call(last_a_kernel, out_shape=[out_shape, acc_shape], in_specs=...  2.66 us
    ppermute x1, starting transfers between devices, per_device(): got = lax.ppermute(to_other, 'event', [(0, 1), (1, 0)])  1.92 us
    pallas_call x1, Pallas kernels, per_device(): pl.pallas_call(last_b_kernel, out_shape=acc_shape, in_specs=[VMEM] * 4, o...  1.68 us
    pallas_call x1, Pallas kernels, per_device(): pl.pallas_call(send_kernel, out_shape=sums, in_specs=[HBM, HBM], out_spec...  1.64 us
  transfers between devices with their start and end apart: 5, of which 4 were waited for; matrix products, arithmetic and copies ran while one was open for 0% of the time, Pallas kernels for 37%

profile of v7, /device:TPU:448, one launch (start us, length us, event | category | flops | bytes accessed | tf_op | source)
XLA Modules:
  0.0 44.0 jit_solution(10435607061510461344)
XLA Ops:
  0.0 0.0 copy-start.2
  0.0 0.0 copy-start.3
  0.0 1.6 %send.1 = bf16[126,32,128]{2,1,0:T(8,128)(2,1)S(1)} custom-call(bf16[2,1,125,64,128]{4,3,2,1,0:T(8,128)(2,1)} %bitcast.6, s32[2,1,64,128]{3,2,1,0:T(8,128)} %counts.3), custom_call_target="tpu_custom_call" | custom-call | flops 1048576 | bytes 4194304 | tf_op jit(solution)/shard_map/send/pallas_call | solution.py:259
  1.7 0.0 copy-start.1
  1.7 1.9 %collective-permute-start = (bf16[126,32,128]{2,1,0:T(8,128)(2,1)S(1)}, bf16[126,32,128]{2,1,0:T(8,128)(2,1)S(1)}, u32[]{:S(2)}, u32[]{:S(2)}) collective-permute-start(bf16[126,32,128]{2,1,0:T(8,128)(2,1)S(1)} %send.1), channel_id=1, source_target_pairs={{0,256},{256,0},{1,257},{257,1},{2,258},{258,2},{3,259},{259,3},{4... | collective-permute-start | bytes 3096584 | tf_op jit(solution)/shard_map/ppermute | solution.py:269
  3.6 0.0 copy-done.2
  3.6 0.0 copy-done.3
  3.6 1.6 %keep.1 = (bf16[126,32,128]{2,1,0:T(8,128)(2,1)S(1)}, f32[32,128]{1,0:T(8,128)S(1)}) custom-call(bf16[2,1,125,64,128]{4,3,2,1,0:T(8,128)(2,1)} %bitcast.7, s32[2,1,64,128]{3,2,1,0:T(8,128)} %counts.3, s32[1,1,16,32]{3,2,1,0:T(8,128)S(1)} %bitcast.4, s32[1,1,16,32]{3,2,1,0:T(8,128)S(1)} %bitcast.5), custom_call_target="tpu_custom_call" | custom-call | flops 1048576 | bytes 4194304 | tf_op jit(solution)/shard_map/keep/pallas_call | solution.py:270
  5.3 0.9 %collective-permute-done.got = bf16[126,32,128]{2,1,0:T(8,128)(2,1)S(1)} collective-permute-done((bf16[126,32,128]{2,1,0:T(8,128)(2,1)S(1)}, bf16[126,32,128]{2,1,0:T(8,128)(2,1)S(1)}, u32[]{:S(2)}, u32[]{:S(2)}) %collective-permute-start) | collective-permute-done | bytes 1032224 | tf_op jit(solution)/shard_map/ppermute | solution.py:269
  6.2 0.0 copy-done.1
  6.2 0.0 copy-start
  6.2 0.3 shard_map.64.first
  6.6 7.6 %collective-permute-start.2 = (bf16[16,128,128]{2,1,0:T(8,128)(2,1)S(1)}, bf16[16,128,128]{2,1,0:T(8,128)(2,1)S(1)}, u32[]{:S(2)}, u32[]{:S(2)}) collective-permute-start(bf16[16,128,128]{2,1,0:T(8,128)(2,1)S(1)} %shard_map.64.first), channel_id=1, source_target_pairs={{1,2},{3,4},{5,6},{7,8},{9,10},{11,12},{13,14},{15,16},{17,18},{19... | collective-permute-start | bytes 1572872 | tf_op jit(solution)/shard_map/ppermute | solution.py:296
  14.1 0.4 shard_map.65.second
  14.5 1.9 %collective-permute-start.3 = (bf16[16,128,128]{2,1,0:T(8,128)(2,1)S(1)}, bf16[16,128,128]{2,1,0:T(8,128)(2,1)S(1)}, u32[]{:S(2)}, u32[]{:S(2)}) collective-permute-start(bf16[16,128,128]{2,1,0:T(8,128)(2,1)S(1)} %shard_map.65.second), channel_id=1, source_target_pairs={{0,1},{2,3},{4,5},{6,7},{8,9},{10,11},{12,13},{14,15},{16,17},{18,... | collective-permute-start | bytes 1572872 | tf_op jit(solution)/shard_map/ppermute | solution.py:296
  16.4 3.3 %collective-permute-start.4 = (bf16[16,128,128]{2,1,0:T(8,128)(2,1)S(1)}, bf16[16,128,128]{2,1,0:T(8,128)(2,1)S(1)}, u32[]{:S(2)}, u32[]{:S(2)}) collective-permute-start(bf16[16,128,128]{2,1,0:T(8,128)(2,1)S(1)} %shard_map.65.second), channel_id=1, source_target_pairs={{1,2},{3,4},{5,6},{7,8},{9,10},{11,12},{13,14},{15,16},{17,18},{19... | collective-permute-start | bytes 1572872 | tf_op jit(solution)/shard_map/ppermute | solution.py:296
  19.7 2.6 %collective-permute-start.1 = (bf16[16,128,128]{2,1,0:T(8,128)(2,1)S(1)}, bf16[16,128,128]{2,1,0:T(8,128)(2,1)S(1)}, u32[]{:S(2)}, u32[]{:S(2)}) collective-permute-start(bf16[16,128,128]{2,1,0:T(8,128)(2,1)S(1)} %shard_map.64.first), channel_id=1, source_target_pairs={{0,1},{2,3},{4,5},{6,7},{8,9},{10,11},{12,13},{14,15},{16,17},{18,... | collective-permute-start | bytes 1572872 | tf_op jit(solution)/shard_map/ppermute | solution.py:296
  22.3 0.0 copy-done
  22.3 7.0 %own_terms.1.acc_in = f32[33,128,128]{2,1,0:T(8,128)S(1)} custom-call(bf16[16,128,128]{2,1,0:T(8,128)(2,1)S(1)} %shard_map.64.first, bf16[16,128,128]{2,1,0:T(8,128)(2,1)S(1)} %shard_map.65.second, bf16[32,128,128]{2,1,0:T(8,128)(2,1)S(1)} %copy-done), custom_call_target="tpu_custom_call" | custom-call | flops 1073741824 | bytes 16777216 | tf_op jit(solution)/shard_map/own_terms/pallas_call | solution.py:316
  29.3 0.0 collective-permute-done.2.from_b
  29.3 1.9 %collective-permute-done.3.from_a = bf16[16,128,128]{2,1,0:T(8,128)(2,1)S(1)} collective-permute-done((bf16[16,128,128]{2,1,0:T(8,128)(2,1)S(1)}, bf16[16,128,128]{2,1,0:T(8,128)(2,1)S(1)}, u32[]{:S(2)}, u32[]{:S(2)}) %collective-permute-start.3) | collective-permute-done | bytes 524320 | tf_op jit(solution)/shard_map/ppermute | solution.py:296
  31.2 5.4 %chunk_terms.1 = (f32[33,128,128]{2,1,0:T(8,128)S(1)}, s32[24,128]{1,0:T(8,128)S(1)}, s32[24,128]{1,0:T(8,128)S(1)}) custom-call(bf16[16,128,128]{2,1,0:T(8,128)(2,1)S(1)} %collective-permute-done.2.from_b, bf16[16,128,128]{2,1,0:T(8,128)(2,1)S(1)} %collective-permute-done.3.from_a, ...), custom_call_target="tpu_custom_call", output_to_operand_aliasing={{0}: (3, {})} | custom-call | flops 805306368 | bytes 12582912 | tf_op jit(solution)/shard_map/chunk_terms/pallas_call | solution.py:326
  36.6 1.2 %collective-permute-done.4.from_b = bf16[16,128,128]{2,1,0:T(8,128)(2,1)S(1)} collective-permute-done((bf16[16,128,128]{2,1,0:T(8,128)(2,1)S(1)}, bf16[16,128,128]{2,1,0:T(8,128)(2,1)S(1)}, u32[]{:S(2)}, u32[]{:S(2)}) %collective-permute-start.4) | collective-permute-done | bytes 524320 | tf_op jit(solution)/shard_map/ppermute | solution.py:296
  37.9 1.7 %last_b.1.acc_in = f32[33,128,128]{2,1,0:T(8,128)S(1)} custom-call(bf16[16,128,128]{2,1,0:T(8,128)(2,1)S(1)} %collective-permute-done.4.from_b, s32[24,128]{1,0:T(8,128)S(1)} %get-tuple-element.14.lists, bf16[32,128,128]{2,1,0:T(8,128)(2,1)S(1)} %copy-done, f32[33,128,128]{2,1,0:T(8,128)S(1)} %get-tuple-element.15.acc_in), custom_call_target="tpu_custom_call", output_to_operand_aliasing={{}: (3, {})} | custom-call | flops 134217728 | bytes 2097152 | tf_op jit(solution)/shard_map/last_b/pallas_call | solution.py:337
  39.5 1.7 %collective-permute-done.1.from_a = bf16[16,128,128]{2,1,0:T(8,128)(2,1)S(1)} collective-permute-done((bf16[16,128,128]{2,1,0:T(8,128)(2,1)S(1)}, bf16[16,128,128]{2,1,0:T(8,128)(2,1)S(1)}, u32[]{:S(2)}, u32[]{:S(2)}) %collective-permute-start.1) | collective-permute-done | bytes 524320 | tf_op jit(solution)/shard_map/ppermute | solution.py:296
  41.3 2.7 %last_a.1 = (bf16[1,125,32,128]{3,2,1,0:T(8,128)(2,1)}, f32[33,128,128]{2,1,0:T(8,128)S(1)}) custom-call(bf16[16,128,128]{2,1,0:T(8,128)(2,1)S(1)} %collective-permute-done.1.from_a, s32[24,128]{1,0:T(8,128)S(1)} %get-tuple-element.13.lists, bf16[32,128,128]{2,1,0:T(8,128)(2,1)S(1)} %copy-done, ...), custom_call_target="tpu_custom_call", output_to_operand_aliasing={{1}: (3, {})} | custom-call | flops 134217728 | bytes 2097152 | tf_op jit(solution)/shard_map/last_a/pallas_call | solution.py:348
Async XLA Ops:
  0.0 3.6 %copy-start.2 = (s32[1,1,32,16]{2,3,1,0:T(8,128)S(1)}, s32[1,1,32,16]{2,3,1,0:T(8,128)}, u32[]{:S(2)}) copy-start(s32[1,1,32,16]{2,3,1,0:T(8,128)} %param.10) | copy-start | bytes 6148
  0.0 3.6 %copy-start.3 = (s32[1,1,32,16]{2,3,1,0:T(8,128)S(1)}, s32[1,1,32,16]{2,3,1,0:T(8,128)}, u32[]{:S(2)}) copy-start(s32[1,1,32,16]{2,3,1,0:T(8,128)} %param.11) | copy-start | bytes 6148
  1.7 4.5 %copy-start.1 = (bf16[1,32,128]{2,1,0:T(8,128)(2,1)S(1)}, bf16[1,32,128]{2,1,0:T(8,128)(2,1)}, u32[]{:S(2)}) copy-start(bf16[1,32,128]{2,1,0:T(8,128)(2,1)} %vol.3) | copy-start | bytes 24580
  1.7 4.5 %collective-permute-start = (bf16[126,32,128]{2,1,0:T(8,128)(2,1)S(1)}, bf16[126,32,128]{2,1,0:T(8,128)(2,1)S(1)}, u32[]{:S(2)}, u32[]{:S(2)}) collective-permute-start(bf16[126,32,128]{2,1,0:T(8,128)(2,1)S(1)} %send.1), channel_id=1, source_target_pairs={{0,256},{256,0},{1,257},{257,1},{2,258},{258,2},{3,259},{259,3},{4... | collective-permute-start | bytes 3096584 | tf_op jit(solution)/shard_map/ppermute | solution.py:269
  6.2 16.1 %copy-start = (bf16[32,128,128]{2,1,0:T(8,128)(2,1)S(1)}, bf16[32,128,128]{2,1,0:T(8,128)(2,1)}, u32[]{:S(2)}) copy-start(bf16[32,128,128]{2,1,0:T(8,128)(2,1)} %tables.7) | copy-start | bytes 3145732
  6.6 22.8 %collective-permute-start.2 = (bf16[16,128,128]{2,1,0:T(8,128)(2,1)S(1)}, bf16[16,128,128]{2,1,0:T(8,128)(2,1)S(1)}, u32[]{:S(2)}, u32[]{:S(2)}) collective-permute-start(bf16[16,128,128]{2,1,0:T(8,128)(2,1)S(1)} %shard_map.64.first), channel_id=1, source_target_pairs={{1,2},{3,4},{5,6},{7,8},{9,10},{11,12},{13,14},{15,16},{17,18},{19... | collective-permute-start | bytes 1572872 | tf_op jit(solution)/shard_map/ppermute | solution.py:296
  14.5 16.7 %collective-permute-start.3 = (bf16[16,128,128]{2,1,0:T(8,128)(2,1)S(1)}, bf16[16,128,128]{2,1,0:T(8,128)(2,1)S(1)}, u32[]{:S(2)}, u32[]{:S(2)}) collective-permute-start(bf16[16,128,128]{2,1,0:T(8,128)(2,1)S(1)} %shard_map.65.second), channel_id=1, source_target_pairs={{0,1},{2,3},{4,5},{6,7},{8,9},{10,11},{12,13},{14,15},{16,17},{18,... | collective-permute-start | bytes 1572872 | tf_op jit(solution)/shard_map/ppermute | solution.py:296
  16.4 21.4 %collective-permute-start.4 = (bf16[16,128,128]{2,1,0:T(8,128)(2,1)S(1)}, bf16[16,128,128]{2,1,0:T(8,128)(2,1)S(1)}, u32[]{:S(2)}, u32[]{:S(2)}) collective-permute-start(bf16[16,128,128]{2,1,0:T(8,128)(2,1)S(1)} %shard_map.65.second), channel_id=1, source_target_pairs={{1,2},{3,4},{5,6},{7,8},{9,10},{11,12},{13,14},{15,16},{17,18},{19... | collective-permute-start | bytes 1572872 | tf_op jit(solution)/shard_map/ppermute | solution.py:296
  19.7 21.6 %collective-permute-start.1 = (bf16[16,128,128]{2,1,0:T(8,128)(2,1)S(1)}, bf16[16,128,128]{2,1,0:T(8,128)(2,1)S(1)}, u32[]{:S(2)}, u32[]{:S(2)}) collective-permute-start(bf16[16,128,128]{2,1,0:T(8,128)(2,1)S(1)} %shard_map.64.first), channel_id=1, source_target_pairs={{0,1},{2,3},{4,5},{6,7},{8,9},{10,11},{12,13},{14,15},{16,17},{18,... | collective-permute-start | bytes 1572872 | tf_op jit(solution)/shard_map/ppermute | solution.py:296
